TPU v7x, 1024 devices: a whole 8x8x8 slice. The times are simulated.
1024 devices in a mesh: vec: 64 (over y, x_lo, core), field: 16 (over z, x_hi).
Axes of the slice: x: 8 (x_hi: 2, x_lo: 4; x = x_hi * 4 + x_lo), y: 8, z: 8, core: 2. Of those that a mesh axis runs over, the one named last changes fastest.
Arguments:
- vectors: float32 [4096, 24576], P('vec', 'field'), may hold values from -6 to 6
Outputs:
- first_tensor: float32 [4096, 4096], P(('vec', 'field'))
- second_tensor: float32 [4096, 4096], P(('vec', 'field'))
All inputs are finite; a program needn't handle non-finite values.
Results may differ from a plain program's by a relative error of at most 0.000098.
Values sent between devices are 32-bit elements; how exact they have to be, the bound alone decides.
No kernel may reach another device: no remote copies, remote signals or barrier semaphores. Data moves between devices by JAX's collectives and lax.ppermute only.
A program may use at most 64 MiB of HBM per device.

v0:
```python
import math

import jax
import jax.numpy as jnp
from jax import lax
from jax.sharding import PartitionSpec as P


def passed_along(x, axis, by):
    peers = lax.axis_size(axis)
    return lax.ppermute(x, axis, [(i, (i + by) % peers) for i in range(peers)])


def cut_along(x, dim, peers):
    shape = x.shape
    pieces = x.reshape(*shape[:dim], peers, shape[dim] // peers, *shape[dim + 1 :])
    return jnp.moveaxis(pieces, dim, 0)


def summed_on_arrival(x, axis, dim):
    pieces = cut_along(x, dim, lax.axis_size(axis))
    arrived = lax.all_to_all(pieces, axis, split_axis=0, concat_axis=0, tiled=True)
    return arrived.sum(axis=0)


def triple_rows(a_rows, partner, third):
    count = a_rows.shape[0]
    group_size = math.gcd(count, 8)
    groups = a_rows.reshape(count // group_size, group_size, a_rows.shape[1])

    def single_group(group):
        product = (group[:, None, :] * partner[None, :, :]).reshape(
            group_size * partner.shape[0], group.shape[1]
        )
        result = lax.dot_general(
            product,
            third,
            (((1,), (1,)), ((), ())),
            precision=lax.Precision.HIGHEST,
            preferred_element_type=jnp.float32,
        )
        return result.reshape(group_size, partner.shape[0] * third.shape[0])

    return lax.map(single_group, groups).reshape(count, partner.shape[0] * third.shape[0])


def per_device(vectors):
    parts = lax.axis_size("field")
    block_rows = vectors.shape[0]
    owned = block_rows // parts
    scale = 1.0 / math.sqrt(vectors.shape[1] * parts)
    following = passed_along(vectors, "vec", -1)
    further = passed_along(vectors, "vec", -2)
    first_tensor = summed_on_arrival(triple_rows(vectors, following, further), "field", 0) * scale
    earlier = passed_along(first_tensor, "vec", 1)
    earlier = earlier.reshape(owned, parts, owned * block_rows)
    turned = lax.all_to_all(earlier, "field", split_axis=1, concat_axis=0, tiled=True)
    turned = turned.reshape(block_rows, owned, block_rows)
    second_tensor = jnp.transpose(turned, (1, 0, 2)).reshape(owned, block_rows * block_rows)
    return (first_tensor, second_tensor)


def solution(mesh):
    placed = (P("vec", "field"),)
    return jax.shard_map(
        per_device,
        mesh=mesh,
        in_specs=placed,
        out_specs=(P(("vec", "field"), None), P(("vec", "field"), None)),
        check_vma=False,
    )
```

profile of v0, /device:TPU:128, one launch (start us, length us, event | category | flops | bytes accessed | tf_op | source)
XLA Modules:
  0.0 130.8 jit_solution(15006018386878995710)
XLA Ops:
  0.6 8.4 %collective-permute-start = (f32[64,1536]{1,0:T(8,128)}, f32[64,1536]{1,0:T(8,128)S(1)}, u32[]{:S(2)}, u32[]{:S(2)}) collective-permute-start(f32[64,1536]{1,0:T(8,128)} %param.3), channel_id=1, source_target_pairs={{0,1008},{16,0},{32,16},{48,32},{64,48},{80,64},{96,80},{112,96},{... | collective-permute-start | bytes 1179656 | tf_op jit(solution)/shard_map/ppermute | solution.py:11
  9.0 2.5 %collective-permute-start.1 = (f32[64,1536]{1,0:T(8,128)}, f32[64,1536]{1,0:T(8,128)S(1)}, u32[]{:S(2)}, u32[]{:S(2)}) collective-permute-start(f32[64,1536]{1,0:T(8,128)} %param.3), channel_id=1, source_target_pairs={{0,992},{16,1008},{32,0},{48,16},{64,32},{80,48},{96,64},{112,80},... | collective-permute-start | bytes 1179656 | tf_op jit(solution)/shard_map/ppermute | solution.py:11
  11.5 5.3 %collective-permute-done = f32[64,1536]{1,0:T(8,128)S(1)} collective-permute-done((f32[64,1536]{1,0:T(8,128)}, f32[64,1536]{1,0:T(8,128)S(1)}, u32[]{:S(2)}, u32[]{:S(2)}) %collective-permute-start) | collective-permute-done | bytes 393248 | tf_op jit(solution)/shard_map/ppermute | solution.py:11
  16.8 6.2 %collective-permute-done.1 = f32[64,1536]{1,0:T(8,128)S(1)} collective-permute-done((f32[64,1536]{1,0:T(8,128)}, f32[64,1536]{1,0:T(8,128)S(1)}, u32[]{:S(2)}, u32[]{:S(2)}) %collective-permute-start.1) | collective-permute-done | bytes 393248 | tf_op jit(solution)/shard_map/ppermute | solution.py:11
  23.0 31.4 %while.10 = (s32[]{:T(128)}, f32[8,8,4096]{2,1,0:T(8,128)S(1)}, f32[8,8,1536]{2,1,0:T(8,128)}, f32[64,1536]{1,0:T(8,128)S(1)}, f32[64,1536]{1,0:T(8,128)S(1)}, /*index=5*/s32[]{:T(128)}) while((s32[]{:T(128)}, f32[8,8,4096]{2,1,0:T(8,128)S(1)}, f32[8,8,1536]{2,1,0:T(8,128)}, f32[64,1536]{1,0:T(8,128)S(1)}, f32[64,1536]{1,0:T(8,128)S(1)}, ...), condition=%wide.region_1.2_spmd, body=%wide.region_0.1_spmd.sunk | while | flops 604766208 | bytes 7880781 | solution.py:44
  23.0 0.8 dynamic-slice_bitcast_fusion.2
  23.9 0.4 broadcast_multiply_fusion.3
  24.2 2.6 %fusion.8 = f32[512,64]{1,0:T(8,128)S(1)} fusion(f32[512,1536]{1,0:T(8,128)S(1)} %bitcast.21, f32[64,1536]{1,0:T(8,128)S(1)} %get-tuple-element.87), kind=kOutput, calls=%fused_computation.4.clone.1 | convolution fusion | flops 603979776 | bytes 3670016 | tf_op jit(solution)/shard_map/while/body/eval_jaxpr/dot_general | solution.py:35
  26.8 0.1 broadcast_in_dim.11
  27.0 0.8 dynamic-slice_bitcast_fusion.2
  27.8 0.4 broadcast_multiply_fusion.3
  28.2 2.6 %fusion.8 = f32[512,64]{1,0:T(8,128)S(1)} fusion(f32[512,1536]{1,0:T(8,128)S(1)} %bitcast.21, f32[64,1536]{1,0:T(8,128)S(1)} %get-tuple-element.87), kind=kOutput, calls=%fused_computation.4.clone.1 | convolution fusion | flops 603979776 | bytes 3670016 | tf_op jit(solution)/shard_map/while/body/eval_jaxpr/dot_general | solution.py:35
  30.8 0.1 broadcast_in_dim.11
  30.9 0.8 dynamic-slice_bitcast_fusion.2
  31.7 0.4 broadcast_multiply_fusion.3
  32.1 2.6 %fusion.8 = f32[512,64]{1,0:T(8,128)S(1)} fusion(f32[512,1536]{1,0:T(8,128)S(1)} %bitcast.21, f32[64,1536]{1,0:T(8,128)S(1)} %get-tuple-element.87), kind=kOutput, calls=%fused_computation.4.clone.1 | convolution fusion | flops 603979776 | bytes 3670016 | tf_op jit(solution)/shard_map/while/body/eval_jaxpr/dot_general | solution.py:35
  34.7 0.1 broadcast_in_dim.11
  34.8 0.8 dynamic-slice_bitcast_fusion.2
  35.6 0.4 broadcast_multiply_fusion.3
  36.0 2.6 %fusion.8 = f32[512,64]{1,0:T(8,128)S(1)} fusion(f32[512,1536]{1,0:T(8,128)S(1)} %bitcast.21, f32[64,1536]{1,0:T(8,128)S(1)} %get-tuple-element.87), kind=kOutput, calls=%fused_computation.4.clone.1 | convolution fusion | flops 603979776 | bytes 3670016 | tf_op jit(solution)/shard_map/while/body/eval_jaxpr/dot_general | solution.py:35
  38.6 0.1 broadcast_in_dim.11
  38.8 0.8 dynamic-slice_bitcast_fusion.2
  39.6 0.4 broadcast_multiply_fusion.3
  40.0 2.6 %fusion.8 = f32[512,64]{1,0:T(8,128)S(1)} fusion(f32[512,1536]{1,0:T(8,128)S(1)} %bitcast.21, f32[64,1536]{1,0:T(8,128)S(1)} %get-tuple-element.87), kind=kOutput, calls=%fused_computation.4.clone.1 | convolution fusion | flops 603979776 | bytes 3670016 | tf_op jit(solution)/shard_map/while/body/eval_jaxpr/dot_general | solution.py:35
  42.5 0.1 broadcast_in_dim.11
  42.7 0.8 dynamic-slice_bitcast_fusion.2
  43.5 0.4 broadcast_multiply_fusion.3
  43.9 2.6 %fusion.8 = f32[512,64]{1,0:T(8,128)S(1)} fusion(f32[512,1536]{1,0:T(8,128)S(1)} %bitcast.21, f32[64,1536]{1,0:T(8,128)S(1)} %get-tuple-element.87), kind=kOutput, calls=%fused_computation.4.clone.1 | convolution fusion | flops 603979776 | bytes 3670016 | tf_op jit(solution)/shard_map/while/body/eval_jaxpr/dot_general | solution.py:35
  46.5 0.1 broadcast_in_dim.11
  46.6 0.8 dynamic-slice_bitcast_fusion.2
  47.4 0.4 broadcast_multiply_fusion.3
  47.8 2.6 %fusion.8 = f32[512,64]{1,0:T(8,128)S(1)} fusion(f32[512,1536]{1,0:T(8,128)S(1)} %bitcast.21, f32[64,1536]{1,0:T(8,128)S(1)} %get-tuple-element.87), kind=kOutput, calls=%fused_computation.4.clone.1 | convolution fusion | flops 603979776 | bytes 3670016 | tf_op jit(solution)/shard_map/while/body/eval_jaxpr/dot_general | solution.py:35
  50.4 0.1 broadcast_in_dim.11
  50.6 0.8 dynamic-slice_bitcast_fusion.2
  51.4 0.4 broadcast_multiply_fusion.3
  51.7 2.6 %fusion.8 = f32[512,64]{1,0:T(8,128)S(1)} fusion(f32[512,1536]{1,0:T(8,128)S(1)} %bitcast.21, f32[64,1536]{1,0:T(8,128)S(1)} %get-tuple-element.87), kind=kOutput, calls=%fused_computation.4.clone.1 | convolution fusion | flops 603979776 | bytes 3670016 | tf_op jit(solution)/shard_map/while/body/eval_jaxpr/dot_general | solution.py:35
  54.3 0.1 broadcast_in_dim.11
  54.5 0.3 reshape_reshape.3
  54.8 44.0 %all_to_all.20 = f32[16,4,4096]{2,1,0:T(4,128)S(1)} all-to-all(f32[16,4,4096]{2,1,0:T(4,128)S(1)} %reshape_reshape.3), channel_id=1, replica_groups=mesh['vec'=64,'field'=16] {'field'}, dimensions={0} | all-to-all | bytes 2097152 | tf_op jit(solution)/shard_map/all_to_all | solution.py:22
  98.8 0.2 reduce_sum.9
  99.0 0.0 copy-start
  99.0 1.9 %collective-permute-start.2 = (f32[4,4096]{1,0:T(4,128)S(1)}, f32[4,4096]{1,0:T(4,128)S(1)}, u32[]{:S(2)}, u32[]{:S(2)}) collective-permute-start(f32[4,4096]{1,0:T(4,128)S(1)} %broadcast_multiply_fusion.1), channel_id=1, source_target_pairs={{0,16},{16,32},{32,48},{48,64},{64,80},{80,96},{96,112},{112,128},... | collective-permute-start | bytes 196616 | tf_op jit(solution)/shard_map/ppermute | solution.py:11
  100.9 8.7 %collective-permute-done.2 = f32[4,4096]{1,0:T(4,128)S(1)} collective-permute-done((f32[4,4096]{1,0:T(4,128)S(1)}, f32[4,4096]{1,0:T(4,128)S(1)}, u32[]{:S(2)}, u32[]{:S(2)}) %collective-permute-start.2) | collective-permute-done | bytes 65568 | tf_op jit(solution)/shard_map/ppermute | solution.py:11
  109.6 20.3 %all_to_all.21 = f32[4,16,256]{2,0,1:T(4,128)S(1)} all-to-all(f32[4,16,256]{2,0,1:T(4,128)S(1)} %bitcast.25), channel_id=1, replica_groups=mesh['vec'=64,'field'=16] {'field'}, dimensions={1} | all-to-all | bytes 131072 | tf_op jit(solution)/shard_map/all_to_all | solution.py:57
  130.0 0.1 reshape.28
  130.1 0.7 reshape.29
  130.8 0.0 copy-done
  (11 shorter events, 0.1 us)
Async XLA Ops:
  0.6 16.2 %collective-permute-start = (f32[64,1536]{1,0:T(8,128)}, f32[64,1536]{1,0:T(8,128)S(1)}, u32[]{:S(2)}, u32[]{:S(2)}) collective-permute-start(f32[64,1536]{1,0:T(8,128)} %param.3), channel_id=1, source_target_pairs={{0,1008},{16,0},{32,16},{48,32},{64,48},{80,64},{96,80},{112,96},{... | collective-permute-start | bytes 1179656 | tf_op jit(solution)/shard_map/ppermute | solution.py:11
  9.0 14.0 %collective-permute-start.1 = (f32[64,1536]{1,0:T(8,128)}, f32[64,1536]{1,0:T(8,128)S(1)}, u32[]{:S(2)}, u32[]{:S(2)}) collective-permute-start(f32[64,1536]{1,0:T(8,128)} %param.3), channel_id=1, source_target_pairs={{0,992},{16,1008},{32,0},{48,16},{64,32},{80,48},{96,64},{112,80},... | collective-permute-start | bytes 1179656 | tf_op jit(solution)/shard_map/ppermute | solution.py:11
  99.0 31.9 %copy-start = (f32[4,4096]{1,0:T(4,128)}, f32[4,4096]{1,0:T(4,128)S(1)}, u32[]{:S(2)}) copy-start(f32[4,4096]{1,0:T(4,128)S(1)} %broadcast_multiply_fusion.1) | copy-start | bytes 196612
  99.0 10.7 %collective-permute-start.2 = (f32[4,4096]{1,0:T(4,128)S(1)}, f32[4,4096]{1,0:T(4,128)S(1)}, u32[]{:S(2)}, u32[]{:S(2)}) collective-permute-start(f32[4,4096]{1,0:T(4,128)S(1)} %broadcast_multiply_fusion.1), channel_id=1, source_target_pairs={{0,16},{16,32},{32,48},{48,64},{64,80},{80,96},{96,112},{112,128},... | collective-permute-start | bytes 196616 | tf_op jit(solution)/shard_map/ppermute | solution.py:11
where the time goes:
time: 132 us; the launch traced here: 131 us
  blocking collectives  64.3 us (49%)
  matrix products  20.7 us (16%)
  waiting for transfers between devices  20.2 us (15%)
  starting transfers between devices  12.8 us (10%)
  local copies, waits for them, and re-layouts  8.67 us (7%)
  other arithmetic  3.13 us (2%)
    all_to_all x1, blocking collectives, summed_on_arrival(): lax.all_to_all(pieces, axis, split_axis=0, concat_axis=0, tiled=True)  44 us
    dot_general x8, matrix products, single_group(): lax.dot_general(product, third, (((1,), (1,)), ((), ())), precision=lax.P...  20.7 us
    all_to_all x1, blocking collectives, per_device(): lax.all_to_all(earlier, 'field', split_axis=1, concat_axis=0, tiled=True)  20.3 us
    ppermute x3, waiting for transfers between devices, passed_along(): return lax.ppermute(x, axis, [(i, (i + by) % peers) for i in range(peers)])  20.2 us
    ppermute x3, starting transfers between devices, passed_along(): return lax.ppermute(x, axis, [(i, (i + by) % peers) for i in range(peers)])  12.8 us
    mul x8, local copies, waits for them, and re-layouts, single_group(): group[:, None, :] * partner[None, :, :]  6.45 us
    mul x8, other arithmetic, single_group(): group[:, None, :] * partner[None, :, :]  2.95 us
  transfers between devices with their start and end apart: 3, of which 3 were waited for; matrix products, arithmetic and copies ran while one was open for 0% of the time, Pallas kernels for 0%

commit v1 on v0

v1 whole, which is shorter than its diff:
```python
import math

import jax
import jax.numpy as jnp
from jax import lax
from jax.experimental import pallas as pl
from jax.experimental.pallas import tpu as pltpu
from jax.sharding import PartitionSpec as P

GROUP = 16


def passed_along(x, axis, by):
    peers = lax.axis_size(axis)
    return lax.ppermute(x, axis, [(i, (i + by) % peers) for i in range(peers)])


def two_halves(x):
    high = x.astype(jnp.bfloat16)
    return high, (x - high.astype(jnp.float32)).astype(jnp.bfloat16)


def triple_kernel(scale, a_ref, b_ref, c_ref, out_ref, w_ref):
    rows = b_ref.shape[0]
    w_ref[...] = jnp.concatenate(two_halves(c_ref[...]), 0).T
    first_half = lax.broadcasted_iota(jnp.int32, (rows, 2 * rows), 1) < rows

    def step(g, carry):
        highs, lows = [], []
        for u in range(GROUP):
            high, low = two_halves(a_ref[pl.ds(g * GROUP + u, 1), :] * b_ref[...])
            highs.append(high)
            lows.append(low)
        w = w_ref[...]
        r = jnp.dot(jnp.concatenate(highs, 0), w, preferred_element_type=jnp.float32)
        r = r + jnp.dot(jnp.concatenate(lows, 0), w, preferred_element_type=jnp.float32)
        r = (r + pltpu.roll(r, rows, 1)) * scale
        for u in range(GROUP // 2):
            even = r[2 * u * rows : (2 * u + 1) * rows]
            odd = r[(2 * u + 1) * rows : (2 * u + 2) * rows]
            out_ref[g * (GROUP // 2) + u] = jnp.where(first_half, even, odd)
        return carry

    lax.fori_loop(0, rows // GROUP, step, 0)


def triples(a, b, c, scale):
    rows, fields = b.shape
    return pl.pallas_call(
        lambda *refs: triple_kernel(scale, *refs),
        name="triples",
        out_shape=jax.ShapeDtypeStruct((rows // 2, rows, 2 * rows), jnp.float32),
        in_specs=[pl.BlockSpec(memory_space=pltpu.VMEM)] * 3,
        out_specs=pl.BlockSpec(memory_space=pltpu.VMEM),
        scratch_shapes=[pltpu.VMEM((fields, 2 * rows), jnp.bfloat16)],
        compiler_params=pltpu.CompilerParams(vmem_limit_bytes=40 * 2**20),
        cost_estimate=pl.CostEstimate(
            flops=8 * rows**3 * fields, bytes_accessed=4 * (rows**3 + 3 * rows * fields), transcendentals=0
        ),
    )(a, b, c)


def per_device(vectors):
    parts = lax.axis_size("field")
    rows = vectors.shape[0]
    pairs = rows // parts // 2
    scale = 1.0 / math.sqrt(vectors.shape[1] * parts)
    previous = passed_along(vectors, "vec", 1)
    following = passed_along(vectors, "vec", -1)
    partial = triples(previous, vectors, following, scale)
    pieces = partial.reshape(parts, pairs, rows, 2 * rows)
    arrived = lax.all_to_all(pieces, "field", split_axis=0, concat_axis=0, tiled=True)
    mine = arrived.sum(axis=0)
    first = passed_along(mine, "vec", -1)
    first = first.reshape(pairs, rows, 2, rows).transpose(0, 2, 1, 3).reshape(2 * pairs, rows * rows)
    split = mine.reshape(pairs, parts, rows // parts, 2 * rows).transpose(1, 0, 2, 3)
    turned = lax.all_to_all(split, "field", split_axis=0, concat_axis=0, tiled=True)
    turned = turned.reshape(rows // 2, rows // parts, 2 * rows)
    second = jnp.transpose(turned, (1, 0, 2)).reshape(rows // parts, rows * rows)
    return (first, second)


def solution(mesh):
    placed = (P("vec", "field"),)
    return jax.shard_map(
        per_device,
        mesh=mesh,
        in_specs=placed,
        out_specs=(P(("vec", "field"), None), P(("vec", "field"), None)),
        check_vma=False,
    )
```

time: 132 us -> 102 us (0.77)
  the two profiles are of different devices: /device:TPU:128 before, /device:TPU:32 now
where the time goes in v1:
time: 102 us; the launch traced here: 101 us
  blocking collectives  54.8 us (54%)
  starting transfers between devices  19.5 us (19%)
  waiting for transfers between devices  15.5 us (15%)
  Pallas kernels  7.63 us (7%)
  local copies, waits for them, and re-layouts  3.22 us (3%)
    all_to_all x1, blocking collectives, per_device(): lax.all_to_all(pieces, 'field', split_axis=0, concat_axis=0, tiled=True)  54.8 us
    ppermute x3, starting transfers between devices, passed_along(): return lax.ppermute(x, axis, [(i, (i + by) % peers) for i in range(peers)])  10.2 us
    all_to_all x1, starting transfers between devices, per_device(): lax.all_to_all(split, 'field', split_axis=0, concat_axis=0, tiled=True)  9.29 us
    all_to_all x1, waiting for transfers between devices, per_device(): lax.all_to_all(split, 'field', split_axis=0, concat_axis=0, tiled=True)  7.99 us
    pallas_call x1, Pallas kernels, triples(): pl.pallas_call(lambda *refs: triple_kernel(scale, *refs), name='triples',...  7.63 us
    ppermute x3, waiting for transfers between devices, passed_along(): return lax.ppermute(x, axis, [(i, (i + by) % peers) for i in range(peers)])  7.47 us
  transfers between devices with their start and end apart: 4, of which 4 were waited for; matrix products, arithmetic and copies ran while one was open for 1% of the time, Pallas kernels for 0%

profile of v1, /device:TPU:32, one launch (start us, length us, event | category | flops | bytes accessed | tf_op | source)
XLA Modules:
  0.0 101.3 jit_solution(369680662855336640)
XLA Ops:
  0.6 1.9 %collective-permute-start = (f32[64,1536]{1,0:T(8,128)}, f32[64,1536]{1,0:T(8,128)S(1)}, u32[]{:S(2)}, u32[]{:S(2)}) collective-permute-start(f32[64,1536]{1,0:T(8,128)} %refs_1_.1), channel_id=1, source_target_pairs={{0,16},{16,32},{32,48},{48,64},{64,80},{80,96},{96,112},{112,128},... | collective-permute-start | bytes 1179656 | tf_op jit(solution)/shard_map/ppermute | solution.py:15
  2.6 6.3 %collective-permute-start.1 = (f32[64,1536]{1,0:T(8,128)}, f32[64,1536]{1,0:T(8,128)S(1)}, u32[]{:S(2)}, u32[]{:S(2)}) collective-permute-start(f32[64,1536]{1,0:T(8,128)} %refs_1_.1), channel_id=1, source_target_pairs={{0,1008},{16,0},{32,16},{48,32},{64,48},{80,64},{96,80},{112,96},{... | collective-permute-start | bytes 1179656 | tf_op jit(solution)/shard_map/ppermute | solution.py:15
  8.9 5.3 %collective-permute-done.refs_0_ = f32[64,1536]{1,0:T(8,128)S(1)} collective-permute-done((f32[64,1536]{1,0:T(8,128)}, f32[64,1536]{1,0:T(8,128)S(1)}, u32[]{:S(2)}, u32[]{:S(2)}) %collective-permute-start) | collective-permute-done | bytes 393248 | tf_op jit(solution)/shard_map/ppermute | solution.py:15
  14.2 0.3 collective-permute-done.1.refs_2_
  14.5 0.0 copy-start
  14.5 1.0 copy-done
  15.5 7.6 %triples.1 = f32[32,64,128]{2,1,0:T(8,128)S(1)} custom-call(f32[64,1536]{1,0:T(8,128)S(1)} %collective-permute-done.refs_0_, f32[64,1536]{1,0:T(8,128)S(1)} %copy-done, f32[64,1536]{1,0:T(8,128)S(1)} %collective-permute-done.1.refs_2_), custom_call_target="tpu_custom_call" | custom-call | flops 3221225472 | bytes 2228224 | tf_op jit(solution)/shard_map/triples/pallas_call | solution.py:49
  23.1 54.8 %all_to_all.10 = f32[16,2,64,128]{3,2,1,0:T(8,128)S(1)} all-to-all(f32[16,2,64,128]{3,2,1,0:T(8,128)S(1)} %bitcast.14), channel_id=1, replica_groups=mesh['vec'=64,'field'=16] {'field'}, dimensions={0} | all-to-all | bytes 2097152 | tf_op jit(solution)/shard_map/all_to_all | solution.py:72
  77.9 0.1 reduce_sum.9
  78.0 0.6 copy.6
  78.6 9.3 %all-to-all-start.1 = ((f32[16,2,4,128]{3,2,1,0:T(4,128)}), f32[16,2,4,128]{3,2,1,0:T(4,128)S(1)}, u32[]{:S(2)}, u32[]{:S(2)}) async-start(f32[16,2,4,128]{3,2,1,0:T(4,128)} %copy.6), calls=%async_computation.1 | async-start | bytes 131072 | tf_op jit(solution)/shard_map/all_to_all | solution.py:77
  87.9 1.9 %collective-permute-start.2 = (f32[2,64,128]{2,1,0:T(8,128)S(1)}, f32[2,64,128]{2,1,0:T(8,128)S(1)}, u32[]{:S(2)}, u32[]{:S(2)}) collective-permute-start(f32[2,64,128]{2,1,0:T(8,128)S(1)} %reduce_sum.9), channel_id=1, source_target_pairs={{0,1008},{16,0},{32,16},{48,32},{64,48},{80,64},{96,80},{112,96},{... | collective-permute-start | bytes 196616 | tf_op jit(solution)/shard_map/ppermute | solution.py:15
  89.9 1.9 %collective-permute-done.2 = f32[2,64,128]{2,1,0:T(8,128)S(1)} collective-permute-done((f32[2,64,128]{2,1,0:T(8,128)S(1)}, f32[2,64,128]{2,1,0:T(8,128)S(1)}, u32[]{:S(2)}, u32[]{:S(2)}) %collective-permute-start.2) | collective-permute-done | bytes 65568 | tf_op jit(solution)/shard_map/ppermute | solution.py:15
  91.7 0.1 reshape.23
  91.9 0.7 reshape.24
  92.6 8.0 %all-to-all-done.1 = f32[16,2,4,128]{3,2,1,0:T(4,128)S(1)} async-done(((f32[16,2,4,128]{3,2,1,0:T(4,128)}), f32[16,2,4,128]{3,2,1,0:T(4,128)S(1)}, u32[]{:S(2)}, u32[]{:S(2)}) %all-to-all-start.1) | async-done | bytes 65568 | tf_op jit(solution)/shard_map/all_to_all | solution.py:77
  100.7 0.7 copy.10
  (2 shorter events, 0.0 us)
Async XLA Ops:
  0.6 13.6 %collective-permute-start = (f32[64,1536]{1,0:T(8,128)}, f32[64,1536]{1,0:T(8,128)S(1)}, u32[]{:S(2)}, u32[]{:S(2)}) collective-permute-start(f32[64,1536]{1,0:T(8,128)} %refs_1_.1), channel_id=1, source_target_pairs={{0,16},{16,32},{32,48},{48,64},{64,80},{80,96},{96,112},{112,128},... | collective-permute-start | bytes 1179656 | tf_op jit(solution)/shard_map/ppermute | solution.py:15
  2.6 11.9 %collective-permute-start.1 = (f32[64,1536]{1,0:T(8,128)}, f32[64,1536]{1,0:T(8,128)S(1)}, u32[]{:S(2)}, u32[]{:S(2)}) collective-permute-start(f32[64,1536]{1,0:T(8,128)} %refs_1_.1), channel_id=1, source_target_pairs={{0,1008},{16,0},{32,16},{48,32},{64,48},{80,64},{96,80},{112,96},{... | collective-permute-start | bytes 1179656 | tf_op jit(solution)/shard_map/ppermute | solution.py:15
  14.5 1.0 copy-start
  78.6 22.0 %all-to-all-start.1 = ((f32[16,2,4,128]{3,2,1,0:T(4,128)}), f32[16,2,4,128]{3,2,1,0:T(4,128)S(1)}, u32[]{:S(2)}, u32[]{:S(2)}) async-start(f32[16,2,4,128]{3,2,1,0:T(4,128)} %copy.6), calls=%async_computation.1 | async-start | bytes 131072 | tf_op jit(solution)/shard_map/all_to_all | solution.py:77
  87.9 3.8 %collective-permute-start.2 = (f32[2,64,128]{2,1,0:T(8,128)S(1)}, f32[2,64,128]{2,1,0:T(8,128)S(1)}, u32[]{:S(2)}, u32[]{:S(2)}) collective-permute-start(f32[2,64,128]{2,1,0:T(8,128)S(1)} %reduce_sum.9), channel_id=1, source_target_pairs={{0,1008},{16,0},{32,16},{48,32},{64,48},{80,64},{96,80},{112,96},{... | collective-permute-start | bytes 196616 | tf_op jit(solution)/shard_map/ppermute | solution.py:15

commit v2 on v1

--- a/solution.py
+++ b/solution.py
@@ -20,10 +20,13 @@
     return high, (x - high.astype(jnp.float32)).astype(jnp.bfloat16)
 
 
-def triple_kernel(scale, a_ref, b_ref, c_ref, out_ref, w_ref):
+def triple_kernel(scale, a_ref, b_hbm, c_ref, out_ref, b_ref, w_ref, arrived):
     rows = b_ref.shape[0]
+    fetch = pltpu.make_async_copy(b_hbm, b_ref, arrived)
+    fetch.start()
     w_ref[...] = jnp.concatenate(two_halves(c_ref[...]), 0).T
     first_half = lax.broadcasted_iota(jnp.int32, (rows, 2 * rows), 1) < rows
+    fetch.wait()
 
     def step(g, carry):
         highs, lows = [], []
@@ -44,15 +47,23 @@
     lax.fori_loop(0, rows // GROUP, step, 0)
 
 
+def in_vmem(count):
+    return [pl.BlockSpec(memory_space=pltpu.VMEM)] * count
+
+
 def triples(a, b, c, scale):
     rows, fields = b.shape
     return pl.pallas_call(
         lambda *refs: triple_kernel(scale, *refs),
         name="triples",
         out_shape=jax.ShapeDtypeStruct((rows // 2, rows, 2 * rows), jnp.float32),
-        in_specs=[pl.BlockSpec(memory_space=pltpu.VMEM)] * 3,
+        in_specs=in_vmem(1) + [pl.BlockSpec(memory_space=pltpu.HBM)] + in_vmem(1),
         out_specs=pl.BlockSpec(memory_space=pltpu.VMEM),
-        scratch_shapes=[pltpu.VMEM((fields, 2 * rows), jnp.bfloat16)],
+        scratch_shapes=[
+            pltpu.VMEM((rows, fields), jnp.float32),
+            pltpu.VMEM((fields, 2 * rows), jnp.bfloat16),
+            pltpu.SemaphoreType.DMA,
+        ],
         compiler_params=pltpu.CompilerParams(vmem_limit_bytes=40 * 2**20),
         cost_estimate=pl.CostEstimate(
             flops=8 * rows**3 * fields, bytes_accessed=4 * (rows**3 + 3 * rows * fields), transcendentals=0
@@ -60,24 +71,102 @@
     )(a, b, c)
 
 
+def regroup_kernel(half_ref, arrived_ref, send_ref, own_ref, other_ref, sum_ref):
+    pairs, rows, lanes = sum_ref.shape
+    per_owner = rows // send_ref.shape[0]
+    sum_ref[...] = jnp.sum(arrived_ref[...], axis=0)
+    for g in range(send_ref.shape[0]):
+        for p in range(pairs):
+            send_ref[g, p * per_owner : (p + 1) * per_owner] = sum_ref[p, g * per_owner : (g + 1) * per_owner]
+    half = half_ref[0]
+    for p in range(pairs // 2):
+        own_ref[p] = sum_ref[half * (pairs // 2) + p]
+        other_ref[p] = sum_ref[(1 - half) * (pairs // 2) + p]
+
+
+def regroup(half, arrived, parts):
+    _, pairs, rows, lanes = arrived.shape
+    kept = jax.ShapeDtypeStruct((pairs // 2, rows, lanes), jnp.float32)
+    return pl.pallas_call(
+        regroup_kernel,
+        name="regroup",
+        out_shape=(jax.ShapeDtypeStruct((parts, pairs * rows // parts, lanes), jnp.float32), kept, kept),
+        in_specs=[pl.BlockSpec(memory_space=pltpu.SMEM)] + in_vmem(1),
+        out_specs=tuple(in_vmem(3)),
+        scratch_shapes=[pltpu.VMEM((pairs, rows, lanes), jnp.float32)],
+        compiler_params=pltpu.CompilerParams(vmem_limit_bytes=8 * 2**20),
+    )(half, arrived)
+
+
+def first_kernel(own_ref, other_ref, out_ref, sum_ref, row_ref):
+    pairs, rows, lanes = own_ref.shape
+    left = lax.broadcasted_iota(jnp.int32, (rows // 2, lanes), 1) < lanes // 2
+    for p in range(pairs):
+        sum_ref[p * rows : (p + 1) * rows] = own_ref[p] + other_ref[p]
+    for p in range(pairs):
+        even = sum_ref[pl.ds(p * rows, rows // 2, stride=2), :]
+        odd = sum_ref[pl.ds(p * rows + 1, rows // 2, stride=2), :]
+        row_ref[p * rows : p * rows + rows // 2] = jnp.where(left, even, pltpu.roll(odd, lanes // 2, 1))
+        row_ref[p * rows + rows // 2 : (p + 1) * rows] = jnp.where(left, pltpu.roll(even, lanes // 2, 1), odd)
+    for c in range(rows // 2):
+        out_ref[:, c * lanes : (c + 1) * lanes] = row_ref[pl.ds(c, 2 * pairs, stride=rows // 2), :]
+
+
+def first_rows(own, other):
+    pairs, rows, lanes = own.shape
+    return pl.pallas_call(
+        first_kernel,
+        name="first_rows",
+        out_shape=jax.ShapeDtypeStruct((2 * pairs, rows * lanes // 2), jnp.float32),
+        in_specs=in_vmem(2),
+        out_specs=pl.BlockSpec(memory_space=pltpu.VMEM),
+        scratch_shapes=[pltpu.VMEM((pairs * rows, lanes), jnp.float32)] * 2,
+        compiler_params=pltpu.CompilerParams(vmem_limit_bytes=4 * 2**20),
+    )(own, other)
+
+
+def second_kernel(turned_ref, out_ref):
+    parts, height, lanes = turned_ref.shape
+    per_owner = out_ref.shape[0]
+    pairs = height // per_owner
+    for z in range(parts // 2):
+        for p in range(pairs):
+            c = z * pairs + p
+            rows = slice(p * per_owner, (p + 1) * per_owner)
+            out_ref[:, c * lanes : (c + 1) * lanes] = turned_ref[2 * z, rows] + turned_ref[2 * z + 1, rows]
+
+
+def second_rows(turned, per_owner):
+    parts, height, lanes = turned.shape
+    return pl.pallas_call(
+        second_kernel,
+        name="second_rows",
+        out_shape=jax.ShapeDtypeStruct((per_owner, parts // 2 * height // per_owner * lanes), jnp.float32),
+        in_specs=in_vmem(1),
+        out_specs=pl.BlockSpec(memory_space=pltpu.VMEM),
+        compiler_params=pltpu.CompilerParams(vmem_limit_bytes=4 * 2**20),
+    )(turned)
+
+
 def per_device(vectors):
-    parts = lax.axis_size("field")
+    blocks, parts = lax.axis_size("vec"), lax.axis_size("field")
     rows = vectors.shape[0]
-    pairs = rows // parts // 2
     scale = 1.0 / math.sqrt(vectors.shape[1] * parts)
     previous = passed_along(vectors, "vec", 1)
     following = passed_along(vectors, "vec", -1)
     partial = triples(previous, vectors, following, scale)
-    pieces = partial.reshape(parts, pairs, rows, 2 * rows)
-    arrived = lax.all_to_all(pieces, "field", split_axis=0, concat_axis=0, tiled=True)
-    mine = arrived.sum(axis=0)
-    first = passed_along(mine, "vec", -1)
-    first = first.reshape(pairs, rows, 2, rows).transpose(0, 2, 1, 3).reshape(2 * pairs, rows * rows)
-    split = mine.reshape(pairs, parts, rows // parts, 2 * rows).transpose(1, 0, 2, 3)
-    turned = lax.all_to_all(split, "field", split_axis=0, concat_axis=0, tiled=True)
-    turned = turned.reshape(rows // 2, rows // parts, 2 * rows)
-    second = jnp.transpose(turned, (1, 0, 2)).reshape(rows // parts, rows * rows)
-    return (first, second)
+    along_z = [[2 * z + half for z in range(parts // 2)] for half in range(2)]
+    pieces = partial.reshape(parts // 2, rows // parts, rows, 2 * rows)
+    arrived = lax.all_to_all(pieces, "field", 0, 0, axis_index_groups=along_z, tiled=True)
+    half = lax.rem(lax.axis_index("field"), 2).reshape(1)
+    send, own, other = regroup(half, arrived, parts)
+    turned = lax.all_to_all(send, "field", split_axis=0, concat_axis=0, tiled=True)
+    crossed = [
+        (b * parts + f, (b - 1) % blocks * parts + (f ^ 1)) for b in range(blocks) for f in range(parts)
+    ]
+    own = passed_along(own, "vec", -1)
+    other = lax.ppermute(other, ("vec", "field"), crossed)
+    return (first_rows(own, other), second_rows(turned, rows // parts))
 
 
 def solution(mesh):

time: 102 us -> 95.8 us (0.939)
  the two profiles are of different devices: /device:TPU:32 before, /device:TPU:28 now
where the time goes in v2:
time: 95.8 us; the launch traced here: 95.4 us
  waiting for transfers between devices  49 us (51%)
  starting transfers between devices  33.8 us (35%)
  Pallas kernels  10.9 us (11%)
  local copies, waits for them, and re-layouts  1 us (1%)
    all_to_all x1, waiting for transfers between devices, per_device(): lax.all_to_all(pieces, 'field', 0, 0, axis_index_groups=along_z, tiled=True)  30 us
    all_to_all x1, starting transfers between devices, per_device(): lax.all_to_all(pieces, 'field', 0, 0, axis_index_groups=along_z, tiled=True)  16.7 us
    ppermute x3, waiting for transfers between devices, passed_along(): return lax.ppermute(x, axis, [(i, (i + by) % peers) for i in range(peers)])  9.56 us
    ppermute x1, waiting for transfers between devices, per_device(): other = lax.ppermute(other, ('vec', 'field'), crossed)  9.51 us
    pallas_call x1, Pallas kernels, triples(): pl.pallas_call(lambda *refs: triple_kernel(scale, *refs), name='triples',...  8.78 us
    ppermute x3, starting transfers between devices, passed_along(): return lax.ppermute(x, axis, [(i, (i + by) % peers) for i in range(peers)])  7.95 us
    all_to_all x1, starting transfers between devices, per_device(): lax.all_to_all(send, 'field', split_axis=0, concat_axis=0, tiled=True)  7.22 us
    ppermute x1, starting transfers between devices, per_device(): other = lax.ppermute(other, ('vec', 'field'), crossed)  1.92 us
  transfers between devices with their start and end apart: 6, of which 4 were waited for; matrix products, arithmetic and copies ran while one was open for 0% of the time, Pallas kernels for 1%

profile of v2, /device:TPU:28, one launch (start us, length us, event | category | flops | bytes accessed | tf_op | source)
XLA Modules:
  0.0 95.4 jit_solution(14866786761880554210)
XLA Ops:
  0.6 1.9 %collective-permute-start = (f32[64,1536]{1,0:T(8,128)}, f32[64,1536]{1,0:T(8,128)S(1)}, u32[]{:S(2)}, u32[]{:S(2)}) collective-permute-start(f32[64,1536]{1,0:T(8,128)} %refs_1_.1), channel_id=1, source_target_pairs={{0,16},{16,32},{32,48},{48,64},{64,80},{80,96},{96,112},{112,128},... | collective-permute-start | bytes 1179656 | tf_op jit(solution)/shard_map/ppermute | solution.py:15
  2.6 3.6 %collective-permute-start.1 = (f32[64,1536]{1,0:T(8,128)}, f32[64,1536]{1,0:T(8,128)S(1)}, u32[]{:S(2)}, u32[]{:S(2)}) collective-permute-start(f32[64,1536]{1,0:T(8,128)} %refs_1_.1), channel_id=1, source_target_pairs={{0,1008},{16,0},{32,16},{48,32},{64,48},{80,64},{96,80},{112,96},{... | collective-permute-start | bytes 1179656 | tf_op jit(solution)/shard_map/ppermute | solution.py:15
  6.2 3.7 %collective-permute-done.refs_0_ = f32[64,1536]{1,0:T(8,128)S(1)} collective-permute-done((f32[64,1536]{1,0:T(8,128)}, f32[64,1536]{1,0:T(8,128)S(1)}, u32[]{:S(2)}, u32[]{:S(2)}) %collective-permute-start) | collective-permute-done | bytes 393248 | tf_op jit(solution)/shard_map/ppermute | solution.py:15
  9.9 5.8 %collective-permute-done.1.refs_2_ = f32[64,1536]{1,0:T(8,128)S(1)} collective-permute-done((f32[64,1536]{1,0:T(8,128)}, f32[64,1536]{1,0:T(8,128)S(1)}, u32[]{:S(2)}, u32[]{:S(2)}) %collective-permute-start.1) | collective-permute-done | bytes 393248 | tf_op jit(solution)/shard_map/ppermute | solution.py:15
  15.8 0.0 copy-start
  15.8 1.0 %copy-done = f32[64,1536]{1,0:T(8,128)S(1)} copy-done((f32[64,1536]{1,0:T(8,128)S(1)}, f32[64,1536]{1,0:T(8,128)}, u32[]{:S(2)}) %copy-start) | copy-done | bytes 393240
  16.8 8.8 %triples.1 = f32[32,64,128]{2,1,0:T(8,128)} custom-call(f32[64,1536]{1,0:T(8,128)S(1)} %collective-permute-done.refs_0_, f32[64,1536]{1,0:T(8,128)S(1)} %copy-done, f32[64,1536]{1,0:T(8,128)S(1)} %collective-permute-done.1.refs_2_), custom_call_target="tpu_custom_call" | custom-call | flops 3221225472 | bytes 2228224 | tf_op jit(solution)/shard_map/triples/pallas_call | solution.py:56
  25.5 16.7 %all-to-all-start = ((f32[8,4,64,128]{3,2,1,0:T(8,128)}), f32[8,4,64,128]{3,2,1,0:T(8,128)S(1)}, u32[]{:S(2)}, u32[]{:S(2)}) async-start(f32[8,4,64,128]{3,2,1,0:T(8,128)} %bitcast.1), calls=%async_computation | async-start | bytes 2097152 | tf_op jit(solution)/shard_map/all_to_all | solution.py:160
  42.2 30.0 %all-to-all-done.arrived_ref = f32[8,4,64,128]{3,2,1,0:T(8,128)S(1)} async-done(((f32[8,4,64,128]{3,2,1,0:T(8,128)}), f32[8,4,64,128]{3,2,1,0:T(8,128)S(1)}, u32[]{:S(2)}, u32[]{:S(2)}) %all-to-all-start) | async-done | bytes 1048608 | tf_op jit(solution)/shard_map/all_to_all | solution.py:160
  72.2 0.7 regroup.1
  72.9 7.2 %all-to-all-start.1 = ((f32[16,16,128]{2,1,0:T(8,128)}), f32[16,16,128]{2,1,0:T(8,128)S(1)}, u32[]{:S(2)}, u32[]{:S(2)}) async-start(f32[16,16,128]{2,1,0:T(8,128)} %get-tuple-element.7), calls=%async_computation.1 | async-start | bytes 262144 | tf_op jit(solution)/shard_map/all_to_all | solution.py:163
  80.2 2.4 %collective-permute-start.2 = (f32[2,64,128]{2,1,0:T(8,128)S(1)}, f32[2,64,128]{2,1,0:T(8,128)S(1)}, u32[]{:S(2)}, u32[]{:S(2)}) collective-permute-start(f32[2,64,128]{2,1,0:T(8,128)S(1)} %get-tuple-element.5), channel_id=1, source_target_pairs={{0,1008},{16,0},{32,16},{48,32},{64,48},{80,64},{96,80},{112,96},{... | collective-permute-start | bytes 196616 | tf_op jit(solution)/shard_map/ppermute | solution.py:15
  82.6 1.9 %collective-permute-start.3 = (f32[2,64,128]{2,1,0:T(8,128)S(1)}, f32[2,64,128]{2,1,0:T(8,128)S(1)}, u32[]{:S(2)}, u32[]{:S(2)}) collective-permute-start(f32[2,64,128]{2,1,0:T(8,128)S(1)} %get-tuple-element.6), channel_id=1, source_target_pairs={{0,1009},{1,1008},{2,1011},{3,1010},{4,1013},{5,1012},{6,1015},{7,... | collective-permute-start | bytes 196616 | tf_op jit(solution)/shard_map/ppermute | solution.py:168
  84.5 0.0 collective-permute-done.2.own_ref
  84.5 9.5 %collective-permute-done.3.other_ref = f32[2,64,128]{2,1,0:T(8,128)S(1)} collective-permute-done((f32[2,64,128]{2,1,0:T(8,128)S(1)}, f32[2,64,128]{2,1,0:T(8,128)S(1)}, u32[]{:S(2)}, u32[]{:S(2)}) %collective-permute-start.3) | collective-permute-done | bytes 65568 | tf_op jit(solution)/shard_map/ppermute | solution.py:168
  94.0 0.8 first_rows.1
  94.8 0.0 all-to-all-done.1.turned_ref
  94.8 0.6 second_rows.1
Async XLA Ops:
  0.6 9.3 %collective-permute-start = (f32[64,1536]{1,0:T(8,128)}, f32[64,1536]{1,0:T(8,128)S(1)}, u32[]{:S(2)}, u32[]{:S(2)}) collective-permute-start(f32[64,1536]{1,0:T(8,128)} %refs_1_.1), channel_id=1, source_target_pairs={{0,16},{16,32},{32,48},{48,64},{64,80},{80,96},{96,112},{112,128},... | collective-permute-start | bytes 1179656 | tf_op jit(solution)/shard_map/ppermute | solution.py:15
  2.6 13.2 %collective-permute-start.1 = (f32[64,1536]{1,0:T(8,128)}, f32[64,1536]{1,0:T(8,128)S(1)}, u32[]{:S(2)}, u32[]{:S(2)}) collective-permute-start(f32[64,1536]{1,0:T(8,128)} %refs_1_.1), channel_id=1, source_target_pairs={{0,1008},{16,0},{32,16},{48,32},{64,48},{80,64},{96,80},{112,96},{... | collective-permute-start | bytes 1179656 | tf_op jit(solution)/shard_map/ppermute | solution.py:15
  15.8 1.0 %copy-start = (f32[64,1536]{1,0:T(8,128)S(1)}, f32[64,1536]{1,0:T(8,128)}, u32[]{:S(2)}) copy-start(f32[64,1536]{1,0:T(8,128)} %refs_1_.1) | copy-start | bytes 1179652
  25.5 46.7 %all-to-all-start = ((f32[8,4,64,128]{3,2,1,0:T(8,128)}), f32[8,4,64,128]{3,2,1,0:T(8,128)S(1)}, u32[]{:S(2)}, u32[]{:S(2)}) async-start(f32[8,4,64,128]{3,2,1,0:T(8,128)} %bitcast.1), calls=%async_computation | async-start | bytes 2097152 | tf_op jit(solution)/shard_map/all_to_all | solution.py:160
  72.9 21.8 %all-to-all-start.1 = ((f32[16,16,128]{2,1,0:T(8,128)}), f32[16,16,128]{2,1,0:T(8,128)S(1)}, u32[]{:S(2)}, u32[]{:S(2)}) async-start(f32[16,16,128]{2,1,0:T(8,128)} %get-tuple-element.7), calls=%async_computation.1 | async-start | bytes 262144 | tf_op jit(solution)/shard_map/all_to_all | solution.py:163
  80.2 4.3 %collective-permute-start.2 = (f32[2,64,128]{2,1,0:T(8,128)S(1)}, f32[2,64,128]{2,1,0:T(8,128)S(1)}, u32[]{:S(2)}, u32[]{:S(2)}) collective-permute-start(f32[2,64,128]{2,1,0:T(8,128)S(1)} %get-tuple-element.5), channel_id=1, source_target_pairs={{0,1008},{16,0},{32,16},{48,32},{64,48},{80,64},{96,80},{112,96},{... | collective-permute-start | bytes 196616 | tf_op jit(solution)/shard_map/ppermute | solution.py:15
  82.6 11.4 %collective-permute-start.3 = (f32[2,64,128]{2,1,0:T(8,128)S(1)}, f32[2,64,128]{2,1,0:T(8,128)S(1)}, u32[]{:S(2)}, u32[]{:S(2)}) collective-permute-start(f32[2,64,128]{2,1,0:T(8,128)S(1)} %get-tuple-element.6), channel_id=1, source_target_pairs={{0,1009},{1,1008},{2,1011},{3,1010},{4,1013},{5,1012},{6,1015},{7,... | collective-permute-start | bytes 196616 | tf_op jit(solution)/shard_map/ppermute | solution.py:168

commit v3 on v2

v3 whole, which is shorter than its diff:
```python
import math

import jax
import jax.numpy as jnp
from jax import lax
from jax.experimental import pallas as pl
from jax.experimental.pallas import tpu as pltpu
from jax.sharding import PartitionSpec as P


STEPS = 4


def passed_along(x, axis, by):
    peers = lax.axis_size(axis)
    return lax.ppermute(x, axis, [(i, (i + by) % peers) for i in range(peers)])


def two_halves(x):
    high = x.astype(jnp.bfloat16)
    return high, (x - high.astype(jnp.float32)).astype(jnp.bfloat16)


def in_vmem(count):
    return [pl.BlockSpec(memory_space=pltpu.VMEM)] * count


def fetch_kernel(in_ref, out_ref):
    out_ref[...] = in_ref[...]


def fetched(x):
    return pl.pallas_call(
        fetch_kernel,
        name="fetch",
        out_shape=jax.ShapeDtypeStruct(x.shape, x.dtype),
        in_specs=in_vmem(1),
        out_specs=pl.BlockSpec(memory_space=pltpu.VMEM),
        compiler_params=pltpu.CompilerParams(vmem_limit_bytes=4 * 2**20),
        cost_estimate=pl.CostEstimate(flops=0, bytes_accessed=2 * x.size * 4, transcendentals=0),
    )(x)


def triple_kernel(scale, a_ref, b_ref, c_ref, out_ref, w_ref):
    rows = b_ref.shape[0]
    group = 2 * out_ref.shape[0]

    @pl.when(pl.program_id(0) == 0)
    def _():
        w_ref[...] = jnp.concatenate(two_halves(c_ref[...]), 0).T

    first_half = lax.broadcasted_iota(jnp.int32, (rows, 2 * rows), 1) < rows
    highs, lows = [], []
    for u in range(group):
        high, low = two_halves(a_ref[pl.ds(pl.program_id(0) * group + u, 1), :] * b_ref[...])
        highs.append(high)
        lows.append(low)
    w = w_ref[...]
    r = jnp.dot(jnp.concatenate(highs, 0), w, preferred_element_type=jnp.float32)
    r = r + jnp.dot(jnp.concatenate(lows, 0), w, preferred_element_type=jnp.float32)
    r = (r + pltpu.roll(r, rows, 1)) * scale
    for u in range(group // 2):
        even = r[2 * u * rows : (2 * u + 1) * rows]
        odd = r[(2 * u + 1) * rows : (2 * u + 2) * rows]
        out_ref[u] = jnp.where(first_half, even, odd)


def triples(a, b, c, scale):
    rows, fields = b.shape
    return pl.pallas_call(
        lambda *refs: triple_kernel(scale, *refs),
        name="triples",
        grid=(STEPS,),
        out_shape=jax.ShapeDtypeStruct((rows // 2, rows, 2 * rows), jnp.float32),
        in_specs=in_vmem(3),
        out_specs=pl.BlockSpec((rows // 2 // STEPS, rows, 2 * rows), lambda s: (s, 0, 0)),
        scratch_shapes=[pltpu.VMEM((fields, 2 * rows), jnp.bfloat16)],
        compiler_params=pltpu.CompilerParams(vmem_limit_bytes=40 * 2**20),
        cost_estimate=pl.CostEstimate(
            flops=8 * rows**3 * fields, bytes_accessed=4 * (rows**3 + 3 * rows * fields), transcendentals=0
        ),
    )(a, b, c)


def regroup_kernel(half_ref, arrived_ref, send_ref, own_ref, other_ref, sum_ref):
    pairs, rows, _ = sum_ref.shape
    per_owner = rows // send_ref.shape[0]
    sum_ref[...] = jnp.sum(arrived_ref[...], axis=0)
    for g in range(send_ref.shape[0]):
        for p in range(pairs):
            send_ref[g, p * per_owner : (p + 1) * per_owner] = sum_ref[p, g * per_owner : (g + 1) * per_owner]
    half = half_ref[0]
    for p in range(pairs // 2):
        own_ref[p] = sum_ref[half * (pairs // 2) + p]
        other_ref[p] = sum_ref[(1 - half) * (pairs // 2) + p]


def regroup(half, arrived, parts):
    _, pairs, rows, lanes = arrived.shape
    kept = jax.ShapeDtypeStruct((pairs // 2, rows, lanes), jnp.float32)
    return pl.pallas_call(
        regroup_kernel,
        name="regroup",
        out_shape=(jax.ShapeDtypeStruct((parts, pairs * rows // parts, lanes), jnp.float32), kept, kept),
        in_specs=[pl.BlockSpec(memory_space=pltpu.SMEM)] + in_vmem(1),
        out_specs=tuple(in_vmem(3)),
        scratch_shapes=[pltpu.VMEM((pairs, rows, lanes), jnp.float32)],
        compiler_params=pltpu.CompilerParams(vmem_limit_bytes=8 * 2**20),
    )(half, arrived)


def finish_kernel(own_ref, other_ref, turned_ref, first_ref, second_ref, sum_ref, row_ref):
    pairs, rows, lanes = own_ref.shape
    left = lax.broadcasted_iota(jnp.int32, (rows // 2, lanes), 1) < lanes // 2
    for p in range(pairs):
        sum_ref[p * rows : (p + 1) * rows] = own_ref[p] + other_ref[p]
    for p in range(pairs):
        even = sum_ref[pl.ds(p * rows, rows // 2, stride=2), :]
        odd = sum_ref[pl.ds(p * rows + 1, rows // 2, stride=2), :]
        row_ref[p * rows : p * rows + rows // 2] = jnp.where(left, even, pltpu.roll(odd, lanes // 2, 1))
        row_ref[p * rows + rows // 2 : (p + 1) * rows] = jnp.where(left, pltpu.roll(even, lanes // 2, 1), odd)
    for c in range(rows // 2):
        first_ref[:, c * lanes : (c + 1) * lanes] = row_ref[pl.ds(c, 2 * pairs, stride=rows // 2), :]

    parts, height, _ = turned_ref.shape
    per_owner = second_ref.shape[0]
    pairs = height // per_owner
    for z in range(parts // 2):
        for p in range(pairs):
            c = z * pairs + p
            at = slice(p * per_owner, (p + 1) * per_owner)
            second_ref[:, c * lanes : (c + 1) * lanes] = turned_ref[2 * z, at] + turned_ref[2 * z + 1, at]


def finish(own, other, turned):
    pairs, rows, lanes = own.shape
    out = jax.ShapeDtypeStruct((2 * pairs, rows * lanes // 2), jnp.float32)
    return pl.pallas_call(
        finish_kernel,
        name="finish",
        out_shape=(out, out),
        in_specs=in_vmem(3),
        out_specs=tuple(in_vmem(2)),
        scratch_shapes=[pltpu.VMEM((pairs * rows, lanes), jnp.float32)] * 2,
        compiler_params=pltpu.CompilerParams(vmem_limit_bytes=4 * 2**20),
    )(own, other, turned)


def per_device(vectors):
    blocks, parts = lax.axis_size("vec"), lax.axis_size("field")
    rows = vectors.shape[0]
    scale = 1.0 / math.sqrt(vectors.shape[1] * parts)
    previous = passed_along(vectors, "vec", 1)
    following = passed_along(vectors, "vec", -1)
    partial = triples(previous, fetched(vectors), following, scale)
    along_z = [[2 * z + half for z in range(parts // 2)] for half in range(2)]
    pieces = partial.reshape(parts // 2, rows // parts, rows, 2 * rows)
    arrived = lax.all_to_all(pieces, "field", 0, 0, axis_index_groups=along_z, tiled=True)
    half = (lax.axis_index("field") & 1).reshape(1)
    send, own, other = regroup(half, arrived, parts)
    crossed = [(b * parts + f, (b - 1) % blocks * parts + (f ^ 1)) for b in range(blocks) for f in range(parts)]
    turned = lax.all_to_all(send, "field", split_axis=0, concat_axis=0, tiled=True)
    other = lax.ppermute(other, ("vec", "field"), crossed)
    own = passed_along(own, "vec", -1)
    return finish(own, other, turned)


def solution(mesh):
    placed = (P("vec", "field"),)
    return jax.shard_map(
        per_device,
        mesh=mesh,
        in_specs=placed,
        out_specs=(P(("vec", "field"), None), P(("vec", "field"), None)),
        check_vma=False,
    )
```

time: 95.8 us -> 93.8 us (0.979)
  waiting for transfers between devices: 49 us -> 48 us
  Pallas kernels: 10.9 us -> 9.91 us
    ppermute x3, waiting for transfers between devices: 9.56 us -> 8.53 us  [passed_along(): return lax.ppermute(x, axis, [(i, (i + by) % peers) for i in range(peers)])]
  transfers between devices with their start and end apart: 6 -> 6, of which waited for: 4 -> 4; matrix products, arithmetic and copies ran while one was open for 0% -> 0% of each run, Pallas kernels for 1% -> 0%
where the time goes in v3:
time: 93.8 us; the launch traced here: 93.4 us
  waiting for transfers between devices  48 us (51%)
  starting transfers between devices  33.8 us (36%)
  Pallas kernels  9.91 us (11%)
  local copies, waits for them, and re-layouts  1 us (1%)
    all_to_all x1, waiting for transfers between devices, per_device(): lax.all_to_all(pieces, 'field', 0, 0, axis_index_groups=along_z, tiled=True)  30 us
    all_to_all x1, starting transfers between devices, per_device(): lax.all_to_all(pieces, 'field', 0, 0, axis_index_groups=along_z, tiled=True)  16.7 us
    ppermute x1, waiting for transfers between devices, per_device(): other = lax.ppermute(other, ('vec', 'field'), crossed)  9.53 us
    ppermute x3, waiting for transfers between devices, passed_along(): return lax.ppermute(x, axis, [(i, (i + by) % peers) for i in range(peers)])  8.53 us
    pallas_call x1, Pallas kernels, triples(): pl.pallas_call(lambda *refs: triple_kernel(scale, *refs), name='triples',...  8.4 us
    ppermute x3, starting transfers between devices, passed_along(): return lax.ppermute(x, axis, [(i, (i + by) % peers) for i in range(peers)])  7.94 us
    all_to_all x1, starting transfers between devices, per_device(): lax.all_to_all(send, 'field', split_axis=0, concat_axis=0, tiled=True)  7.22 us
    ppermute x1, starting transfers between devices, per_device(): other = lax.ppermute(other, ('vec', 'field'), crossed)  1.92 us
  transfers between devices with their start and end apart: 6, of which 4 were waited for; matrix products, arithmetic and copies ran while one was open for 0% of the time, Pallas kernels for 0%

profile of v3, /device:TPU:28, one launch (start us, length us, event | category | flops | bytes accessed | tf_op | source)
XLA Modules:
  0.0 93.4 jit_solution(10446737855693433789)
XLA Ops:
  0.6 1.9 %collective-permute-start = (f32[64,1536]{1,0:T(8,128)}, f32[64,1536]{1,0:T(8,128)S(1)}, u32[]{:S(2)}, u32[]{:S(2)}) collective-permute-start(f32[64,1536]{1,0:T(8,128)} %in_ref.1), channel_id=1, source_target_pairs={{0,16},{16,32},{32,48},{48,64},{64,80},{80,96},{96,112},{112,128},... | collective-permute-start | bytes 1179656 | tf_op jit(solution)/shard_map/ppermute | solution.py:16
  2.6 3.6 %collective-permute-start.1 = (f32[64,1536]{1,0:T(8,128)}, f32[64,1536]{1,0:T(8,128)S(1)}, u32[]{:S(2)}, u32[]{:S(2)}) collective-permute-start(f32[64,1536]{1,0:T(8,128)} %in_ref.1), channel_id=1, source_target_pairs={{0,1008},{16,0},{32,16},{48,32},{64,48},{80,64},{96,80},{112,96},{... | collective-permute-start | bytes 1179656 | tf_op jit(solution)/shard_map/ppermute | solution.py:16
  6.2 0.0 copy-start
  6.2 1.0 %copy-done = f32[64,1536]{1,0:T(8,128)S(1)} copy-done((f32[64,1536]{1,0:T(8,128)S(1)}, f32[64,1536]{1,0:T(8,128)}, u32[]{:S(2)}) %copy-start) | copy-done | bytes 393240
  7.2 2.7 %collective-permute-done.refs_0_ = f32[64,1536]{1,0:T(8,128)S(1)} collective-permute-done((f32[64,1536]{1,0:T(8,128)}, f32[64,1536]{1,0:T(8,128)S(1)}, u32[]{:S(2)}, u32[]{:S(2)}) %collective-permute-start) | collective-permute-done | bytes 393248 | tf_op jit(solution)/shard_map/ppermute | solution.py:16
  9.9 5.8 %collective-permute-done.1.refs_2_ = f32[64,1536]{1,0:T(8,128)S(1)} collective-permute-done((f32[64,1536]{1,0:T(8,128)}, f32[64,1536]{1,0:T(8,128)S(1)}, u32[]{:S(2)}, u32[]{:S(2)}) %collective-permute-start.1) | collective-permute-done | bytes 393248 | tf_op jit(solution)/shard_map/ppermute | solution.py:16
  15.8 8.4 %triples.1 = f32[32,64,128]{2,1,0:T(8,128)} custom-call(f32[64,1536]{1,0:T(8,128)S(1)} %collective-permute-done.refs_0_, f32[64,1536]{1,0:T(8,128)S(1)} %fetch.1.refs_1_, f32[64,1536]{1,0:T(8,128)S(1)} %collective-permute-done.1.refs_2_), custom_call_target="tpu_custom_call" | custom-call | flops 3221225472 | bytes 2228224 | tf_op jit(solution)/shard_map/triples/pallas_call | solution.py:70
  24.2 16.7 %all-to-all-start = ((f32[8,4,64,128]{3,2,1,0:T(8,128)}), f32[8,4,64,128]{3,2,1,0:T(8,128)S(1)}, u32[]{:S(2)}, u32[]{:S(2)}) async-start(f32[8,4,64,128]{3,2,1,0:T(8,128)} %bitcast.1), calls=%async_computation | async-start | bytes 2097152 | tf_op jit(solution)/shard_map/all_to_all | solution.py:158
  40.8 30.0 %all-to-all-done.arrived_ref = f32[8,4,64,128]{3,2,1,0:T(8,128)S(1)} async-done(((f32[8,4,64,128]{3,2,1,0:T(8,128)}), f32[8,4,64,128]{3,2,1,0:T(8,128)S(1)}, u32[]{:S(2)}, u32[]{:S(2)}) %all-to-all-start) | async-done | bytes 1048608 | tf_op jit(solution)/shard_map/all_to_all | solution.py:158
  70.8 0.7 regroup.1
  71.5 7.2 %all-to-all-start.1 = ((f32[16,16,128]{2,1,0:T(8,128)}), f32[16,16,128]{2,1,0:T(8,128)S(1)}, u32[]{:S(2)}, u32[]{:S(2)}) async-start(f32[16,16,128]{2,1,0:T(8,128)} %get-tuple-element.7), calls=%async_computation.1 | async-start | bytes 262144 | tf_op jit(solution)/shard_map/all_to_all | solution.py:162
  78.8 2.4 %collective-permute-start.2 = (f32[2,64,128]{2,1,0:T(8,128)S(1)}, f32[2,64,128]{2,1,0:T(8,128)S(1)}, u32[]{:S(2)}, u32[]{:S(2)}) collective-permute-start(f32[2,64,128]{2,1,0:T(8,128)S(1)} %get-tuple-element.5), channel_id=1, source_target_pairs={{0,1008},{16,0},{32,16},{48,32},{64,48},{80,64},{96,80},{112,96},{... | collective-permute-start | bytes 196616 | tf_op jit(solution)/shard_map/ppermute | solution.py:16
  81.2 1.9 %collective-permute-start.3 = (f32[2,64,128]{2,1,0:T(8,128)S(1)}, f32[2,64,128]{2,1,0:T(8,128)S(1)}, u32[]{:S(2)}, u32[]{:S(2)}) collective-permute-start(f32[2,64,128]{2,1,0:T(8,128)S(1)} %get-tuple-element.6), channel_id=1, source_target_pairs={{0,1009},{1,1008},{2,1011},{3,1010},{4,1013},{5,1012},{6,1015},{7,... | collective-permute-start | bytes 196616 | tf_op jit(solution)/shard_map/ppermute | solution.py:163
  83.1 0.0 collective-permute-done.2.own_ref
  83.1 9.5 %collective-permute-done.3.other_ref = f32[2,64,128]{2,1,0:T(8,128)S(1)} collective-permute-done((f32[2,64,128]{2,1,0:T(8,128)S(1)}, f32[2,64,128]{2,1,0:T(8,128)S(1)}, u32[]{:S(2)}, u32[]{:S(2)}) %collective-permute-start.3) | collective-permute-done | bytes 65568 | tf_op jit(solution)/shard_map/ppermute | solution.py:163
  92.6 0.0 all-to-all-done.1.turned_ref
  92.6 0.8 finish.1
  (1 shorter events, 0.0 us)
Async XLA Ops:
  0.6 9.3 %collective-permute-start = (f32[64,1536]{1,0:T(8,128)}, f32[64,1536]{1,0:T(8,128)S(1)}, u32[]{:S(2)}, u32[]{:S(2)}) collective-permute-start(f32[64,1536]{1,0:T(8,128)} %in_ref.1), channel_id=1, source_target_pairs={{0,16},{16,32},{32,48},{48,64},{64,80},{80,96},{96,112},{112,128},... | collective-permute-start | bytes 1179656 | tf_op jit(solution)/shard_map/ppermute | solution.py:16
  2.6 13.2 %collective-permute-start.1 = (f32[64,1536]{1,0:T(8,128)}, f32[64,1536]{1,0:T(8,128)S(1)}, u32[]{:S(2)}, u32[]{:S(2)}) collective-permute-start(f32[64,1536]{1,0:T(8,128)} %in_ref.1), channel_id=1, source_target_pairs={{0,1008},{16,0},{32,16},{48,32},{64,48},{80,64},{96,80},{112,96},{... | collective-permute-start | bytes 1179656 | tf_op jit(solution)/shard_map/ppermute | solution.py:16
  6.2 1.0 %copy-start = (f32[64,1536]{1,0:T(8,128)S(1)}, f32[64,1536]{1,0:T(8,128)}, u32[]{:S(2)}) copy-start(f32[64,1536]{1,0:T(8,128)} %in_ref.1) | copy-start | bytes 1179652
  24.2 46.7 %all-to-all-start = ((f32[8,4,64,128]{3,2,1,0:T(8,128)}), f32[8,4,64,128]{3,2,1,0:T(8,128)S(1)}, u32[]{:S(2)}, u32[]{:S(2)}) async-start(f32[8,4,64,128]{3,2,1,0:T(8,128)} %bitcast.1), calls=%async_computation | async-start | bytes 2097152 | tf_op jit(solution)/shard_map/all_to_all | solution.py:158
  71.5 21.1 %all-to-all-start.1 = ((f32[16,16,128]{2,1,0:T(8,128)}), f32[16,16,128]{2,1,0:T(8,128)S(1)}, u32[]{:S(2)}, u32[]{:S(2)}) async-start(f32[16,16,128]{2,1,0:T(8,128)} %get-tuple-element.7), calls=%async_computation.1 | async-start | bytes 262144 | tf_op jit(solution)/shard_map/all_to_all | solution.py:162
  78.8 4.3 %collective-permute-start.2 = (f32[2,64,128]{2,1,0:T(8,128)S(1)}, f32[2,64,128]{2,1,0:T(8,128)S(1)}, u32[]{:S(2)}, u32[]{:S(2)}) collective-permute-start(f32[2,64,128]{2,1,0:T(8,128)S(1)} %get-tuple-element.5), channel_id=1, source_target_pairs={{0,1008},{16,0},{32,16},{48,32},{64,48},{80,64},{96,80},{112,96},{... | collective-permute-start | bytes 196616 | tf_op jit(solution)/shard_map/ppermute | solution.py:16
  81.2 11.5 %collective-permute-start.3 = (f32[2,64,128]{2,1,0:T(8,128)S(1)}, f32[2,64,128]{2,1,0:T(8,128)S(1)}, u32[]{:S(2)}, u32[]{:S(2)}) collective-permute-start(f32[2,64,128]{2,1,0:T(8,128)S(1)} %get-tuple-element.6), channel_id=1, source_target_pairs={{0,1009},{1,1008},{2,1011},{3,1010},{4,1013},{5,1012},{6,1015},{7,... | collective-permute-start | bytes 196616 | tf_op jit(solution)/shard_map/ppermute | solution.py:163

commit v4 on v3

--- a/solution.py
+++ b/solution.py
@@ -8,7 +8,7 @@
 from jax.sharding import PartitionSpec as P
 
 
-STEPS = 4
+GROUP = 16
 
 
 def passed_along(x, axis, by):
@@ -41,45 +41,79 @@
     )(x)
 
 
-def triple_kernel(scale, a_ref, b_ref, c_ref, out_ref, w_ref):
+def weights_kernel(c_ref, w_ref):
+    w_ref[...] = jnp.concatenate(two_halves(c_ref[...]), 0).T
+
+
+def weights(c):
+    rows, fields = c.shape
+    return pl.pallas_call(
+        weights_kernel,
+        name="weights",
+        out_shape=jax.ShapeDtypeStruct((fields, 2 * rows), jnp.bfloat16),
+        in_specs=in_vmem(1),
+        out_specs=pl.BlockSpec(memory_space=pltpu.VMEM),
+        compiler_params=pltpu.CompilerParams(vmem_limit_bytes=8 * 2**20),
+        cost_estimate=pl.CostEstimate(flops=c.size, bytes_accessed=8 * c.size, transcendentals=0),
+    )(c)
+
+
+def triple_kernel(scale, run, stride, start_ref, a_ref, b_ref, w_ref, out_ref):
     rows = b_ref.shape[0]
-    group = 2 * out_ref.shape[0]
-
-    @pl.when(pl.program_id(0) == 0)
-    def _():
-        w_ref[...] = jnp.concatenate(two_halves(c_ref[...]), 0).T
-
     first_half = lax.broadcasted_iota(jnp.int32, (rows, 2 * rows), 1) < rows
+    start = start_ref[0] + pl.program_id(0) * (GROUP // run * stride)
     highs, lows = [], []
-    for u in range(group):
-        high, low = two_halves(a_ref[pl.ds(pl.program_id(0) * group + u, 1), :] * b_ref[...])
+    for u in range(GROUP):
+        high, low = two_halves(a_ref[pl.ds(start + u // run * stride + u % run, 1), :] * b_ref[...])
         highs.append(high)
         lows.append(low)
     w = w_ref[...]
     r = jnp.dot(jnp.concatenate(highs, 0), w, preferred_element_type=jnp.float32)
     r = r + jnp.dot(jnp.concatenate(lows, 0), w, preferred_element_type=jnp.float32)
     r = (r + pltpu.roll(r, rows, 1)) * scale
-    for u in range(group // 2):
+    for u in range(GROUP // 2):
         even = r[2 * u * rows : (2 * u + 1) * rows]
         odd = r[(2 * u + 1) * rows : (2 * u + 2) * rows]
         out_ref[u] = jnp.where(first_half, even, odd)
 
 
-def triples(a, b, c, scale):
+def triples(start, a, b, w, scale, steps, run, stride):
     rows, fields = b.shape
     return pl.pallas_call(
-        lambda *refs: triple_kernel(scale, *refs),
+        lambda *refs: triple_kernel(scale, run, stride, *refs),
         name="triples",
-        grid=(STEPS,),
-        out_shape=jax.ShapeDtypeStruct((rows // 2, rows, 2 * rows), jnp.float32),
-        in_specs=in_vmem(3),
-        out_specs=pl.BlockSpec((rows // 2 // STEPS, rows, 2 * rows), lambda s: (s, 0, 0)),
-        scratch_shapes=[pltpu.VMEM((fields, 2 * rows), jnp.bfloat16)],
+        grid=(steps,),
+        out_shape=jax.ShapeDtypeStruct((steps * GROUP // 2, rows, 2 * rows), jnp.float32),
+        in_specs=[pl.BlockSpec(memory_space=pltpu.SMEM)] + in_vmem(3),
+        out_specs=pl.BlockSpec((GROUP // 2, rows, 2 * rows), lambda s: (s, 0, 0)),
         compiler_params=pltpu.CompilerParams(vmem_limit_bytes=40 * 2**20),
         cost_estimate=pl.CostEstimate(
-            flops=8 * rows**3 * fields, bytes_accessed=4 * (rows**3 + 3 * rows * fields), transcendentals=0
+            flops=8 * steps * GROUP * rows**2 * fields,
+            bytes_accessed=4 * (steps * GROUP * rows**2 + 3 * rows * fields),
+            transcendentals=0,
         ),
-    )(a, b, c)
+    )(start.reshape(1), a, b, w)
+
+
+def merge_kernel(mine_ref, low_ref, high_ref, out_ref):
+    pairs = low_ref.shape[0]
+    out_ref[:pairs] = mine_ref[:pairs] + low_ref[...]
+    out_ref[pairs:] = mine_ref[pairs:] + high_ref[...]
+
+
+def merge(mine, low, high, owners):
+    pairs, rows, lanes = mine.shape[0] // owners, *mine.shape[1:]
+    whole = pl.BlockSpec((pairs, rows, lanes), lambda m: (m, 0, 0))
+    part = pl.BlockSpec((pairs // 2, rows, lanes), lambda m: (m, 0, 0))
+    return pl.pallas_call(
+        merge_kernel,
+        name="merge",
+        grid=(owners,),
+        out_shape=jax.ShapeDtypeStruct(mine.shape, jnp.float32),
+        in_specs=[whole, part, part],
+        out_specs=whole,
+        compiler_params=pltpu.CompilerParams(vmem_limit_bytes=8 * 2**20),
+    )(mine, low, high)
 
 
 def regroup_kernel(half_ref, arrived_ref, send_ref, own_ref, other_ref, sum_ref):
@@ -152,9 +186,25 @@
     scale = 1.0 / math.sqrt(vectors.shape[1] * parts)
     previous = passed_along(vectors, "vec", 1)
     following = passed_along(vectors, "vec", -1)
-    partial = triples(previous, fetched(vectors), following, scale)
-    along_z = [[2 * z + half for z in range(parts // 2)] for half in range(2)]
-    pieces = partial.reshape(parts // 2, rows // parts, rows, 2 * rows)
+    here = fetched(vectors)
+    peers = parts // 2
+    run = rows // peers
+    parity = lax.axis_index("field") // 2 % 2
+    w = weights(following)
+
+    def sent(part, towards):
+        sums = triples(
+            (1 - parity) * run + part * (run // 2), previous, here, w, scale, rows // 4 // GROUP, run // 2, 2 * run
+        )
+        moves = [(2 * z + half, 2 * (towards(z) % peers) + half) for z in range(peers) for half in range(2)]
+        return lax.ppermute(sums, "field", moves)
+
+    low = sent(0, lambda z: z ^ 1)
+    high = sent(1, lambda z: z + 1 if z % 2 else z - 1)
+    mine = triples(parity * run, previous, here, w, scale, rows // 2 // GROUP, run, 2 * run)
+    merged = merge(mine, low, high, peers // 2)
+    along_z = [[2 * z + half for z in range(q, peers, 2)] for q in range(2) for half in range(2)]
+    pieces = merged.reshape(peers // 2, run // 2, rows, 2 * rows)
     arrived = lax.all_to_all(pieces, "field", 0, 0, axis_index_groups=along_z, tiled=True)
     half = (lax.axis_index("field") & 1).reshape(1)
     send, own, other = regroup(half, arrived, parts)

time: 93.8 us -> 93.2 us (level)
  the two profiles are of different devices: /device:TPU:28 before, /device:TPU:1 now
where the time goes in v4:
time: 93.2 us; the launch traced here: 92.8 us
  starting transfers between devices  63.4 us (68%)
  waiting for transfers between devices  17 us (18%)
  Pallas kernels  10.6 us (11%)
  local copies, waits for them, and re-layouts  1.01 us (1%)
    ppermute x3, starting transfers between devices, passed_along(): return lax.ppermute(x, axis, [(i, (i + by) % peers) for i in range(peers)])  32.3 us
    all_to_all x1, starting transfers between devices, per_device(): lax.all_to_all(send, 'field', split_axis=0, concat_axis=0, tiled=True)  11 us
    ppermute x1, starting transfers between devices, per_device(): other = lax.ppermute(other, ('vec', 'field'), crossed)  9.54 us
    all_to_all x1, waiting for transfers between devices, per_device(): lax.all_to_all(pieces, 'field', 0, 0, axis_index_groups=along_z, tiled=True)  9.49 us
    pallas_call x3, Pallas kernels, triples(): pl.pallas_call(lambda *refs: triple_kernel(scale, run, stride, *refs), na...  7.51 us
    ppermute x2, starting transfers between devices, sent(): return lax.ppermute(sums, 'field', moves)  6.73 us
    ppermute x3, waiting for transfers between devices, passed_along(): return lax.ppermute(x, axis, [(i, (i + by) % peers) for i in range(peers)])  6.24 us
    all_to_all x1, starting transfers between devices, per_device(): lax.all_to_all(pieces, 'field', 0, 0, axis_index_groups=along_z, tiled=True)  3.8 us
  transfers between devices with their start and end apart: 8, of which 3 were waited for; matrix products, arithmetic and copies ran while one was open for 0% of the time, Pallas kernels for 6%

profile of v4, /device:TPU:1, one launch (start us, length us, event | category | flops | bytes accessed | tf_op | source)
XLA Modules:
  0.0 92.8 jit_solution(6097028686896336015)
XLA Ops:
  0.6 16.0 %collective-permute-start.1 = (f32[64,1536]{1,0:T(8,128)}, f32[64,1536]{1,0:T(8,128)S(1)}, u32[]{:S(2)}, u32[]{:S(2)}) collective-permute-start(f32[64,1536]{1,0:T(8,128)} %in_ref.1), channel_id=1, source_target_pairs={{0,1008},{16,0},{32,16},{48,32},{64,48},{80,64},{96,80},{112,96},{... | collective-permute-start | bytes 1179656 | tf_op jit(solution)/shard_map/ppermute | solution.py:16
  16.7 1.9 %collective-permute-start = (f32[64,1536]{1,0:T(8,128)}, f32[64,1536]{1,0:T(8,128)S(1)}, u32[]{:S(2)}, u32[]{:S(2)}) collective-permute-start(f32[64,1536]{1,0:T(8,128)} %in_ref.1), channel_id=1, source_target_pairs={{0,16},{16,32},{32,48},{48,64},{64,80},{80,96},{96,112},{112,128},... | collective-permute-start | bytes 1179656 | tf_op jit(solution)/shard_map/ppermute | solution.py:16
  18.6 0.0 copy-start
  18.6 1.0 %copy-done = f32[64,1536]{1,0:T(8,128)S(1)} copy-done((f32[64,1536]{1,0:T(8,128)S(1)}, f32[64,1536]{1,0:T(8,128)}, u32[]{:S(2)}) %copy-start) | copy-done | bytes 393240
  19.7 0.0 collective-permute-done.1.c_ref
  19.7 0.2 weights.1.refs_3_
  19.8 6.2 %collective-permute-done.refs_1_ = f32[64,1536]{1,0:T(8,128)S(1)} collective-permute-done((f32[64,1536]{1,0:T(8,128)}, f32[64,1536]{1,0:T(8,128)S(1)}, u32[]{:S(2)}, u32[]{:S(2)}) %collective-permute-start) | collective-permute-done | bytes 393248 | tf_op jit(solution)/shard_map/ppermute | solution.py:16
  26.1 1.9 %triples.4 = f32[8,64,128]{2,1,0:T(8,128)S(1)} custom-call(s32[1]{0:T(128)} %bitcast.2.refs_0_, f32[64,1536]{1,0:T(8,128)S(1)} %collective-permute-done.refs_1_, f32[64,1536]{1,0:T(8,128)S(1)} %fetch.1.refs_2_, bf16[1536,128]{1,0:T(8,128)(2,1)S(1)} %weights.1.refs_3_), custom_call_target="tpu_custom_call" | custom-call | flops 805306368 | bytes 1441792 | tf_op jit(solution)/shard_map/triples/pallas_call | solution.py:82
  28.0 1.9 %collective-permute-start.2 = (f32[8,64,128]{2,1,0:T(8,128)S(1)}, f32[8,64,128]{2,1,0:T(8,128)S(1)}, u32[]{:S(2)}, u32[]{:S(2)}) collective-permute-start(f32[8,64,128]{2,1,0:T(8,128)S(1)} %triples.4), channel_id=1, source_target_pairs={{0,2},{1,3},{2,0},{3,1},{4,6},{5,7},{6,4},{7,5},{8,10},{9,11},{10,... | collective-permute-start | bytes 786440 | tf_op jit(solution)/shard_map/ppermute | solution.py:200
  29.9 1.9 %triples.5 = f32[8,64,128]{2,1,0:T(8,128)S(1)} custom-call(s32[1]{0:T(128)} %bitcast.3.refs_0_, f32[64,1536]{1,0:T(8,128)S(1)} %collective-permute-done.refs_1_, f32[64,1536]{1,0:T(8,128)S(1)} %fetch.1.refs_2_, bf16[1536,128]{1,0:T(8,128)(2,1)S(1)} %weights.1.refs_3_), custom_call_target="tpu_custom_call" | custom-call | flops 805306368 | bytes 1441792 | tf_op jit(solution)/shard_map/triples/pallas_call | solution.py:82
  31.8 4.8 %collective-permute-start.3 = (f32[8,64,128]{2,1,0:T(8,128)S(1)}, f32[8,64,128]{2,1,0:T(8,128)S(1)}, u32[]{:S(2)}, u32[]{:S(2)}) collective-permute-start(f32[8,64,128]{2,1,0:T(8,128)S(1)} %triples.5), channel_id=1, source_target_pairs={{0,14},{1,15},{2,4},{3,5},{4,2},{5,3},{6,8},{7,9},{8,6},{9,7},{10,... | collective-permute-start | bytes 786440 | tf_op jit(solution)/shard_map/ppermute | solution.py:200
  36.6 3.8 %triples.3.mine_ref = f32[16,64,128]{2,1,0:T(8,128)S(1)} custom-call(s32[1]{0:T(128)} %bitcast.1.refs_0_, f32[64,1536]{1,0:T(8,128)S(1)} %collective-permute-done.refs_1_, f32[64,1536]{1,0:T(8,128)S(1)} %fetch.1.refs_2_, bf16[1536,128]{1,0:T(8,128)(2,1)S(1)} %weights.1.refs_3_), custom_call_target="tpu_custom_call" | custom-call | flops 1610612736 | bytes 1703936 | tf_op jit(solution)/shard_map/triples/pallas_call | solution.py:82
  40.4 0.0 collective-permute-done.2.low_ref
  40.4 0.0 collective-permute-done.3.high_ref
  40.4 1.4 %merge.1 = f32[16,64,128]{2,1,0:T(8,128)} custom-call(f32[16,64,128]{2,1,0:T(8,128)S(1)} %triples.3.mine_ref, f32[8,64,128]{2,1,0:T(8,128)S(1)} %collective-permute-done.2.low_ref, f32[8,64,128]{2,1,0:T(8,128)S(1)} %collective-permute-done.3.high_ref), custom_call_target="tpu_custom_call" | custom-call | tf_op jit(solution)/shard_map/merge/pallas_call | solution.py:108
  41.8 3.8 %all-to-all-start = ((f32[4,4,64,128]{3,2,1,0:T(8,128)}), f32[4,4,64,128]{3,2,1,0:T(8,128)S(1)}, u32[]{:S(2)}, u32[]{:S(2)}) async-start(f32[4,4,64,128]{3,2,1,0:T(8,128)} %bitcast.4), calls=%async_computation | async-start | bytes 1048576 | tf_op jit(solution)/shard_map/all_to_all | solution.py:208
  45.6 9.5 %all-to-all-done.arrived_ref = f32[4,4,64,128]{3,2,1,0:T(8,128)S(1)} async-done(((f32[4,4,64,128]{3,2,1,0:T(8,128)}), f32[4,4,64,128]{3,2,1,0:T(8,128)S(1)}, u32[]{:S(2)}, u32[]{:S(2)}) %all-to-all-start) | async-done | bytes 524320 | tf_op jit(solution)/shard_map/all_to_all | solution.py:208
  55.1 0.7 regroup.1
  55.8 11.0 %all-to-all-start.1 = ((f32[16,16,128]{2,1,0:T(8,128)}), f32[16,16,128]{2,1,0:T(8,128)S(1)}, u32[]{:S(2)}, u32[]{:S(2)}) async-start(f32[16,16,128]{2,1,0:T(8,128)} %get-tuple-element.7), calls=%async_computation.1 | async-start | bytes 262144 | tf_op jit(solution)/shard_map/all_to_all | solution.py:212
  66.7 14.4 %collective-permute-start.4 = (f32[2,64,128]{2,1,0:T(8,128)S(1)}, f32[2,64,128]{2,1,0:T(8,128)S(1)}, u32[]{:S(2)}, u32[]{:S(2)}) collective-permute-start(f32[2,64,128]{2,1,0:T(8,128)S(1)} %get-tuple-element.5), channel_id=1, source_target_pairs={{0,1008},{16,0},{32,16},{48,32},{64,48},{80,64},{96,80},{112,96},{... | collective-permute-start | bytes 196616 | tf_op jit(solution)/shard_map/ppermute | solution.py:16
  81.1 9.5 %collective-permute-start.5 = (f32[2,64,128]{2,1,0:T(8,128)S(1)}, f32[2,64,128]{2,1,0:T(8,128)S(1)}, u32[]{:S(2)}, u32[]{:S(2)}) collective-permute-start(f32[2,64,128]{2,1,0:T(8,128)S(1)} %get-tuple-element.6), channel_id=1, source_target_pairs={{0,1009},{1,1008},{2,1011},{3,1010},{4,1013},{5,1012},{6,1015},{7,... | collective-permute-start | bytes 196616 | tf_op jit(solution)/shard_map/ppermute | solution.py:213
  90.7 0.0 collective-permute-done.4.own_ref
  90.7 1.3 %collective-permute-done.5.other_ref = f32[2,64,128]{2,1,0:T(8,128)S(1)} collective-permute-done((f32[2,64,128]{2,1,0:T(8,128)S(1)}, f32[2,64,128]{2,1,0:T(8,128)S(1)}, u32[]{:S(2)}, u32[]{:S(2)}) %collective-permute-start.5) | collective-permute-done | bytes 65568 | tf_op jit(solution)/shard_map/ppermute | solution.py:213
  92.0 0.0 all-to-all-done.1.turned_ref
  92.0 0.8 finish.1
  (1 shorter events, 0.0 us)
Async XLA Ops:
  0.6 19.0 %collective-permute-start.1 = (f32[64,1536]{1,0:T(8,128)}, f32[64,1536]{1,0:T(8,128)S(1)}, u32[]{:S(2)}, u32[]{:S(2)}) collective-permute-start(f32[64,1536]{1,0:T(8,128)} %in_ref.1), channel_id=1, source_target_pairs={{0,1008},{16,0},{32,16},{48,32},{64,48},{80,64},{96,80},{112,96},{... | collective-permute-start | bytes 1179656 | tf_op jit(solution)/shard_map/ppermute | solution.py:16
  16.7 9.4 %collective-permute-start = (f32[64,1536]{1,0:T(8,128)}, f32[64,1536]{1,0:T(8,128)S(1)}, u32[]{:S(2)}, u32[]{:S(2)}) collective-permute-start(f32[64,1536]{1,0:T(8,128)} %in_ref.1), channel_id=1, source_target_pairs={{0,16},{16,32},{32,48},{48,64},{64,80},{80,96},{96,112},{112,128},... | collective-permute-start | bytes 1179656 | tf_op jit(solution)/shard_map/ppermute | solution.py:16
  18.6 1.0 %copy-start = (f32[64,1536]{1,0:T(8,128)S(1)}, f32[64,1536]{1,0:T(8,128)}, u32[]{:S(2)}) copy-start(f32[64,1536]{1,0:T(8,128)} %in_ref.1) | copy-start | bytes 1179652
  28.0 12.4 %collective-permute-start.2 = (f32[8,64,128]{2,1,0:T(8,128)S(1)}, f32[8,64,128]{2,1,0:T(8,128)S(1)}, u32[]{:S(2)}, u32[]{:S(2)}) collective-permute-start(f32[8,64,128]{2,1,0:T(8,128)S(1)} %triples.4), channel_id=1, source_target_pairs={{0,2},{1,3},{2,0},{3,1},{4,6},{5,7},{6,4},{7,5},{8,10},{9,11},{10,... | collective-permute-start | bytes 786440 | tf_op jit(solution)/shard_map/ppermute | solution.py:200
  31.8 8.6 %collective-permute-start.3 = (f32[8,64,128]{2,1,0:T(8,128)S(1)}, f32[8,64,128]{2,1,0:T(8,128)S(1)}, u32[]{:S(2)}, u32[]{:S(2)}) collective-permute-start(f32[8,64,128]{2,1,0:T(8,128)S(1)} %triples.5), channel_id=1, source_target_pairs={{0,14},{1,15},{2,4},{3,5},{4,2},{5,3},{6,8},{7,9},{8,6},{9,7},{10,... | collective-permute-start | bytes 786440 | tf_op jit(solution)/shard_map/ppermute | solution.py:200
  41.8 13.3 %all-to-all-start = ((f32[4,4,64,128]{3,2,1,0:T(8,128)}), f32[4,4,64,128]{3,2,1,0:T(8,128)S(1)}, u32[]{:S(2)}, u32[]{:S(2)}) async-start(f32[4,4,64,128]{3,2,1,0:T(8,128)} %bitcast.4), calls=%async_computation | async-start | bytes 1048576 | tf_op jit(solution)/shard_map/all_to_all | solution.py:208
  55.8 36.2 %all-to-all-start.1 = ((f32[16,16,128]{2,1,0:T(8,128)}), f32[16,16,128]{2,1,0:T(8,128)S(1)}, u32[]{:S(2)}, u32[]{:S(2)}) async-start(f32[16,16,128]{2,1,0:T(8,128)} %get-tuple-element.7), calls=%async_computation.1 | async-start | bytes 262144 | tf_op jit(solution)/shard_map/all_to_all | solution.py:212
  66.7 23.9 %collective-permute-start.4 = (f32[2,64,128]{2,1,0:T(8,128)S(1)}, f32[2,64,128]{2,1,0:T(8,128)S(1)}, u32[]{:S(2)}, u32[]{:S(2)}) collective-permute-start(f32[2,64,128]{2,1,0:T(8,128)S(1)} %get-tuple-element.5), channel_id=1, source_target_pairs={{0,1008},{16,0},{32,16},{48,32},{64,48},{80,64},{96,80},{112,96},{... | collective-permute-start | bytes 196616 | tf_op jit(solution)/shard_map/ppermute | solution.py:16
  81.1 10.9 %collective-permute-start.5 = (f32[2,64,128]{2,1,0:T(8,128)S(1)}, f32[2,64,128]{2,1,0:T(8,128)S(1)}, u32[]{:S(2)}, u32[]{:S(2)}) collective-permute-start(f32[2,64,128]{2,1,0:T(8,128)S(1)} %get-tuple-element.6), channel_id=1, source_target_pairs={{0,1009},{1,1008},{2,1011},{3,1010},{4,1013},{5,1012},{6,1015},{7,... | collective-permute-start | bytes 196616 | tf_op jit(solution)/shard_map/ppermute | solution.py:213

commit v5 on v4

--- a/solution.py
+++ b/solution.py
@@ -1,3 +1,4 @@
+import functools
 import math
 
 import jax
@@ -25,20 +26,26 @@
     return [pl.BlockSpec(memory_space=pltpu.VMEM)] * count
 
 
-def fetch_kernel(in_ref, out_ref):
+def fetch_kernel(parity_ref, in_ref, out_ref, early_ref, late_ref, *, run):
     out_ref[...] = in_ref[...]
-
-
-def fetched(x):
-    return pl.pallas_call(
-        fetch_kernel,
+    for m in range(early_ref.shape[0] // run):
+        at = pl.ds(m * run, run)
+        early_ref[at, :] = in_ref[pl.ds(pl.multiple_of(2 * m * run + (1 - parity_ref[0]) * run, run), run), :]
+        late_ref[at, :] = in_ref[pl.ds(pl.multiple_of(2 * m * run + parity_ref[0] * run, run), run), :]
+
+
+def fetched(parity, x, run):
+    rows, fields = x.shape
+    half = jax.ShapeDtypeStruct((rows // 2, fields), x.dtype)
+    return pl.pallas_call(
+        functools.partial(fetch_kernel, run=run),
         name="fetch",
-        out_shape=jax.ShapeDtypeStruct(x.shape, x.dtype),
-        in_specs=in_vmem(1),
-        out_specs=pl.BlockSpec(memory_space=pltpu.VMEM),
+        out_shape=(jax.ShapeDtypeStruct(x.shape, x.dtype), half, half),
+        in_specs=[pl.BlockSpec(memory_space=pltpu.SMEM)] + in_vmem(1),
+        out_specs=tuple(in_vmem(3)),
         compiler_params=pltpu.CompilerParams(vmem_limit_bytes=4 * 2**20),
-        cost_estimate=pl.CostEstimate(flops=0, bytes_accessed=2 * x.size * 4, transcendentals=0),
-    )(x)
+        cost_estimate=pl.CostEstimate(flops=0, bytes_accessed=3 * x.size * 4, transcendentals=0),
+    )(parity.reshape(1), x)
 
 
 def weights_kernel(c_ref, w_ref):
@@ -58,10 +65,10 @@
     )(c)
 
 
-def triple_kernel(scale, run, stride, start_ref, a_ref, b_ref, w_ref, out_ref):
+def triple_kernel(scale, start, run, stride, a_ref, b_ref, w_ref, out_ref):
     rows = b_ref.shape[0]
     first_half = lax.broadcasted_iota(jnp.int32, (rows, 2 * rows), 1) < rows
-    start = start_ref[0] + pl.program_id(0) * (GROUP // run * stride)
+    start = start + pl.program_id(0) * (GROUP // run * stride)
     highs, lows = [], []
     for u in range(GROUP):
         high, low = two_halves(a_ref[pl.ds(start + u // run * stride + u % run, 1), :] * b_ref[...])
@@ -77,14 +84,14 @@
         out_ref[u] = jnp.where(first_half, even, odd)
 
 
-def triples(start, a, b, w, scale, steps, run, stride):
+def triples(a, b, w, scale, steps, start, run, stride):
     rows, fields = b.shape
     return pl.pallas_call(
-        lambda *refs: triple_kernel(scale, run, stride, *refs),
+        lambda *refs: triple_kernel(scale, start, run, stride, *refs),
         name="triples",
         grid=(steps,),
         out_shape=jax.ShapeDtypeStruct((steps * GROUP // 2, rows, 2 * rows), jnp.float32),
-        in_specs=[pl.BlockSpec(memory_space=pltpu.SMEM)] + in_vmem(3),
+        in_specs=in_vmem(3),
         out_specs=pl.BlockSpec((GROUP // 2, rows, 2 * rows), lambda s: (s, 0, 0)),
         compiler_params=pltpu.CompilerParams(vmem_limit_bytes=40 * 2**20),
         cost_estimate=pl.CostEstimate(
@@ -92,28 +99,28 @@
             bytes_accessed=4 * (steps * GROUP * rows**2 + 3 * rows * fields),
             transcendentals=0,
         ),
-    )(start.reshape(1), a, b, w)
-
-
-def merge_kernel(mine_ref, low_ref, high_ref, out_ref):
-    pairs = low_ref.shape[0]
-    out_ref[:pairs] = mine_ref[:pairs] + low_ref[...]
-    out_ref[pairs:] = mine_ref[pairs:] + high_ref[...]
-
-
-def merge(mine, low, high, owners):
-    pairs, rows, lanes = mine.shape[0] // owners, *mine.shape[1:]
-    whole = pl.BlockSpec((pairs, rows, lanes), lambda m: (m, 0, 0))
-    part = pl.BlockSpec((pairs // 2, rows, lanes), lambda m: (m, 0, 0))
+    )(a, b, w)
+
+
+def merge_kernel(mine_ref, theirs_ref, *refs):
+    refs[-1][...] = mine_ref[...] + theirs_ref[...]
+
+
+def merge(mine, theirs, part, held=None):
+    owners, _, pairs, rows, lanes = mine.shape
+    block = pl.BlockSpec((owners, 1, pairs, rows, lanes), lambda step: (0, part, 0, 0, 0))
+    whole = pl.BlockSpec((owners, 1, pairs, rows, lanes), lambda step: (0, 0, 0, 0, 0))
+    more = () if held is None else (held,)
     return pl.pallas_call(
         merge_kernel,
         name="merge",
-        grid=(owners,),
+        grid=(1,),
         out_shape=jax.ShapeDtypeStruct(mine.shape, jnp.float32),
-        in_specs=[whole, part, part],
-        out_specs=whole,
+        in_specs=[block, whole] + [pl.BlockSpec(memory_space=pl.ANY)] * len(more),
+        out_specs=block,
+        input_output_aliases={2: 0} if more else {},
         compiler_params=pltpu.CompilerParams(vmem_limit_bytes=8 * 2**20),
-    )(mine, low, high)
+    )(mine, theirs.reshape(owners, 1, pairs, rows, lanes), *more)
 
 
 def regroup_kernel(half_ref, arrived_ref, send_ref, own_ref, other_ref, sum_ref):
@@ -184,25 +191,24 @@
     blocks, parts = lax.axis_size("vec"), lax.axis_size("field")
     rows = vectors.shape[0]
     scale = 1.0 / math.sqrt(vectors.shape[1] * parts)
-    previous = passed_along(vectors, "vec", 1)
-    following = passed_along(vectors, "vec", -1)
-    here = fetched(vectors)
     peers = parts // 2
     run = rows // peers
-    parity = lax.axis_index("field") // 2 % 2
+    following = passed_along(vectors, "vec", -1)
+    here, early, late = fetched(lax.axis_index("field") // 2 % 2, vectors, run)
+    early = passed_along(early, "vec", 1)
+    late = passed_along(late, "vec", 1)
     w = weights(following)
 
     def sent(part, towards):
-        sums = triples(
-            (1 - parity) * run + part * (run // 2), previous, here, w, scale, rows // 4 // GROUP, run // 2, 2 * run
-        )
+        sums = triples(early, here, w, scale, rows // 4 // GROUP, part * (run // 2), run // 2, run)
         moves = [(2 * z + half, 2 * (towards(z) % peers) + half) for z in range(peers) for half in range(2)]
         return lax.ppermute(sums, "field", moves)
 
     low = sent(0, lambda z: z ^ 1)
     high = sent(1, lambda z: z + 1 if z % 2 else z - 1)
-    mine = triples(parity * run, previous, here, w, scale, rows // 2 // GROUP, run, 2 * run)
-    merged = merge(mine, low, high, peers // 2)
+    mine = triples(late, here, w, scale, rows // 2 // GROUP, 0, run, run)
+    mine = mine.reshape(peers // 2, 2, run // 4, rows, 2 * rows)
+    merged = merge(mine, high, 1, merge(mine, low, 0))
     along_z = [[2 * z + half for z in range(q, peers, 2)] for q in range(2) for half in range(2)]
     pieces = merged.reshape(peers // 2, run // 2, rows, 2 * rows)
     arrived = lax.all_to_all(pieces, "field", 0, 0, axis_index_groups=along_z, tiled=True)

time: 93.2 us -> 91 us (0.976)
  waiting for transfers between devices: 17 us -> 14.1 us
    all_to_all x1, starting transfers between devices: 11 us -> 6.77 us  [per_device(): lax.all_to_all(send, 'field', split_axis=0, concat_axis=0, tiled=True)]
    ppermute x3 -> x4, waiting for transfers between devices: 6.24 us -> 2.11 us  [passed_along(): return lax.ppermute(x, axis, [(i, (i + by) % peers) for i in range(peers)])]
    ppermute x3 -> x4, starting transfers between devices: 32.3 us -> 35.2 us  [passed_along(): return lax.ppermute(x, axis, [(i, (i + by) % peers) for i in range(peers)])]
    ppermute x2, starting transfers between devices: 6.73 us -> 9.55 us  [sent(): return lax.ppermute(sums, 'field', moves)]
    all_to_all x1, waiting for transfers between devices: 9.49 us -> 10.7 us  [per_device(): lax.all_to_all(pieces, 'field', 0, 0, axis_index_groups=along_z, tiled=True)]
    pallas_call x5 -> x6, Pallas kernels: 8.94 us -> 9.02 us  [the longest x3 7.5 us: triples(): pl.pallas_call(lambda *refs: triple_kernel(scale, start, run, stride, *re...]
  transfers between devices with their start and end apart: 8 -> 9, of which waited for: 3 -> 3; matrix products, arithmetic and copies ran while one was open for 0% -> 0% of each run, Pallas kernels for 6% -> 9%
where the time goes in v5:
time: 91 us; the launch traced here: 90.5 us
  starting transfers between devices  64 us (70%)
  waiting for transfers between devices  14.1 us (15%)
  Pallas kernels  10.6 us (12%)
  local copies, waits for them, and re-layouts  0.99 us (1%)
    ppermute x4, starting transfers between devices, passed_along(): return lax.ppermute(x, axis, [(i, (i + by) % peers) for i in range(peers)])  35.2 us
    all_to_all x1, waiting for transfers between devices, per_device(): lax.all_to_all(pieces, 'field', 0, 0, axis_index_groups=along_z, tiled=True)  10.7 us
    ppermute x2, starting transfers between devices, sent(): return lax.ppermute(sums, 'field', moves)  9.55 us
    ppermute x1, starting transfers between devices, per_device(): other = lax.ppermute(other, ('vec', 'field'), crossed)  8.97 us
    pallas_call x3, Pallas kernels, triples(): pl.pallas_call(lambda *refs: triple_kernel(scale, start, run, stride, *re...  7.5 us
    all_to_all x1, starting transfers between devices, per_device(): lax.all_to_all(send, 'field', split_axis=0, concat_axis=0, tiled=True)  6.77 us
    all_to_all x1, starting transfers between devices, per_device(): lax.all_to_all(pieces, 'field', 0, 0, axis_index_groups=along_z, tiled=True)  3.47 us
    ppermute x4, waiting for transfers between devices, passed_along(): return lax.ppermute(x, axis, [(i, (i + by) % peers) for i in range(peers)])  2.11 us
  transfers between devices with their start and end apart: 9, of which 3 were waited for; matrix products, arithmetic and copies ran while one was open for 0% of the time, Pallas kernels for 9%

profile of v5, /device:TPU:1, one launch (start us, length us, event | category | flops | bytes accessed | tf_op | source)
XLA Modules:
  0.0 90.5 jit_solution(18232026590336306694)
XLA Ops:
  0.6 16.0 %collective-permute-start.1 = (f32[64,1536]{1,0:T(8,128)}, f32[64,1536]{1,0:T(8,128)S(1)}, u32[]{:S(2)}, u32[]{:S(2)}) collective-permute-start(f32[64,1536]{1,0:T(8,128)} %in_ref.1), channel_id=1, source_target_pairs={{0,1008},{16,0},{32,16},{48,32},{64,48},{80,64},{96,80},{112,96},{... | collective-permute-start | bytes 1179656 | tf_op jit(solution)/shard_map/ppermute | solution.py:17
  16.7 0.0 copy-start
  16.7 1.0 %copy-done = f32[64,1536]{1,0:T(8,128)S(1)} copy-done((f32[64,1536]{1,0:T(8,128)S(1)}, f32[64,1536]{1,0:T(8,128)}, u32[]{:S(2)}) %copy-start) | copy-done | bytes 393240
  17.7 0.1 fetch.1
  17.7 1.9 %collective-permute-start.2 = (f32[32,1536]{1,0:T(8,128)S(1)}, f32[32,1536]{1,0:T(8,128)S(1)}, u32[]{:S(2)}, u32[]{:S(2)}) collective-permute-start(f32[32,1536]{1,0:T(8,128)S(1)} %get-tuple-element.10), channel_id=1, source_target_pairs={{0,16},{16,32},{32,48},{48,64},{64,80},{80,96},{96,112},{112,128},... | collective-permute-start | bytes 589832 | tf_op jit(solution)/shard_map/ppermute | solution.py:17
  19.7 1.9 %collective-permute-start = (f32[32,1536]{1,0:T(8,128)S(1)}, f32[32,1536]{1,0:T(8,128)S(1)}, u32[]{:S(2)}, u32[]{:S(2)}) collective-permute-start(f32[32,1536]{1,0:T(8,128)S(1)} %get-tuple-element.8), channel_id=1, source_target_pairs={{0,16},{16,32},{32,48},{48,64},{64,80},{80,96},{96,112},{112,128},... | collective-permute-start | bytes 589832 | tf_op jit(solution)/shard_map/ppermute | solution.py:17
  21.6 0.0 collective-permute-done.1.c_ref
  21.6 0.2 weights.1.refs_2_
  21.8 2.1 %collective-permute-done.2.refs_0_ = f32[32,1536]{1,0:T(8,128)S(1)} collective-permute-done((f32[32,1536]{1,0:T(8,128)S(1)}, f32[32,1536]{1,0:T(8,128)S(1)}, u32[]{:S(2)}, u32[]{:S(2)}) %collective-permute-start.2) | collective-permute-done | bytes 196640 | tf_op jit(solution)/shard_map/ppermute | solution.py:17
  23.9 1.9 %triples.5 = f32[8,64,128]{2,1,0:T(8,128)S(1)} custom-call(f32[32,1536]{1,0:T(8,128)S(1)} %collective-permute-done.2.refs_0_, f32[64,1536]{1,0:T(8,128)S(1)} %get-tuple-element.9.refs_1_, bf16[1536,128]{1,0:T(8,128)(2,1)S(1)} %weights.1.refs_2_), custom_call_target="tpu_custom_call" | custom-call | flops 805306368 | bytes 1441792 | tf_op jit(solution)/shard_map/triples/pallas_call | solution.py:89
  25.7 1.9 %collective-permute-start.4 = (f32[8,64,128]{2,1,0:T(8,128)S(1)}, f32[8,64,128]{2,1,0:T(8,128)S(1)}, u32[]{:S(2)}, u32[]{:S(2)}) collective-permute-start(f32[8,64,128]{2,1,0:T(8,128)S(1)} %triples.5), channel_id=1, source_target_pairs={{0,2},{1,3},{2,0},{3,1},{4,6},{5,7},{6,4},{7,5},{8,10},{9,11},{10,... | collective-permute-start | bytes 786440 | tf_op jit(solution)/shard_map/ppermute | solution.py:205
  27.7 1.9 %triples.4 = f32[8,64,128]{2,1,0:T(8,128)S(1)} custom-call(f32[32,1536]{1,0:T(8,128)S(1)} %collective-permute-done.2.refs_0_, f32[64,1536]{1,0:T(8,128)S(1)} %get-tuple-element.9.refs_1_, bf16[1536,128]{1,0:T(8,128)(2,1)S(1)} %weights.1.refs_2_), custom_call_target="tpu_custom_call" | custom-call | flops 805306368 | bytes 1441792 | tf_op jit(solution)/shard_map/triples/pallas_call | solution.py:89
  29.5 7.6 %collective-permute-start.3 = (f32[8,64,128]{2,1,0:T(8,128)S(1)}, f32[8,64,128]{2,1,0:T(8,128)S(1)}, u32[]{:S(2)}, u32[]{:S(2)}) collective-permute-start(f32[8,64,128]{2,1,0:T(8,128)S(1)} %triples.4), channel_id=1, source_target_pairs={{0,14},{1,15},{2,4},{3,5},{4,2},{5,3},{6,8},{7,9},{8,6},{9,7},{10,... | collective-permute-start | bytes 786440 | tf_op jit(solution)/shard_map/ppermute | solution.py:205
  37.2 0.0 collective-permute-done.refs_0_
  37.2 3.8 %triples.3 = f32[16,64,128]{2,1,0:T(8,128)S(1)} custom-call(f32[32,1536]{1,0:T(8,128)S(1)} %collective-permute-done.refs_0_, f32[64,1536]{1,0:T(8,128)S(1)} %get-tuple-element.9.refs_1_, bf16[1536,128]{1,0:T(8,128)(2,1)S(1)} %weights.1.refs_2_), custom_call_target="tpu_custom_call" | custom-call | flops 1610612736 | bytes 1703936 | tf_op jit(solution)/shard_map/triples/pallas_call | solution.py:89
  41.0 0.0 collective-permute-done.4
  41.0 0.7 merge.2.refs_0_
  41.7 0.0 collective-permute-done.3
  41.7 0.7 merge.3
  42.4 3.5 %all-to-all-start = ((f32[4,4,64,128]{3,2,1,0:T(8,128)}), f32[4,4,64,128]{3,2,1,0:T(8,128)S(1)}, u32[]{:S(2)}, u32[]{:S(2)}) async-start(f32[4,4,64,128]{3,2,1,0:T(8,128)} %bitcast.5), calls=%async_computation | async-start | bytes 1048576 | tf_op jit(solution)/shard_map/all_to_all | solution.py:214
  45.9 10.7 %all-to-all-done.arrived_ref = f32[4,4,64,128]{3,2,1,0:T(8,128)S(1)} async-done(((f32[4,4,64,128]{3,2,1,0:T(8,128)}), f32[4,4,64,128]{3,2,1,0:T(8,128)S(1)}, u32[]{:S(2)}, u32[]{:S(2)}) %all-to-all-start) | async-done | bytes 524320 | tf_op jit(solution)/shard_map/all_to_all | solution.py:214
  56.6 0.7 regroup.1
  57.3 6.8 %all-to-all-start.1 = ((f32[16,16,128]{2,1,0:T(8,128)}), f32[16,16,128]{2,1,0:T(8,128)S(1)}, u32[]{:S(2)}, u32[]{:S(2)}) async-start(f32[16,16,128]{2,1,0:T(8,128)} %get-tuple-element.13), calls=%async_computation.1 | async-start | bytes 262144 | tf_op jit(solution)/shard_map/all_to_all | solution.py:218
  64.1 15.3 %collective-permute-start.5 = (f32[2,64,128]{2,1,0:T(8,128)S(1)}, f32[2,64,128]{2,1,0:T(8,128)S(1)}, u32[]{:S(2)}, u32[]{:S(2)}) collective-permute-start(f32[2,64,128]{2,1,0:T(8,128)S(1)} %get-tuple-element.11), channel_id=1, source_target_pairs={{0,1008},{16,0},{32,16},{48,32},{64,48},{80,64},{96,80},{112,96},{... | collective-permute-start | bytes 196616 | tf_op jit(solution)/shard_map/ppermute | solution.py:17
  79.5 9.0 %collective-permute-start.6 = (f32[2,64,128]{2,1,0:T(8,128)S(1)}, f32[2,64,128]{2,1,0:T(8,128)S(1)}, u32[]{:S(2)}, u32[]{:S(2)}) collective-permute-start(f32[2,64,128]{2,1,0:T(8,128)S(1)} %get-tuple-element.12), channel_id=1, source_target_pairs={{0,1009},{1,1008},{2,1011},{3,1010},{4,1013},{5,1012},{6,1015},{7,... | collective-permute-start | bytes 196616 | tf_op jit(solution)/shard_map/ppermute | solution.py:219
  88.4 0.0 collective-permute-done.5.own_ref
  88.5 1.3 %collective-permute-done.6.other_ref = f32[2,64,128]{2,1,0:T(8,128)S(1)} collective-permute-done((f32[2,64,128]{2,1,0:T(8,128)S(1)}, f32[2,64,128]{2,1,0:T(8,128)S(1)}, u32[]{:S(2)}, u32[]{:S(2)}) %collective-permute-start.6) | collective-permute-done | bytes 65568 | tf_op jit(solution)/shard_map/ppermute | solution.py:219
  89.8 0.0 all-to-all-done.1.turned_ref
  89.8 0.8 finish.1
Async XLA Ops:
  0.6 21.0 %collective-permute-start.1 = (f32[64,1536]{1,0:T(8,128)}, f32[64,1536]{1,0:T(8,128)S(1)}, u32[]{:S(2)}, u32[]{:S(2)}) collective-permute-start(f32[64,1536]{1,0:T(8,128)} %in_ref.1), channel_id=1, source_target_pairs={{0,1008},{16,0},{32,16},{48,32},{64,48},{80,64},{96,80},{112,96},{... | collective-permute-start | bytes 1179656 | tf_op jit(solution)/shard_map/ppermute | solution.py:17
  16.7 1.0 %copy-start = (f32[64,1536]{1,0:T(8,128)S(1)}, f32[64,1536]{1,0:T(8,128)}, u32[]{:S(2)}) copy-start(f32[64,1536]{1,0:T(8,128)} %in_ref.1) | copy-start | bytes 1179652
  17.7 6.1 %collective-permute-start.2 = (f32[32,1536]{1,0:T(8,128)S(1)}, f32[32,1536]{1,0:T(8,128)S(1)}, u32[]{:S(2)}, u32[]{:S(2)}) collective-permute-start(f32[32,1536]{1,0:T(8,128)S(1)} %get-tuple-element.10), channel_id=1, source_target_pairs={{0,16},{16,32},{32,48},{48,64},{64,80},{80,96},{96,112},{112,128},... | collective-permute-start | bytes 589832 | tf_op jit(solution)/shard_map/ppermute | solution.py:17
  19.7 17.5 %collective-permute-start = (f32[32,1536]{1,0:T(8,128)S(1)}, f32[32,1536]{1,0:T(8,128)S(1)}, u32[]{:S(2)}, u32[]{:S(2)}) collective-permute-start(f32[32,1536]{1,0:T(8,128)S(1)} %get-tuple-element.8), channel_id=1, source_target_pairs={{0,16},{16,32},{32,48},{48,64},{64,80},{80,96},{96,112},{112,128},... | collective-permute-start | bytes 589832 | tf_op jit(solution)/shard_map/ppermute | solution.py:17
  25.7 15.2 %collective-permute-start.4 = (f32[8,64,128]{2,1,0:T(8,128)S(1)}, f32[8,64,128]{2,1,0:T(8,128)S(1)}, u32[]{:S(2)}, u32[]{:S(2)}) collective-permute-start(f32[8,64,128]{2,1,0:T(8,128)S(1)} %triples.5), channel_id=1, source_target_pairs={{0,2},{1,3},{2,0},{3,1},{4,6},{5,7},{6,4},{7,5},{8,10},{9,11},{10,... | collective-permute-start | bytes 786440 | tf_op jit(solution)/shard_map/ppermute | solution.py:205
  29.5 12.2 %collective-permute-start.3 = (f32[8,64,128]{2,1,0:T(8,128)S(1)}, f32[8,64,128]{2,1,0:T(8,128)S(1)}, u32[]{:S(2)}, u32[]{:S(2)}) collective-permute-start(f32[8,64,128]{2,1,0:T(8,128)S(1)} %triples.4), channel_id=1, source_target_pairs={{0,14},{1,15},{2,4},{3,5},{4,2},{5,3},{6,8},{7,9},{8,6},{9,7},{10,... | collective-permute-start | bytes 786440 | tf_op jit(solution)/shard_map/ppermute | solution.py:205
  42.4 14.2 %all-to-all-start = ((f32[4,4,64,128]{3,2,1,0:T(8,128)}), f32[4,4,64,128]{3,2,1,0:T(8,128)S(1)}, u32[]{:S(2)}, u32[]{:S(2)}) async-start(f32[4,4,64,128]{3,2,1,0:T(8,128)} %bitcast.5), calls=%async_computation | async-start | bytes 1048576 | tf_op jit(solution)/shard_map/all_to_all | solution.py:214
  57.3 32.4 %all-to-all-start.1 = ((f32[16,16,128]{2,1,0:T(8,128)}), f32[16,16,128]{2,1,0:T(8,128)S(1)}, u32[]{:S(2)}, u32[]{:S(2)}) async-start(f32[16,16,128]{2,1,0:T(8,128)} %get-tuple-element.13), calls=%async_computation.1 | async-start | bytes 262144 | tf_op jit(solution)/shard_map/all_to_all | solution.py:218
  64.1 24.3 %collective-permute-start.5 = (f32[2,64,128]{2,1,0:T(8,128)S(1)}, f32[2,64,128]{2,1,0:T(8,128)S(1)}, u32[]{:S(2)}, u32[]{:S(2)}) collective-permute-start(f32[2,64,128]{2,1,0:T(8,128)S(1)} %get-tuple-element.11), channel_id=1, source_target_pairs={{0,1008},{16,0},{32,16},{48,32},{64,48},{80,64},{96,80},{112,96},{... | collective-permute-start | bytes 196616 | tf_op jit(solution)/shard_map/ppermute | solution.py:17
  79.5 10.3 %collective-permute-start.6 = (f32[2,64,128]{2,1,0:T(8,128)S(1)}, f32[2,64,128]{2,1,0:T(8,128)S(1)}, u32[]{:S(2)}, u32[]{:S(2)}) collective-permute-start(f32[2,64,128]{2,1,0:T(8,128)S(1)} %get-tuple-element.12), channel_id=1, source_target_pairs={{0,1009},{1,1008},{2,1011},{3,1010},{4,1013},{5,1012},{6,1015},{7,... | collective-permute-start | bytes 196616 | tf_op jit(solution)/shard_map/ppermute | solution.py:219

commit v6 on v5

--- a/solution.py
+++ b/solution.py
@@ -10,6 +10,7 @@
 
 
 GROUP = 16
+LINE = 8
 
 
 def passed_along(x, axis, by):
@@ -26,43 +27,47 @@
     return [pl.BlockSpec(memory_space=pltpu.VMEM)] * count
 
 
-def fetch_kernel(parity_ref, in_ref, out_ref, early_ref, late_ref, *, run):
+def fetch_kernel(in_ref, out_ref):
     out_ref[...] = in_ref[...]
-    for m in range(early_ref.shape[0] // run):
-        at = pl.ds(m * run, run)
-        early_ref[at, :] = in_ref[pl.ds(pl.multiple_of(2 * m * run + (1 - parity_ref[0]) * run, run), run), :]
-        late_ref[at, :] = in_ref[pl.ds(pl.multiple_of(2 * m * run + parity_ref[0] * run, run), run), :]
-
-
-def fetched(parity, x, run):
-    rows, fields = x.shape
-    half = jax.ShapeDtypeStruct((rows // 2, fields), x.dtype)
-    return pl.pallas_call(
-        functools.partial(fetch_kernel, run=run),
+
+
+def fetched(x):
+    return pl.pallas_call(
+        fetch_kernel,
         name="fetch",
-        out_shape=(jax.ShapeDtypeStruct(x.shape, x.dtype), half, half),
-        in_specs=[pl.BlockSpec(memory_space=pltpu.SMEM)] + in_vmem(1),
-        out_specs=tuple(in_vmem(3)),
-        compiler_params=pltpu.CompilerParams(vmem_limit_bytes=4 * 2**20),
-        cost_estimate=pl.CostEstimate(flops=0, bytes_accessed=3 * x.size * 4, transcendentals=0),
-    )(parity.reshape(1), x)
-
-
-def weights_kernel(c_ref, w_ref):
-    w_ref[...] = jnp.concatenate(two_halves(c_ref[...]), 0).T
-
-
-def weights(c):
-    rows, fields = c.shape
-    return pl.pallas_call(
-        weights_kernel,
-        name="weights",
-        out_shape=jax.ShapeDtypeStruct((fields, 2 * rows), jnp.bfloat16),
+        out_shape=jax.ShapeDtypeStruct(x.shape, x.dtype),
         in_specs=in_vmem(1),
         out_specs=pl.BlockSpec(memory_space=pltpu.VMEM),
+        compiler_params=pltpu.CompilerParams(vmem_limit_bytes=4 * 2**20),
+        cost_estimate=pl.CostEstimate(flops=0, bytes_accessed=2 * x.size * 4, transcendentals=0),
+    )(x)
+
+
+def inputs_kernel(parity_ref, first_ref, last_ref, previous_ref, following_ref, turned_ref, a_ref, w_ref, *, run):
+    parity, first, last = parity_ref[0], first_ref[0] == 1, last_ref[0] == 1
+    half = a_ref.shape[0] // 2
+    for m in range(half // run):
+        for at, which in ((m * run, 1 - parity), (half + m * run, parity)):
+            rows = pl.ds(pl.multiple_of((2 * m + which) * run, run), run)
+            a_ref[at : at + run, :] = jnp.where(first, turned_ref[rows, :], previous_ref[rows, :])
+    c = jnp.where(last, turned_ref[...], following_ref[...])
+    w_ref[...] = jnp.concatenate(two_halves(c), 0).T
+
+
+def inputs(place, previous, following, turned, run):
+    rows, fields = previous.shape
+    return pl.pallas_call(
+        functools.partial(inputs_kernel, run=run),
+        name="inputs",
+        out_shape=(
+            jax.ShapeDtypeStruct(previous.shape, jnp.float32),
+            jax.ShapeDtypeStruct((fields, 2 * rows), jnp.bfloat16),
+        ),
+        in_specs=[pl.BlockSpec(memory_space=pltpu.SMEM)] * 3 + in_vmem(3),
+        out_specs=tuple(in_vmem(2)),
         compiler_params=pltpu.CompilerParams(vmem_limit_bytes=8 * 2**20),
-        cost_estimate=pl.CostEstimate(flops=c.size, bytes_accessed=8 * c.size, transcendentals=0),
-    )(c)
+        cost_estimate=pl.CostEstimate(flops=previous.size, bytes_accessed=20 * previous.size, transcendentals=0),
+    )(*place, previous, following, turned)
 
 
 def triple_kernel(scale, start, run, stride, a_ref, b_ref, w_ref, out_ref):
@@ -193,20 +198,26 @@
     scale = 1.0 / math.sqrt(vectors.shape[1] * parts)
     peers = parts // 2
     run = rows // peers
-    following = passed_along(vectors, "vec", -1)
-    here, early, late = fetched(lax.axis_index("field") // 2 % 2, vectors, run)
-    early = passed_along(early, "vec", 1)
-    late = passed_along(late, "vec", 1)
-    w = weights(following)
+    line = LINE if blocks % LINE == 0 else blocks
+    ends = [((b - 1) % blocks, b) for b in range(0, blocks, line)]
+    inner = [(b - 1, b) for b in range(blocks) if b % line]
+    turned = lax.ppermute(vectors, "vec", ends + [(b, a) for a, b in ends])
+    here = fetched(vectors)
+    following = lax.ppermute(vectors, "vec", [(b, a) for a, b in inner])
+    previous = lax.ppermute(vectors, "vec", inner)
+    spot = lax.rem(lax.axis_index("vec"), line)
+    parity = lax.axis_index("field") // 2 & 1
+    place = [x.astype(jnp.int32).reshape(1) for x in (parity, spot == 0, spot == line - 1)]
+    a, w = inputs(place, previous, following, turned, run)
 
     def sent(part, towards):
-        sums = triples(early, here, w, scale, rows // 4 // GROUP, part * (run // 2), run // 2, run)
+        sums = triples(a, here, w, scale, rows // 4 // GROUP, part * (run // 2), run // 2, run)
         moves = [(2 * z + half, 2 * (towards(z) % peers) + half) for z in range(peers) for half in range(2)]
         return lax.ppermute(sums, "field", moves)
 
     low = sent(0, lambda z: z ^ 1)
     high = sent(1, lambda z: z + 1 if z % 2 else z - 1)
-    mine = triples(late, here, w, scale, rows // 2 // GROUP, 0, run, run)
+    mine = triples(a, here, w, scale, rows // 2 // GROUP, rows // 2, run, run)
     mine = mine.reshape(peers // 2, 2, run // 4, rows, 2 * rows)
     merged = merge(mine, high, 1, merge(mine, low, 0))
     along_z = [[2 * z + half for z in range(q, peers, 2)] for q in range(2) for half in range(2)]

time: 91 us -> 94.2 us (1.035)
  starting transfers between devices: 64 us -> 68.3 us
  waiting for transfers between devices: 14.1 us -> 13.1 us
    ppermute x4 -> x1, starting transfers between devices: 35.2 us -> 16.4 us  [passed_along(): return lax.ppermute(x, axis, [(i, (i + by) % peers) for i in range(peers)])]
    ppermute x0 -> x3, starting transfers between devices: none -> 18 us  [the longest x1 12.8 us: per_device(): following = lax.ppermute(vectors, 'vec', [(b, a) for a, b in inner])]
    ppermute x2, starting transfers between devices: 9.55 us -> 15.8 us  [sent(): return lax.ppermute(sums, 'field', moves)]
    ppermute x4 -> x1, waiting for transfers between devices: 2.11 us -> 0.01 us  [passed_along(): return lax.ppermute(x, axis, [(i, (i + by) % peers) for i in range(peers)])]
    ppermute x1, starting transfers between devices: 8.97 us -> 7.8 us  [per_device(): other = lax.ppermute(other, ('vec', 'field'), crossed)]
    ppermute x1, waiting for transfers between devices: 1.3 us -> 2.36 us  [per_device(): other = lax.ppermute(other, ('vec', 'field'), crossed)]
  transfers between devices with their start and end apart: 9 -> 9, of which waited for: 3 -> 2; matrix products, arithmetic and copies ran while one was open for 0% -> 0% of each run, Pallas kernels for 9% -> 7%
where the time goes in v6:
time: 94.2 us; the launch traced here: 93.8 us
  starting transfers between devices  68.3 us (73%)
  waiting for transfers between devices  13.1 us (14%)
  Pallas kernels  10.6 us (11%)
  local copies, waits for them, and re-layouts  0.99 us (1%)
    ppermute x1, starting transfers between devices, passed_along(): return lax.ppermute(x, axis, [(i, (i + by) % peers) for i in range(peers)])  16.4 us
    ppermute x2, starting transfers between devices, sent(): return lax.ppermute(sums, 'field', moves)  15.8 us
    ppermute x1, starting transfers between devices, per_device(): following = lax.ppermute(vectors, 'vec', [(b, a) for a, b in inner])  12.8 us
    all_to_all x1, waiting for transfers between devices, per_device(): lax.all_to_all(pieces, 'field', 0, 0, axis_index_groups=along_z, tiled=True)  10.7 us
    ppermute x1, starting transfers between devices, per_device(): other = lax.ppermute(other, ('vec', 'field'), crossed)  7.8 us
    pallas_call x3, Pallas kernels, triples(): pl.pallas_call(lambda *refs: triple_kernel(scale, start, run, stride, *re...  7.52 us
    all_to_all x1, starting transfers between devices, per_device(): lax.all_to_all(send, 'field', split_axis=0, concat_axis=0, tiled=True)  6.71 us
    ppermute x1, starting transfers between devices, per_device(): previous = lax.ppermute(vectors, 'vec', inner)  4.5 us
  transfers between devices with their start and end apart: 9, of which 2 were waited for; matrix products, arithmetic and copies ran while one was open for 0% of the time, Pallas kernels for 7%

profile of v6, /device:TPU:1, one launch (start us, length us, event | category | flops | bytes accessed | tf_op | source)
XLA Modules:
  0.0 93.8 jit_solution(13642980991461775317)
XLA Ops:
  0.6 4.5 %collective-permute-start = (f32[64,1536]{1,0:T(8,128)}, f32[64,1536]{1,0:T(8,128)S(1)}, u32[]{:S(2)}, u32[]{:S(2)}) collective-permute-start(f32[64,1536]{1,0:T(8,128)} %in_ref.1), channel_id=1, source_target_pairs={{0,16},{16,32},{32,48},{48,64},{64,80},{80,96},{96,112},{128,144},... | collective-permute-start | bytes 1179656 | tf_op jit(solution)/shard_map/ppermute | solution.py:207
  5.1 12.8 %collective-permute-start.1 = (f32[64,1536]{1,0:T(8,128)}, f32[64,1536]{1,0:T(8,128)S(1)}, u32[]{:S(2)}, u32[]{:S(2)}) collective-permute-start(f32[64,1536]{1,0:T(8,128)} %in_ref.1), channel_id=1, source_target_pairs={{16,0},{32,16},{48,32},{64,48},{80,64},{96,80},{112,96},{144,128},... | collective-permute-start | bytes 1179656 | tf_op jit(solution)/shard_map/ppermute | solution.py:206
  18.0 0.7 collective-permute-start.2
  18.7 0.0 copy-start
  18.7 1.0 %copy-done = f32[64,1536]{1,0:T(8,128)S(1)} copy-done((f32[64,1536]{1,0:T(8,128)S(1)}, f32[64,1536]{1,0:T(8,128)}, u32[]{:S(2)}) %copy-start) | copy-done | bytes 393240
  19.7 0.0 collective-permute-done.previous_ref
  19.7 0.0 collective-permute-done.1.following_ref
  19.8 0.0 collective-permute-done.2.turned_ref
  19.8 0.2 inputs.1
  19.9 1.9 %triples.5 = f32[8,64,128]{2,1,0:T(8,128)S(1)} custom-call(f32[64,1536]{1,0:T(8,128)S(1)} %get-tuple-element.7.refs_0_, f32[64,1536]{1,0:T(8,128)S(1)} %fetch.1.refs_1_, bf16[1536,128]{1,0:T(8,128)(2,1)S(1)} %get-tuple-element.8.refs_2_), custom_call_target="tpu_custom_call" | custom-call | flops 805306368 | bytes 1441792 | tf_op jit(solution)/shard_map/triples/pallas_call | solution.py:94
  21.8 1.9 %collective-permute-start.4 = (f32[8,64,128]{2,1,0:T(8,128)S(1)}, f32[8,64,128]{2,1,0:T(8,128)S(1)}, u32[]{:S(2)}, u32[]{:S(2)}) collective-permute-start(f32[8,64,128]{2,1,0:T(8,128)S(1)} %triples.5), channel_id=1, source_target_pairs={{0,2},{1,3},{2,0},{3,1},{4,6},{5,7},{6,4},{7,5},{8,10},{9,11},{10,... | collective-permute-start | bytes 786440 | tf_op jit(solution)/shard_map/ppermute | solution.py:216
  23.7 1.9 %triples.4 = f32[8,64,128]{2,1,0:T(8,128)S(1)} custom-call(f32[64,1536]{1,0:T(8,128)S(1)} %get-tuple-element.7.refs_0_, f32[64,1536]{1,0:T(8,128)S(1)} %fetch.1.refs_1_, bf16[1536,128]{1,0:T(8,128)(2,1)S(1)} %get-tuple-element.8.refs_2_), custom_call_target="tpu_custom_call" | custom-call | flops 805306368 | bytes 1441792 | tf_op jit(solution)/shard_map/triples/pallas_call | solution.py:94
  25.6 13.9 %collective-permute-start.3 = (f32[8,64,128]{2,1,0:T(8,128)S(1)}, f32[8,64,128]{2,1,0:T(8,128)S(1)}, u32[]{:S(2)}, u32[]{:S(2)}) collective-permute-start(f32[8,64,128]{2,1,0:T(8,128)S(1)} %triples.4), channel_id=1, source_target_pairs={{0,14},{1,15},{2,4},{3,5},{4,2},{5,3},{6,8},{7,9},{8,6},{9,7},{10,... | collective-permute-start | bytes 786440 | tf_op jit(solution)/shard_map/ppermute | solution.py:216
  39.5 3.8 %triples.3 = f32[16,64,128]{2,1,0:T(8,128)S(1)} custom-call(f32[64,1536]{1,0:T(8,128)S(1)} %get-tuple-element.7.refs_0_, f32[64,1536]{1,0:T(8,128)S(1)} %fetch.1.refs_1_, bf16[1536,128]{1,0:T(8,128)(2,1)S(1)} %get-tuple-element.8.refs_2_), custom_call_target="tpu_custom_call" | custom-call | flops 1610612736 | bytes 1703936 | tf_op jit(solution)/shard_map/triples/pallas_call | solution.py:94
  43.3 0.0 collective-permute-done.4
  43.3 0.7 merge.2.refs_0_
  44.1 0.0 collective-permute-done.3
  44.1 0.7 merge.3
  44.8 3.5 %all-to-all-start = ((f32[4,4,64,128]{3,2,1,0:T(8,128)}), f32[4,4,64,128]{3,2,1,0:T(8,128)S(1)}, u32[]{:S(2)}, u32[]{:S(2)}) async-start(f32[4,4,64,128]{3,2,1,0:T(8,128)} %bitcast.7), calls=%async_computation | async-start | bytes 1048576 | tf_op jit(solution)/shard_map/all_to_all | solution.py:225
  48.3 10.7 %all-to-all-done.arrived_ref = f32[4,4,64,128]{3,2,1,0:T(8,128)S(1)} async-done(((f32[4,4,64,128]{3,2,1,0:T(8,128)}), f32[4,4,64,128]{3,2,1,0:T(8,128)S(1)}, u32[]{:S(2)}, u32[]{:S(2)}) %all-to-all-start) | async-done | bytes 524320 | tf_op jit(solution)/shard_map/all_to_all | solution.py:225
  59.0 0.7 regroup.1
  59.7 6.7 %all-to-all-start.1 = ((f32[16,16,128]{2,1,0:T(8,128)}), f32[16,16,128]{2,1,0:T(8,128)S(1)}, u32[]{:S(2)}, u32[]{:S(2)}) async-start(f32[16,16,128]{2,1,0:T(8,128)} %get-tuple-element.11), calls=%async_computation.1 | async-start | bytes 262144 | tf_op jit(solution)/shard_map/all_to_all | solution.py:229
  66.4 16.4 %collective-permute-start.5 = (f32[2,64,128]{2,1,0:T(8,128)S(1)}, f32[2,64,128]{2,1,0:T(8,128)S(1)}, u32[]{:S(2)}, u32[]{:S(2)}) collective-permute-start(f32[2,64,128]{2,1,0:T(8,128)S(1)} %get-tuple-element.9), channel_id=1, source_target_pairs={{0,1008},{16,0},{32,16},{48,32},{64,48},{80,64},{96,80},{112,96},{... | collective-permute-start | bytes 196616 | tf_op jit(solution)/shard_map/ppermute | solution.py:18
  82.8 7.8 %collective-permute-start.6 = (f32[2,64,128]{2,1,0:T(8,128)S(1)}, f32[2,64,128]{2,1,0:T(8,128)S(1)}, u32[]{:S(2)}, u32[]{:S(2)}) collective-permute-start(f32[2,64,128]{2,1,0:T(8,128)S(1)} %get-tuple-element.10), channel_id=1, source_target_pairs={{0,1009},{1,1008},{2,1011},{3,1010},{4,1013},{5,1012},{6,1015},{7,... | collective-permute-start | bytes 196616 | tf_op jit(solution)/shard_map/ppermute | solution.py:230
  90.6 0.0 collective-permute-done.5.own_ref
  90.7 2.4 %collective-permute-done.6.other_ref = f32[2,64,128]{2,1,0:T(8,128)S(1)} collective-permute-done((f32[2,64,128]{2,1,0:T(8,128)S(1)}, f32[2,64,128]{2,1,0:T(8,128)S(1)}, u32[]{:S(2)}, u32[]{:S(2)}) %collective-permute-start.6) | collective-permute-done | bytes 65568 | tf_op jit(solution)/shard_map/ppermute | solution.py:230
  93.0 0.0 all-to-all-done.1.turned_ref
  93.0 0.8 finish.1
  (1 shorter events, 0.0 us)
Async XLA Ops:
  0.6 19.1 %collective-permute-start = (f32[64,1536]{1,0:T(8,128)}, f32[64,1536]{1,0:T(8,128)S(1)}, u32[]{:S(2)}, u32[]{:S(2)}) collective-permute-start(f32[64,1536]{1,0:T(8,128)} %in_ref.1), channel_id=1, source_target_pairs={{0,16},{16,32},{32,48},{48,64},{64,80},{80,96},{96,112},{128,144},... | collective-permute-start | bytes 1179656 | tf_op jit(solution)/shard_map/ppermute | solution.py:207
  5.1 14.6 %collective-permute-start.1 = (f32[64,1536]{1,0:T(8,128)}, f32[64,1536]{1,0:T(8,128)S(1)}, u32[]{:S(2)}, u32[]{:S(2)}) collective-permute-start(f32[64,1536]{1,0:T(8,128)} %in_ref.1), channel_id=1, source_target_pairs={{16,0},{32,16},{48,32},{64,48},{80,64},{96,80},{112,96},{144,128},... | collective-permute-start | bytes 1179656 | tf_op jit(solution)/shard_map/ppermute | solution.py:206
  18.0 1.8 %collective-permute-start.2 = (f32[64,1536]{1,0:T(8,128)}, f32[64,1536]{1,0:T(8,128)S(1)}, u32[]{:S(2)}, u32[]{:S(2)}) collective-permute-start(f32[64,1536]{1,0:T(8,128)} %in_ref.1), channel_id=1, source_target_pairs={{1008,0},{112,128},{240,256},{368,384},{496,512},{624,640},{752,76... | collective-permute-start | bytes 1179656 | tf_op jit(solution)/shard_map/ppermute | solution.py:204
  18.7 1.0 %copy-start = (f32[64,1536]{1,0:T(8,128)S(1)}, f32[64,1536]{1,0:T(8,128)}, u32[]{:S(2)}) copy-start(f32[64,1536]{1,0:T(8,128)} %in_ref.1) | copy-start | bytes 1179652
  21.8 21.5 %collective-permute-start.4 = (f32[8,64,128]{2,1,0:T(8,128)S(1)}, f32[8,64,128]{2,1,0:T(8,128)S(1)}, u32[]{:S(2)}, u32[]{:S(2)}) collective-permute-start(f32[8,64,128]{2,1,0:T(8,128)S(1)} %triples.5), channel_id=1, source_target_pairs={{0,2},{1,3},{2,0},{3,1},{4,6},{5,7},{6,4},{7,5},{8,10},{9,11},{10,... | collective-permute-start | bytes 786440 | tf_op jit(solution)/shard_map/ppermute | solution.py:216
  25.6 18.4 %collective-permute-start.3 = (f32[8,64,128]{2,1,0:T(8,128)S(1)}, f32[8,64,128]{2,1,0:T(8,128)S(1)}, u32[]{:S(2)}, u32[]{:S(2)}) collective-permute-start(f32[8,64,128]{2,1,0:T(8,128)S(1)} %triples.4), channel_id=1, source_target_pairs={{0,14},{1,15},{2,4},{3,5},{4,2},{5,3},{6,8},{7,9},{8,6},{9,7},{10,... | collective-permute-start | bytes 786440 | tf_op jit(solution)/shard_map/ppermute | solution.py:216
  44.8 14.2 %all-to-all-start = ((f32[4,4,64,128]{3,2,1,0:T(8,128)}), f32[4,4,64,128]{3,2,1,0:T(8,128)S(1)}, u32[]{:S(2)}, u32[]{:S(2)}) async-start(f32[4,4,64,128]{3,2,1,0:T(8,128)} %bitcast.7), calls=%async_computation | async-start | bytes 1048576 | tf_op jit(solution)/shard_map/all_to_all | solution.py:225
  59.7 33.3 %all-to-all-start.1 = ((f32[16,16,128]{2,1,0:T(8,128)}), f32[16,16,128]{2,1,0:T(8,128)S(1)}, u32[]{:S(2)}, u32[]{:S(2)}) async-start(f32[16,16,128]{2,1,0:T(8,128)} %get-tuple-element.11), calls=%async_computation.1 | async-start | bytes 262144 | tf_op jit(solution)/shard_map/all_to_all | solution.py:229
  66.4 24.3 %collective-permute-start.5 = (f32[2,64,128]{2,1,0:T(8,128)S(1)}, f32[2,64,128]{2,1,0:T(8,128)S(1)}, u32[]{:S(2)}, u32[]{:S(2)}) collective-permute-start(f32[2,64,128]{2,1,0:T(8,128)S(1)} %get-tuple-element.9), channel_id=1, source_target_pairs={{0,1008},{16,0},{32,16},{48,32},{64,48},{80,64},{96,80},{112,96},{... | collective-permute-start | bytes 196616 | tf_op jit(solution)/shard_map/ppermute | solution.py:18
  82.8 10.2 %collective-permute-start.6 = (f32[2,64,128]{2,1,0:T(8,128)S(1)}, f32[2,64,128]{2,1,0:T(8,128)S(1)}, u32[]{:S(2)}, u32[]{:S(2)}) collective-permute-start(f32[2,64,128]{2,1,0:T(8,128)S(1)} %get-tuple-element.10), channel_id=1, source_target_pairs={{0,1009},{1,1008},{2,1011},{3,1010},{4,1013},{5,1012},{6,1015},{7,... | collective-permute-start | bytes 196616 | tf_op jit(solution)/shard_map/ppermute | solution.py:230

commit v7 on v6

--- a/solution.py
+++ b/solution.py
@@ -128,38 +128,35 @@
     )(mine, theirs.reshape(owners, 1, pairs, rows, lanes), *more)
 
 
-def regroup_kernel(half_ref, arrived_ref, send_ref, own_ref, other_ref, sum_ref):
-    pairs, rows, _ = sum_ref.shape
+def regroup_kernel(arrived_ref, send_ref, own_ref):
+    pairs, rows, _ = own_ref.shape
     per_owner = rows // send_ref.shape[0]
-    sum_ref[...] = jnp.sum(arrived_ref[...], axis=0)
+    own_ref[...] = jnp.sum(arrived_ref[...], axis=0)
     for g in range(send_ref.shape[0]):
         for p in range(pairs):
-            send_ref[g, p * per_owner : (p + 1) * per_owner] = sum_ref[p, g * per_owner : (g + 1) * per_owner]
-    half = half_ref[0]
-    for p in range(pairs // 2):
-        own_ref[p] = sum_ref[half * (pairs // 2) + p]
-        other_ref[p] = sum_ref[(1 - half) * (pairs // 2) + p]
-
-
-def regroup(half, arrived, parts):
+            send_ref[g, p * per_owner : (p + 1) * per_owner] = own_ref[p, g * per_owner : (g + 1) * per_owner]
+
+
+def regroup(arrived, parts):
     _, pairs, rows, lanes = arrived.shape
-    kept = jax.ShapeDtypeStruct((pairs // 2, rows, lanes), jnp.float32)
     return pl.pallas_call(
         regroup_kernel,
         name="regroup",
-        out_shape=(jax.ShapeDtypeStruct((parts, pairs * rows // parts, lanes), jnp.float32), kept, kept),
-        in_specs=[pl.BlockSpec(memory_space=pltpu.SMEM)] + in_vmem(1),
-        out_specs=tuple(in_vmem(3)),
-        scratch_shapes=[pltpu.VMEM((pairs, rows, lanes), jnp.float32)],
+        out_shape=(
+            jax.ShapeDtypeStruct((parts, pairs * rows // parts, lanes), jnp.float32),
+            jax.ShapeDtypeStruct((pairs, rows, lanes), jnp.float32),
+        ),
+        in_specs=in_vmem(1),
+        out_specs=tuple(in_vmem(2)),
         compiler_params=pltpu.CompilerParams(vmem_limit_bytes=8 * 2**20),
-    )(half, arrived)
-
-
-def finish_kernel(own_ref, other_ref, turned_ref, first_ref, second_ref, sum_ref, row_ref):
+    )(arrived)
+
+
+def finish_kernel(own_ref, turned_ref, first_ref, second_ref, sum_ref, row_ref):
     pairs, rows, lanes = own_ref.shape
     left = lax.broadcasted_iota(jnp.int32, (rows // 2, lanes), 1) < lanes // 2
     for p in range(pairs):
-        sum_ref[p * rows : (p + 1) * rows] = own_ref[p] + other_ref[p]
+        sum_ref[p * rows : (p + 1) * rows] = own_ref[p]
     for p in range(pairs):
         even = sum_ref[pl.ds(p * rows, rows // 2, stride=2), :]
         odd = sum_ref[pl.ds(p * rows + 1, rows // 2, stride=2), :]
@@ -168,28 +165,25 @@
     for c in range(rows // 2):
         first_ref[:, c * lanes : (c + 1) * lanes] = row_ref[pl.ds(c, 2 * pairs, stride=rows // 2), :]
 
-    parts, height, _ = turned_ref.shape
     per_owner = second_ref.shape[0]
-    pairs = height // per_owner
-    for z in range(parts // 2):
+    for f in range(turned_ref.shape[0]):
         for p in range(pairs):
-            c = z * pairs + p
-            at = slice(p * per_owner, (p + 1) * per_owner)
-            second_ref[:, c * lanes : (c + 1) * lanes] = turned_ref[2 * z, at] + turned_ref[2 * z + 1, at]
-
-
-def finish(own, other, turned):
+            c = f * pairs + p
+            second_ref[:, c * lanes : (c + 1) * lanes] = turned_ref[f, p * per_owner : (p + 1) * per_owner]
+
+
+def finish(own, turned):
     pairs, rows, lanes = own.shape
     out = jax.ShapeDtypeStruct((2 * pairs, rows * lanes // 2), jnp.float32)
     return pl.pallas_call(
         finish_kernel,
         name="finish",
         out_shape=(out, out),
-        in_specs=in_vmem(3),
+        in_specs=in_vmem(2),
         out_specs=tuple(in_vmem(2)),
         scratch_shapes=[pltpu.VMEM((pairs * rows, lanes), jnp.float32)] * 2,
         compiler_params=pltpu.CompilerParams(vmem_limit_bytes=4 * 2**20),
-    )(own, other, turned)
+    )(own, turned)
 
 
 def per_device(vectors):
@@ -220,16 +214,13 @@
     mine = triples(a, here, w, scale, rows // 2 // GROUP, rows // 2, run, run)
     mine = mine.reshape(peers // 2, 2, run // 4, rows, 2 * rows)
     merged = merge(mine, high, 1, merge(mine, low, 0))
-    along_z = [[2 * z + half for z in range(q, peers, 2)] for q in range(2) for half in range(2)]
-    pieces = merged.reshape(peers // 2, run // 2, rows, 2 * rows)
-    arrived = lax.all_to_all(pieces, "field", 0, 0, axis_index_groups=along_z, tiled=True)
-    half = (lax.axis_index("field") & 1).reshape(1)
-    send, own, other = regroup(half, arrived, parts)
-    crossed = [(b * parts + f, (b - 1) % blocks * parts + (f ^ 1)) for b in range(blocks) for f in range(parts)]
+    alike = [[2 * z + half for z in range(q, peers, 2) for half in range(2)] for q in range(2)]
+    pieces = merged.reshape(peers, run // 4, rows, 2 * rows)
+    arrived = lax.all_to_all(pieces, "field", 0, 0, axis_index_groups=alike, tiled=True)
+    send, own = regroup(arrived, parts)
     turned = lax.all_to_all(send, "field", split_axis=0, concat_axis=0, tiled=True)
-    other = lax.ppermute(other, ("vec", "field"), crossed)
     own = passed_along(own, "vec", -1)
-    return finish(own, other, turned)
+    return finish(own, turned)
 
 
 def solution(mesh):

time: 94.2 us -> 94.2 us (level)
  the two profiles are of different devices: /device:TPU:1 before, /device:TPU:114 now
where the time goes in v7:
time: 94.2 us; the launch traced here: 93.8 us
  blocking collectives  33.8 us (36%)
  starting transfers between devices  33.1 us (35%)
  waiting for transfers between devices  15.9 us (17%)
  Pallas kernels  9.17 us (10%)
  local copies, waits for them, and re-layouts  0.99 us (1%)
    all_to_all x1, blocking collectives, per_device(): lax.all_to_all(pieces, 'field', 0, 0, axis_index_groups=alike, tiled=True)  33.8 us
    ppermute x2, starting transfers between devices, sent(): return lax.ppermute(sums, 'field', moves)  21.4 us
    all_to_all x1, waiting for transfers between devices, per_device(): lax.all_to_all(send, 'field', split_axis=0, concat_axis=0, tiled=True)  8.88 us
    pallas_call x3, Pallas kernels, triples(): pl.pallas_call(lambda *refs: triple_kernel(scale, start, run, stride, *re...  7.5 us
    ppermute x1, starting transfers between devices, per_device(): following = lax.ppermute(vectors, 'vec', [(b, a) for a, b in inner])  3.64 us
    all_to_all x1, starting transfers between devices, per_device(): lax.all_to_all(send, 'field', split_axis=0, concat_axis=0, tiled=True)  3.53 us
    ppermute x1, waiting for transfers between devices, per_device(): previous = lax.ppermute(vectors, 'vec', inner)  1.97 us
    ppermute x1, starting transfers between devices, passed_along(): return lax.ppermute(x, axis, [(i, (i + by) % peers) for i in range(peers)])  1.92 us
  transfers between devices with their start and end apart: 7, of which 5 were waited for; matrix products, arithmetic and copies ran while one was open for 0% of the time, Pallas kernels for 6%

profile of v7, /device:TPU:114, one launch (start us, length us, event | category | flops | bytes accessed | tf_op | source)
XLA Modules:
  0.0 93.8 jit_solution(13972659956204816139)
XLA Ops:
  0.6 1.9 %collective-permute-start = (f32[64,1536]{1,0:T(8,128)}, f32[64,1536]{1,0:T(8,128)S(1)}, u32[]{:S(2)}, u32[]{:S(2)}) collective-permute-start(f32[64,1536]{1,0:T(8,128)} %in_ref.1), channel_id=1, source_target_pairs={{0,16},{16,32},{32,48},{48,64},{64,80},{80,96},{96,112},{128,144},... | collective-permute-start | bytes 1179656 | tf_op jit(solution)/shard_map/ppermute | solution.py:201
  2.6 3.6 %collective-permute-start.1 = (f32[64,1536]{1,0:T(8,128)}, f32[64,1536]{1,0:T(8,128)S(1)}, u32[]{:S(2)}, u32[]{:S(2)}) collective-permute-start(f32[64,1536]{1,0:T(8,128)} %in_ref.1), channel_id=1, source_target_pairs={{16,0},{32,16},{48,32},{64,48},{80,64},{96,80},{112,96},{144,128},... | collective-permute-start | bytes 1179656 | tf_op jit(solution)/shard_map/ppermute | solution.py:200
  6.2 0.7 collective-permute-start.2
  6.9 0.0 copy-start
  6.9 1.0 %copy-done = f32[64,1536]{1,0:T(8,128)S(1)} copy-done((f32[64,1536]{1,0:T(8,128)S(1)}, f32[64,1536]{1,0:T(8,128)}, u32[]{:S(2)}) %copy-start) | copy-done | bytes 393240
  8.0 2.0 %collective-permute-done.previous_ref = f32[64,1536]{1,0:T(8,128)S(1)} collective-permute-done((f32[64,1536]{1,0:T(8,128)}, f32[64,1536]{1,0:T(8,128)S(1)}, u32[]{:S(2)}, u32[]{:S(2)}) %collective-permute-start) | collective-permute-done | bytes 393248 | tf_op jit(solution)/shard_map/ppermute | solution.py:201
  9.9 1.9 %collective-permute-done.1.following_ref = f32[64,1536]{1,0:T(8,128)S(1)} collective-permute-done((f32[64,1536]{1,0:T(8,128)}, f32[64,1536]{1,0:T(8,128)S(1)}, u32[]{:S(2)}, u32[]{:S(2)}) %collective-permute-start.1) | collective-permute-done | bytes 393248 | tf_op jit(solution)/shard_map/ppermute | solution.py:200
  11.8 0.0 collective-permute-done.2.turned_ref
  11.8 0.2 inputs.1
  12.0 1.9 %triples.5 = f32[8,64,128]{2,1,0:T(8,128)S(1)} custom-call(f32[64,1536]{1,0:T(8,128)S(1)} %get-tuple-element.6.refs_0_, f32[64,1536]{1,0:T(8,128)S(1)} %fetch.1.refs_1_, bf16[1536,128]{1,0:T(8,128)(2,1)S(1)} %get-tuple-element.7.refs_2_), custom_call_target="tpu_custom_call" | custom-call | flops 805306368 | bytes 1441792 | tf_op jit(solution)/shard_map/triples/pallas_call | solution.py:94
  13.8 7.4 %collective-permute-start.4 = (f32[8,64,128]{2,1,0:T(8,128)S(1)}, f32[8,64,128]{2,1,0:T(8,128)S(1)}, u32[]{:S(2)}, u32[]{:S(2)}) collective-permute-start(f32[8,64,128]{2,1,0:T(8,128)S(1)} %triples.5), channel_id=1, source_target_pairs={{0,2},{1,3},{2,0},{3,1},{4,6},{5,7},{6,4},{7,5},{8,10},{9,11},{10,... | collective-permute-start | bytes 786440 | tf_op jit(solution)/shard_map/ppermute | solution.py:210
  21.2 1.9 %triples.4 = f32[8,64,128]{2,1,0:T(8,128)S(1)} custom-call(f32[64,1536]{1,0:T(8,128)S(1)} %get-tuple-element.6.refs_0_, f32[64,1536]{1,0:T(8,128)S(1)} %fetch.1.refs_1_, bf16[1536,128]{1,0:T(8,128)(2,1)S(1)} %get-tuple-element.7.refs_2_), custom_call_target="tpu_custom_call" | custom-call | flops 805306368 | bytes 1441792 | tf_op jit(solution)/shard_map/triples/pallas_call | solution.py:94
  23.1 14.0 %collective-permute-start.3 = (f32[8,64,128]{2,1,0:T(8,128)S(1)}, f32[8,64,128]{2,1,0:T(8,128)S(1)}, u32[]{:S(2)}, u32[]{:S(2)}) collective-permute-start(f32[8,64,128]{2,1,0:T(8,128)S(1)} %triples.4), channel_id=1, source_target_pairs={{0,14},{1,15},{2,4},{3,5},{4,2},{5,3},{6,8},{7,9},{8,6},{9,7},{10,... | collective-permute-start | bytes 786440 | tf_op jit(solution)/shard_map/ppermute | solution.py:210
  37.1 3.8 %triples.3 = f32[16,64,128]{2,1,0:T(8,128)S(1)} custom-call(f32[64,1536]{1,0:T(8,128)S(1)} %get-tuple-element.6.refs_0_, f32[64,1536]{1,0:T(8,128)S(1)} %fetch.1.refs_1_, bf16[1536,128]{1,0:T(8,128)(2,1)S(1)} %get-tuple-element.7.refs_2_), custom_call_target="tpu_custom_call" | custom-call | flops 1610612736 | bytes 1703936 | tf_op jit(solution)/shard_map/triples/pallas_call | solution.py:94
  40.9 0.0 collective-permute-done.4
  41.0 1.3 %collective-permute-done.3 = f32[8,64,128]{2,1,0:T(8,128)S(1)} collective-permute-done((f32[8,64,128]{2,1,0:T(8,128)S(1)}, f32[8,64,128]{2,1,0:T(8,128)S(1)}, u32[]{:S(2)}, u32[]{:S(2)}) %collective-permute-start.3) | collective-permute-done | bytes 262176 | tf_op jit(solution)/shard_map/ppermute | solution.py:210
  42.3 33.8 %all_to_all.10.arrived_ref = f32[8,2,64,128]{3,2,1,0:T(8,128)S(1)} all-to-all(f32[8,2,64,128]{3,2,1,0:T(8,128)S(1)} %bitcast.7), channel_id=1, replica_groups={{0,1,4,5,8,9,12,13},{2,3,6,7,10,11,14,15},{16,17,20,21,24,25,28,29},{18..., dimensions={0} | all-to-all | bytes 1048576 | tf_op jit(solution)/shard_map/all_to_all | solution.py:219
  76.1 0.7 regroup.1
  76.8 3.5 %all-to-all-start.1 = ((f32[16,8,128]{2,1,0:T(8,128)}), f32[16,8,128]{2,1,0:T(8,128)S(1)}, u32[]{:S(2)}, u32[]{:S(2)}) async-start(f32[16,8,128]{2,1,0:T(8,128)} %get-tuple-element.9), calls=%async_computation.1 | async-start | bytes 131072 | tf_op jit(solution)/shard_map/all_to_all | solution.py:221
  80.3 1.9 %collective-permute-start.5 = (f32[2,64,128]{2,1,0:T(8,128)S(1)}, f32[2,64,128]{2,1,0:T(8,128)S(1)}, u32[]{:S(2)}, u32[]{:S(2)}) collective-permute-start(f32[2,64,128]{2,1,0:T(8,128)S(1)} %get-tuple-element.8), channel_id=1, source_target_pairs={{0,1008},{16,0},{32,16},{48,32},{64,48},{80,64},{96,80},{112,96},{... | collective-permute-start | bytes 196616 | tf_op jit(solution)/shard_map/ppermute | solution.py:18
  82.2 1.9 %collective-permute-done.5.own_ref = f32[2,64,128]{2,1,0:T(8,128)S(1)} collective-permute-done((f32[2,64,128]{2,1,0:T(8,128)S(1)}, f32[2,64,128]{2,1,0:T(8,128)S(1)}, u32[]{:S(2)}, u32[]{:S(2)}) %collective-permute-start.5) | collective-permute-done | bytes 65568 | tf_op jit(solution)/shard_map/ppermute | solution.py:18
  84.1 8.9 %all-to-all-done.1.turned_ref = f32[16,8,128]{2,1,0:T(8,128)S(1)} async-done(((f32[16,8,128]{2,1,0:T(8,128)}), f32[16,8,128]{2,1,0:T(8,128)S(1)}, u32[]{:S(2)}, u32[]{:S(2)}) %all-to-all-start.1) | async-done | bytes 65568 | tf_op jit(solution)/shard_map/all_to_all | solution.py:221
  93.0 0.8 finish.1
  (3 shorter events, 0.1 us)
Async XLA Ops:
  0.6 9.3 %collective-permute-start = (f32[64,1536]{1,0:T(8,128)}, f32[64,1536]{1,0:T(8,128)S(1)}, u32[]{:S(2)}, u32[]{:S(2)}) collective-permute-start(f32[64,1536]{1,0:T(8,128)} %in_ref.1), channel_id=1, source_target_pairs={{0,16},{16,32},{32,48},{48,64},{64,80},{80,96},{96,112},{128,144},... | collective-permute-start | bytes 1179656 | tf_op jit(solution)/shard_map/ppermute | solution.py:201
  2.6 9.2 %collective-permute-start.1 = (f32[64,1536]{1,0:T(8,128)}, f32[64,1536]{1,0:T(8,128)S(1)}, u32[]{:S(2)}, u32[]{:S(2)}) collective-permute-start(f32[64,1536]{1,0:T(8,128)} %in_ref.1), channel_id=1, source_target_pairs={{16,0},{32,16},{48,32},{64,48},{80,64},{96,80},{112,96},{144,128},... | collective-permute-start | bytes 1179656 | tf_op jit(solution)/shard_map/ppermute | solution.py:200
  6.2 5.6 %collective-permute-start.2 = (f32[64,1536]{1,0:T(8,128)}, f32[64,1536]{1,0:T(8,128)S(1)}, u32[]{:S(2)}, u32[]{:S(2)}) collective-permute-start(f32[64,1536]{1,0:T(8,128)} %in_ref.1), channel_id=1, source_target_pairs={{1008,0},{112,128},{240,256},{368,384},{496,512},{624,640},{752,76... | collective-permute-start | bytes 1179656 | tf_op jit(solution)/shard_map/ppermute | solution.py:198
  6.9 1.0 %copy-start = (f32[64,1536]{1,0:T(8,128)S(1)}, f32[64,1536]{1,0:T(8,128)}, u32[]{:S(2)}) copy-start(f32[64,1536]{1,0:T(8,128)} %in_ref.1) | copy-start | bytes 1179652
  13.8 27.1 %collective-permute-start.4 = (f32[8,64,128]{2,1,0:T(8,128)S(1)}, f32[8,64,128]{2,1,0:T(8,128)S(1)}, u32[]{:S(2)}, u32[]{:S(2)}) collective-permute-start(f32[8,64,128]{2,1,0:T(8,128)S(1)} %triples.5), channel_id=1, source_target_pairs={{0,2},{1,3},{2,0},{3,1},{4,6},{5,7},{6,4},{7,5},{8,10},{9,11},{10,... | collective-permute-start | bytes 786440 | tf_op jit(solution)/shard_map/ppermute | solution.py:210
  23.1 19.1 %collective-permute-start.3 = (f32[8,64,128]{2,1,0:T(8,128)S(1)}, f32[8,64,128]{2,1,0:T(8,128)S(1)}, u32[]{:S(2)}, u32[]{:S(2)}) collective-permute-start(f32[8,64,128]{2,1,0:T(8,128)S(1)} %triples.4), channel_id=1, source_target_pairs={{0,14},{1,15},{2,4},{3,5},{4,2},{5,3},{6,8},{7,9},{8,6},{9,7},{10,... | collective-permute-start | bytes 786440 | tf_op jit(solution)/shard_map/ppermute | solution.py:210
  76.8 16.2 %all-to-all-start.1 = ((f32[16,8,128]{2,1,0:T(8,128)}), f32[16,8,128]{2,1,0:T(8,128)S(1)}, u32[]{:S(2)}, u32[]{:S(2)}) async-start(f32[16,8,128]{2,1,0:T(8,128)} %get-tuple-element.9), calls=%async_computation.1 | async-start | bytes 131072 | tf_op jit(solution)/shard_map/all_to_all | solution.py:221
  80.3 3.8 %collective-permute-start.5 = (f32[2,64,128]{2,1,0:T(8,128)S(1)}, f32[2,64,128]{2,1,0:T(8,128)S(1)}, u32[]{:S(2)}, u32[]{:S(2)}) collective-permute-start(f32[2,64,128]{2,1,0:T(8,128)S(1)} %get-tuple-element.8), channel_id=1, source_target_pairs={{0,1008},{16,0},{32,16},{48,32},{64,48},{80,64},{96,80},{112,96},{... | collective-permute-start | bytes 196616 | tf_op jit(solution)/shard_map/ppermute | solution.py:18

commit v8 on v6

--- a/solution.py
+++ b/solution.py
@@ -128,31 +128,31 @@
     )(mine, theirs.reshape(owners, 1, pairs, rows, lanes), *more)
 
 
-def regroup_kernel(half_ref, arrived_ref, send_ref, own_ref, other_ref, sum_ref):
+def regroup_kernel(arrived_ref, send_ref, own_ref, other_ref, sum_ref):
     pairs, rows, _ = sum_ref.shape
     per_owner = rows // send_ref.shape[0]
     sum_ref[...] = jnp.sum(arrived_ref[...], axis=0)
     for g in range(send_ref.shape[0]):
         for p in range(pairs):
             send_ref[g, p * per_owner : (p + 1) * per_owner] = sum_ref[p, g * per_owner : (g + 1) * per_owner]
-    half = half_ref[0]
+    half = lax.rem(lax.axis_index("field"), 2)
     for p in range(pairs // 2):
         own_ref[p] = sum_ref[half * (pairs // 2) + p]
         other_ref[p] = sum_ref[(1 - half) * (pairs // 2) + p]
 
 
-def regroup(half, arrived, parts):
+def regroup(arrived, parts):
     _, pairs, rows, lanes = arrived.shape
     kept = jax.ShapeDtypeStruct((pairs // 2, rows, lanes), jnp.float32)
     return pl.pallas_call(
         regroup_kernel,
         name="regroup",
         out_shape=(jax.ShapeDtypeStruct((parts, pairs * rows // parts, lanes), jnp.float32), kept, kept),
-        in_specs=[pl.BlockSpec(memory_space=pltpu.SMEM)] + in_vmem(1),
+        in_specs=in_vmem(1),
         out_specs=tuple(in_vmem(3)),
         scratch_shapes=[pltpu.VMEM((pairs, rows, lanes), jnp.float32)],
         compiler_params=pltpu.CompilerParams(vmem_limit_bytes=8 * 2**20),
-    )(half, arrived)
+    )(arrived)
 
 
 def finish_kernel(own_ref, other_ref, turned_ref, first_ref, second_ref, sum_ref, row_ref):
@@ -223,8 +223,7 @@
     along_z = [[2 * z + half for z in range(q, peers, 2)] for q in range(2) for half in range(2)]
     pieces = merged.reshape(peers // 2, run // 2, rows, 2 * rows)
     arrived = lax.all_to_all(pieces, "field", 0, 0, axis_index_groups=along_z, tiled=True)
-    half = (lax.axis_index("field") & 1).reshape(1)
-    send, own, other = regroup(half, arrived, parts)
+    send, own, other = regroup(arrived, parts)
     crossed = [(b * parts + f, (b - 1) % blocks * parts + (f ^ 1)) for b in range(blocks) for f in range(parts)]
     turned = lax.all_to_all(send, "field", split_axis=0, concat_axis=0, tiled=True)
     other = lax.ppermute(other, ("vec", "field"), crossed)

time: 94.2 us -> 94 us (level)
  blocking collectives: 0 us -> 14.4 us
  waiting for transfers between devices: 13.1 us -> 2.24 us
  starting transfers between devices: 68.3 us -> 65.8 us
  Pallas kernels: 10.6 us -> 9.22 us
    all_to_all x0 -> x1, blocking collectives: none -> 14.4 us  [per_device(): lax.all_to_all(pieces, 'field', 0, 0, axis_index_groups=along_z, tiled=True)]
    all_to_all x1 -> x0, waiting for transfers between devices: 10.7 us -> none  [per_device(): lax.all_to_all(pieces, 'field', 0, 0, axis_index_groups=along_z, tiled=True)]
    all_to_all x1 -> x0, starting transfers between devices: 3.47 us -> none  [per_device(): lax.all_to_all(pieces, 'field', 0, 0, axis_index_groups=along_z, tiled=True)]
    ppermute x1, starting transfers between devices: 16.4 us -> 18 us  [passed_along(): return lax.ppermute(x, axis, [(i, (i + by) % peers) for i in range(peers)])]
    pallas_call x2, Pallas kernels: 1.46 us -> 0.06 us  [merge(): pl.pallas_call(merge_kernel, name='merge', grid=(1,), out_shape=jax.Shape...]
  transfers between devices with their start and end apart: 9 -> 8, of which waited for: 2 -> 1; matrix products, arithmetic and copies ran while one was open for 0% -> 0% of each run, Pallas kernels for 7% -> 6%
where the time goes in v8:
time: 94 us; the launch traced here: 93.6 us
  starting transfers between devices  65.8 us (70%)
  blocking collectives  14.4 us (15%)
  Pallas kernels  9.22 us (10%)
  waiting for transfers between devices  2.24 us (2%)
  local copies, waits for them, and re-layouts  0.99 us (1%)
    ppermute x1, starting transfers between devices, passed_along(): return lax.ppermute(x, axis, [(i, (i + by) % peers) for i in range(peers)])  18 us
    ppermute x2, starting transfers between devices, sent(): return lax.ppermute(sums, 'field', moves)  15.8 us
    all_to_all x1, blocking collectives, per_device(): lax.all_to_all(pieces, 'field', 0, 0, axis_index_groups=along_z, tiled=True)  14.4 us
    ppermute x1, starting transfers between devices, per_device(): following = lax.ppermute(vectors, 'vec', [(b, a) for a, b in inner])  12.8 us
    pallas_call x3, Pallas kernels, triples(): pl.pallas_call(lambda *refs: triple_kernel(scale, start, run, stride, *re...  7.52 us
    ppermute x1, starting transfers between devices, per_device(): other = lax.ppermute(other, ('vec', 'field'), crossed)  7.35 us
    all_to_all x1, starting transfers between devices, per_device(): lax.all_to_all(send, 'field', split_axis=0, concat_axis=0, tiled=True)  6.61 us
    ppermute x1, starting transfers between devices, per_device(): previous = lax.ppermute(vectors, 'vec', inner)  4.5 us
  transfers between devices with their start and end apart: 8, of which 1 were waited for; matrix products, arithmetic and copies ran while one was open for 0% of the time, Pallas kernels for 6%

profile of v8, /device:TPU:1, one launch (start us, length us, event | category | flops | bytes accessed | tf_op | source)
XLA Modules:
  0.0 93.6 jit_solution(10697277289274012526)
XLA Ops:
  0.6 4.5 %collective-permute-start = (f32[64,1536]{1,0:T(8,128)}, f32[64,1536]{1,0:T(8,128)S(1)}, u32[]{:S(2)}, u32[]{:S(2)}) collective-permute-start(f32[64,1536]{1,0:T(8,128)} %in_ref.1), channel_id=1, source_target_pairs={{0,16},{16,32},{32,48},{48,64},{64,80},{80,96},{96,112},{128,144},... | collective-permute-start | bytes 1179656 | tf_op jit(solution)/shard_map/ppermute | solution.py:207
  5.1 12.8 %collective-permute-start.1 = (f32[64,1536]{1,0:T(8,128)}, f32[64,1536]{1,0:T(8,128)S(1)}, u32[]{:S(2)}, u32[]{:S(2)}) collective-permute-start(f32[64,1536]{1,0:T(8,128)} %in_ref.1), channel_id=1, source_target_pairs={{16,0},{32,16},{48,32},{64,48},{80,64},{96,80},{112,96},{144,128},... | collective-permute-start | bytes 1179656 | tf_op jit(solution)/shard_map/ppermute | solution.py:206
  18.0 0.7 collective-permute-start.2
  18.7 0.0 copy-start
  18.7 1.0 %copy-done = f32[64,1536]{1,0:T(8,128)S(1)} copy-done((f32[64,1536]{1,0:T(8,128)S(1)}, f32[64,1536]{1,0:T(8,128)}, u32[]{:S(2)}) %copy-start) | copy-done | bytes 393240
  19.7 0.0 collective-permute-done.previous_ref
  19.7 0.0 collective-permute-done.1.following_ref
  19.8 0.0 collective-permute-done.2.turned_ref
  19.8 0.2 inputs.1
  19.9 1.9 %triples.5 = f32[8,64,128]{2,1,0:T(8,128)S(1)} custom-call(f32[64,1536]{1,0:T(8,128)S(1)} %get-tuple-element.7.refs_0_, f32[64,1536]{1,0:T(8,128)S(1)} %fetch.1.refs_1_, bf16[1536,128]{1,0:T(8,128)(2,1)S(1)} %get-tuple-element.8.refs_2_), custom_call_target="tpu_custom_call" | custom-call | flops 805306368 | bytes 1441792 | tf_op jit(solution)/shard_map/triples/pallas_call | solution.py:94
  21.8 1.9 %collective-permute-start.4 = (f32[8,64,128]{2,1,0:T(8,128)S(1)}, f32[8,64,128]{2,1,0:T(8,128)S(1)}, u32[]{:S(2)}, u32[]{:S(2)}) collective-permute-start(f32[8,64,128]{2,1,0:T(8,128)S(1)} %triples.5), channel_id=1, source_target_pairs={{0,2},{1,3},{2,0},{3,1},{4,6},{5,7},{6,4},{7,5},{8,10},{9,11},{10,... | collective-permute-start | bytes 786440 | tf_op jit(solution)/shard_map/ppermute | solution.py:216
  23.7 1.9 %triples.4 = f32[8,64,128]{2,1,0:T(8,128)S(1)} custom-call(f32[64,1536]{1,0:T(8,128)S(1)} %get-tuple-element.7.refs_0_, f32[64,1536]{1,0:T(8,128)S(1)} %fetch.1.refs_1_, bf16[1536,128]{1,0:T(8,128)(2,1)S(1)} %get-tuple-element.8.refs_2_), custom_call_target="tpu_custom_call" | custom-call | flops 805306368 | bytes 1441792 | tf_op jit(solution)/shard_map/triples/pallas_call | solution.py:94
  25.6 13.9 %collective-permute-start.3 = (f32[8,64,128]{2,1,0:T(8,128)S(1)}, f32[8,64,128]{2,1,0:T(8,128)S(1)}, u32[]{:S(2)}, u32[]{:S(2)}) collective-permute-start(f32[8,64,128]{2,1,0:T(8,128)S(1)} %triples.4), channel_id=1, source_target_pairs={{0,14},{1,15},{2,4},{3,5},{4,2},{5,3},{6,8},{7,9},{8,6},{9,7},{10,... | collective-permute-start | bytes 786440 | tf_op jit(solution)/shard_map/ppermute | solution.py:216
  39.5 3.8 %triples.3 = f32[16,64,128]{2,1,0:T(8,128)S(1)} custom-call(f32[64,1536]{1,0:T(8,128)S(1)} %get-tuple-element.7.refs_0_, f32[64,1536]{1,0:T(8,128)S(1)} %fetch.1.refs_1_, bf16[1536,128]{1,0:T(8,128)(2,1)S(1)} %get-tuple-element.8.refs_2_), custom_call_target="tpu_custom_call" | custom-call | flops 1610612736 | bytes 1703936 | tf_op jit(solution)/shard_map/triples/pallas_call | solution.py:94
  43.3 0.0 collective-permute-done.4
  43.4 0.0 collective-permute-done.3
  43.4 14.4 %all_to_all.10.arrived_ref = f32[4,4,64,128]{3,2,1,0:T(8,128)S(1)} all-to-all(f32[4,4,64,128]{3,2,1,0:T(8,128)S(1)} %bitcast.7), channel_id=1, replica_groups={{0,4,8,12},{1,5,9,13},{2,6,10,14},{3,7,11,15},{16,20,24,28},{17,21,25,2..., dimensions={0} | all-to-all | bytes 1048576 | tf_op jit(solution)/shard_map/all_to_all | solution.py:225
  57.9 0.7 regroup.1
  58.6 6.6 %all-to-all-start.1 = ((f32[16,16,128]{2,1,0:T(8,128)}), f32[16,16,128]{2,1,0:T(8,128)S(1)}, u32[]{:S(2)}, u32[]{:S(2)}) async-start(f32[16,16,128]{2,1,0:T(8,128)} %get-tuple-element.11), calls=%async_computation.1 | async-start | bytes 262144 | tf_op jit(solution)/shard_map/all_to_all | solution.py:228
  65.2 18.0 %collective-permute-start.5 = (f32[2,64,128]{2,1,0:T(8,128)S(1)}, f32[2,64,128]{2,1,0:T(8,128)S(1)}, u32[]{:S(2)}, u32[]{:S(2)}) collective-permute-start(f32[2,64,128]{2,1,0:T(8,128)S(1)} %get-tuple-element.9), channel_id=1, source_target_pairs={{0,1008},{16,0},{32,16},{48,32},{64,48},{80,64},{96,80},{112,96},{... | collective-permute-start | bytes 196616 | tf_op jit(solution)/shard_map/ppermute | solution.py:18
  83.2 7.3 %collective-permute-start.6 = (f32[2,64,128]{2,1,0:T(8,128)S(1)}, f32[2,64,128]{2,1,0:T(8,128)S(1)}, u32[]{:S(2)}, u32[]{:S(2)}) collective-permute-start(f32[2,64,128]{2,1,0:T(8,128)S(1)} %get-tuple-element.10), channel_id=1, source_target_pairs={{0,1009},{1,1008},{2,1011},{3,1010},{4,1013},{5,1012},{6,1015},{7,... | collective-permute-start | bytes 196616 | tf_op jit(solution)/shard_map/ppermute | solution.py:229
  90.6 0.0 collective-permute-done.5.own_ref
  90.6 2.2 %collective-permute-done.6.other_ref = f32[2,64,128]{2,1,0:T(8,128)S(1)} collective-permute-done((f32[2,64,128]{2,1,0:T(8,128)S(1)}, f32[2,64,128]{2,1,0:T(8,128)S(1)}, u32[]{:S(2)}, u32[]{:S(2)}) %collective-permute-start.6) | collective-permute-done | bytes 65568 | tf_op jit(solution)/shard_map/ppermute | solution.py:229
  92.8 0.0 all-to-all-done.1.turned_ref
  92.8 0.8 finish.1
  (3 shorter events, 0.1 us)
Async XLA Ops:
  0.6 19.1 %collective-permute-start = (f32[64,1536]{1,0:T(8,128)}, f32[64,1536]{1,0:T(8,128)S(1)}, u32[]{:S(2)}, u32[]{:S(2)}) collective-permute-start(f32[64,1536]{1,0:T(8,128)} %in_ref.1), channel_id=1, source_target_pairs={{0,16},{16,32},{32,48},{48,64},{64,80},{80,96},{96,112},{128,144},... | collective-permute-start | bytes 1179656 | tf_op jit(solution)/shard_map/ppermute | solution.py:207
  5.1 14.6 %collective-permute-start.1 = (f32[64,1536]{1,0:T(8,128)}, f32[64,1536]{1,0:T(8,128)S(1)}, u32[]{:S(2)}, u32[]{:S(2)}) collective-permute-start(f32[64,1536]{1,0:T(8,128)} %in_ref.1), channel_id=1, source_target_pairs={{16,0},{32,16},{48,32},{64,48},{80,64},{96,80},{112,96},{144,128},... | collective-permute-start | bytes 1179656 | tf_op jit(solution)/shard_map/ppermute | solution.py:206
  18.0 1.8 %collective-permute-start.2 = (f32[64,1536]{1,0:T(8,128)}, f32[64,1536]{1,0:T(8,128)S(1)}, u32[]{:S(2)}, u32[]{:S(2)}) collective-permute-start(f32[64,1536]{1,0:T(8,128)} %in_ref.1), channel_id=1, source_target_pairs={{1008,0},{112,128},{240,256},{368,384},{496,512},{624,640},{752,76... | collective-permute-start | bytes 1179656 | tf_op jit(solution)/shard_map/ppermute | solution.py:204
  18.7 1.0 %copy-start = (f32[64,1536]{1,0:T(8,128)S(1)}, f32[64,1536]{1,0:T(8,128)}, u32[]{:S(2)}) copy-start(f32[64,1536]{1,0:T(8,128)} %in_ref.1) | copy-start | bytes 1179652
  21.8 21.5 %collective-permute-start.4 = (f32[8,64,128]{2,1,0:T(8,128)S(1)}, f32[8,64,128]{2,1,0:T(8,128)S(1)}, u32[]{:S(2)}, u32[]{:S(2)}) collective-permute-start(f32[8,64,128]{2,1,0:T(8,128)S(1)} %triples.5), channel_id=1, source_target_pairs={{0,2},{1,3},{2,0},{3,1},{4,6},{5,7},{6,4},{7,5},{8,10},{9,11},{10,... | collective-permute-start | bytes 786440 | tf_op jit(solution)/shard_map/ppermute | solution.py:216
  25.6 17.7 %collective-permute-start.3 = (f32[8,64,128]{2,1,0:T(8,128)S(1)}, f32[8,64,128]{2,1,0:T(8,128)S(1)}, u32[]{:S(2)}, u32[]{:S(2)}) collective-permute-start(f32[8,64,128]{2,1,0:T(8,128)S(1)} %triples.4), channel_id=1, source_target_pairs={{0,14},{1,15},{2,4},{3,5},{4,2},{5,3},{6,8},{7,9},{8,6},{9,7},{10,... | collective-permute-start | bytes 786440 | tf_op jit(solution)/shard_map/ppermute | solution.py:216
  58.6 34.3 %all-to-all-start.1 = ((f32[16,16,128]{2,1,0:T(8,128)}), f32[16,16,128]{2,1,0:T(8,128)S(1)}, u32[]{:S(2)}, u32[]{:S(2)}) async-start(f32[16,16,128]{2,1,0:T(8,128)} %get-tuple-element.11), calls=%async_computation.1 | async-start | bytes 262144 | tf_op jit(solution)/shard_map/all_to_all | solution.py:228
  65.2 25.4 %collective-permute-start.5 = (f32[2,64,128]{2,1,0:T(8,128)S(1)}, f32[2,64,128]{2,1,0:T(8,128)S(1)}, u32[]{:S(2)}, u32[]{:S(2)}) collective-permute-start(f32[2,64,128]{2,1,0:T(8,128)S(1)} %get-tuple-element.9), channel_id=1, source_target_pairs={{0,1008},{16,0},{32,16},{48,32},{64,48},{80,64},{96,80},{112,96},{... | collective-permute-start | bytes 196616 | tf_op jit(solution)/shard_map/ppermute | solution.py:18
  83.2 9.6 %collective-permute-start.6 = (f32[2,64,128]{2,1,0:T(8,128)S(1)}, f32[2,64,128]{2,1,0:T(8,128)S(1)}, u32[]{:S(2)}, u32[]{:S(2)}) collective-permute-start(f32[2,64,128]{2,1,0:T(8,128)S(1)} %get-tuple-element.10), channel_id=1, source_target_pairs={{0,1009},{1,1008},{2,1011},{3,1010},{4,1013},{5,1012},{6,1015},{7,... | collective-permute-start | bytes 196616 | tf_op jit(solution)/shard_map/ppermute | solution.py:229

commit v9 on v3

--- a/solution.py
+++ b/solution.py
@@ -8,7 +8,8 @@
 from jax.sharding import PartitionSpec as P
 
 
-STEPS = 4
+GROUP = 32
+LINE = 8
 
 
 def passed_along(x, axis, by):
@@ -41,72 +42,91 @@
     )(x)
 
 
-def triple_kernel(scale, a_ref, b_ref, c_ref, out_ref, w_ref):
+def inputs_kernel(first_ref, last_ref, previous_ref, following_ref, turned_ref, a_ref, w_ref):
+    a_ref[...] = jnp.where(first_ref[0] == 1, turned_ref[...], previous_ref[...])
+    c = jnp.where(last_ref[0] == 1, turned_ref[...], following_ref[...])
+    w_ref[...] = jnp.concatenate(two_halves(c), 0).T
+
+
+def inputs(place, previous, following, turned):
+    rows, fields = previous.shape
+    return pl.pallas_call(
+        inputs_kernel,
+        name="inputs",
+        out_shape=(
+            jax.ShapeDtypeStruct(previous.shape, jnp.float32),
+            jax.ShapeDtypeStruct((fields, 2 * rows), jnp.bfloat16),
+        ),
+        in_specs=[pl.BlockSpec(memory_space=pltpu.SMEM)] * 2 + in_vmem(3),
+        out_specs=tuple(in_vmem(2)),
+        compiler_params=pltpu.CompilerParams(vmem_limit_bytes=8 * 2**20),
+        cost_estimate=pl.CostEstimate(flops=previous.size, bytes_accessed=20 * previous.size, transcendentals=0),
+    )(*place, previous, following, turned)
+
+
+def triple_kernel(scale, a_ref, b_ref, w_ref, out_ref):
     rows = b_ref.shape[0]
-    group = 2 * out_ref.shape[0]
-
-    @pl.when(pl.program_id(0) == 0)
-    def _():
-        w_ref[...] = jnp.concatenate(two_halves(c_ref[...]), 0).T
-
     first_half = lax.broadcasted_iota(jnp.int32, (rows, 2 * rows), 1) < rows
-    highs, lows = [], []
-    for u in range(group):
-        high, low = two_halves(a_ref[pl.ds(pl.program_id(0) * group + u, 1), :] * b_ref[...])
-        highs.append(high)
-        lows.append(low)
-    w = w_ref[...]
-    r = jnp.dot(jnp.concatenate(highs, 0), w, preferred_element_type=jnp.float32)
-    r = r + jnp.dot(jnp.concatenate(lows, 0), w, preferred_element_type=jnp.float32)
-    r = (r + pltpu.roll(r, rows, 1)) * scale
-    for u in range(group // 2):
-        even = r[2 * u * rows : (2 * u + 1) * rows]
-        odd = r[(2 * u + 1) * rows : (2 * u + 2) * rows]
-        out_ref[u] = jnp.where(first_half, even, odd)
-
-
-def triples(a, b, c, scale):
+
+    def step(g, carry):
+        highs, lows = [], []
+        for u in range(GROUP):
+            high, low = two_halves(a_ref[pl.ds(g * GROUP + u, 1), :] * b_ref[...])
+            highs.append(high)
+            lows.append(low)
+        w = w_ref[...]
+        r = jnp.dot(jnp.concatenate(highs, 0), w, preferred_element_type=jnp.float32)
+        r = r + jnp.dot(jnp.concatenate(lows, 0), w, preferred_element_type=jnp.float32)
+        r = (r + pltpu.roll(r, rows, 1)) * scale
+        for u in range(GROUP // 2):
+            even = r[2 * u * rows : (2 * u + 1) * rows]
+            odd = r[(2 * u + 1) * rows : (2 * u + 2) * rows]
+            out_ref[g * (GROUP // 2) + u] = jnp.where(first_half, even, odd)
+        return carry
+
+    lax.fori_loop(0, rows // GROUP, step, 0)
+
+
+def triples(a, b, w, scale):
     rows, fields = b.shape
     return pl.pallas_call(
         lambda *refs: triple_kernel(scale, *refs),
         name="triples",
-        grid=(STEPS,),
         out_shape=jax.ShapeDtypeStruct((rows // 2, rows, 2 * rows), jnp.float32),
         in_specs=in_vmem(3),
-        out_specs=pl.BlockSpec((rows // 2 // STEPS, rows, 2 * rows), lambda s: (s, 0, 0)),
-        scratch_shapes=[pltpu.VMEM((fields, 2 * rows), jnp.bfloat16)],
+        out_specs=pl.BlockSpec(memory_space=pltpu.VMEM),
         compiler_params=pltpu.CompilerParams(vmem_limit_bytes=40 * 2**20),
         cost_estimate=pl.CostEstimate(
             flops=8 * rows**3 * fields, bytes_accessed=4 * (rows**3 + 3 * rows * fields), transcendentals=0
         ),
-    )(a, b, c)
-
-
-def regroup_kernel(half_ref, arrived_ref, send_ref, own_ref, other_ref, sum_ref):
+    )(a, b, w)
+
+
+def regroup_kernel(arrived_ref, send_ref, own_ref, other_ref, sum_ref):
     pairs, rows, _ = sum_ref.shape
     per_owner = rows // send_ref.shape[0]
     sum_ref[...] = jnp.sum(arrived_ref[...], axis=0)
     for g in range(send_ref.shape[0]):
         for p in range(pairs):
             send_ref[g, p * per_owner : (p + 1) * per_owner] = sum_ref[p, g * per_owner : (g + 1) * per_owner]
-    half = half_ref[0]
+    half = lax.rem(lax.axis_index("field"), 2)
     for p in range(pairs // 2):
         own_ref[p] = sum_ref[half * (pairs // 2) + p]
         other_ref[p] = sum_ref[(1 - half) * (pairs // 2) + p]
 
 
-def regroup(half, arrived, parts):
+def regroup(arrived, parts):
     _, pairs, rows, lanes = arrived.shape
     kept = jax.ShapeDtypeStruct((pairs // 2, rows, lanes), jnp.float32)
     return pl.pallas_call(
         regroup_kernel,
         name="regroup",
         out_shape=(jax.ShapeDtypeStruct((parts, pairs * rows // parts, lanes), jnp.float32), kept, kept),
-        in_specs=[pl.BlockSpec(memory_space=pltpu.SMEM)] + in_vmem(1),
+        in_specs=in_vmem(1),
         out_specs=tuple(in_vmem(3)),
         scratch_shapes=[pltpu.VMEM((pairs, rows, lanes), jnp.float32)],
         compiler_params=pltpu.CompilerParams(vmem_limit_bytes=8 * 2**20),
-    )(half, arrived)
+    )(arrived)
 
 
 def finish_kernel(own_ref, other_ref, turned_ref, first_ref, second_ref, sum_ref, row_ref):
@@ -150,14 +170,21 @@
     blocks, parts = lax.axis_size("vec"), lax.axis_size("field")
     rows = vectors.shape[0]
     scale = 1.0 / math.sqrt(vectors.shape[1] * parts)
-    previous = passed_along(vectors, "vec", 1)
-    following = passed_along(vectors, "vec", -1)
-    partial = triples(previous, fetched(vectors), following, scale)
+    line = LINE if blocks % LINE == 0 else blocks
+    ends = [((b - 1) % blocks, b) for b in range(0, blocks, line)]
+    inner = [(b - 1, b) for b in range(blocks) if b % line]
+    turned = lax.ppermute(vectors, "vec", ends + [(b, a) for a, b in ends])
+    here = fetched(vectors)
+    following = lax.ppermute(vectors, "vec", [(b, a) for a, b in inner])
+    previous = lax.ppermute(vectors, "vec", inner)
+    spot = lax.rem(lax.axis_index("vec"), line)
+    place = [x.astype(jnp.int32).reshape(1) for x in (spot == 0, spot == line - 1)]
+    a, w = inputs(place, previous, following, turned)
+    partial = triples(a, here, w, scale)
     along_z = [[2 * z + half for z in range(parts // 2)] for half in range(2)]
     pieces = partial.reshape(parts // 2, rows // parts, rows, 2 * rows)
     arrived = lax.all_to_all(pieces, "field", 0, 0, axis_index_groups=along_z, tiled=True)
-    half = (lax.axis_index("field") & 1).reshape(1)
-    send, own, other = regroup(half, arrived, parts)
+    send, own, other = regroup(arrived, parts)
     crossed = [(b * parts + f, (b - 1) % blocks * parts + (f ^ 1)) for b in range(blocks) for f in range(parts)]
     turned = lax.all_to_all(send, "field", split_axis=0, concat_axis=0, tiled=True)
     other = lax.ppermute(other, ("vec", "field"), crossed)

time: 93.8 us -> 93.5 us (level)
  the two profiles are of different devices: /device:TPU:28 before, /device:TPU:1 now
where the time goes in v9:
time: 93.5 us; the launch traced here: 93.1 us
  starting transfers between devices  48.3 us (52%)
  blocking collectives  33 us (35%)
  Pallas kernels  8.76 us (9%)
  waiting for transfers between devices  1.31 us (1%)
  local copies, waits for them, and re-layouts  0.99 us (1%)
    all_to_all x1, blocking collectives, per_device(): lax.all_to_all(pieces, 'field', 0, 0, axis_index_groups=along_z, tiled=True)  33 us
    ppermute x1, starting transfers between devices, per_device(): other = lax.ppermute(other, ('vec', 'field'), crossed)  13.5 us
    ppermute x1, starting transfers between devices, per_device(): following = lax.ppermute(vectors, 'vec', [(b, a) for a, b in inner])  12.8 us
    ppermute x1, starting transfers between devices, passed_along(): return lax.ppermute(x, axis, [(i, (i + by) % peers) for i in range(peers)])  9.29 us
    all_to_all x1, starting transfers between devices, per_device(): lax.all_to_all(send, 'field', split_axis=0, concat_axis=0, tiled=True)  7.5 us
    pallas_call x1, Pallas kernels, triples(): pl.pallas_call(lambda *refs: triple_kernel(scale, *refs), name='triples',...  7.08 us
    ppermute x1, starting transfers between devices, per_device(): previous = lax.ppermute(vectors, 'vec', inner)  4.5 us
  transfers between devices with their start and end apart: 6, of which 1 were waited for; matrix products, arithmetic and copies ran while one was open for 0% of the time, Pallas kernels for 0%

profile of v9, /device:TPU:1, one launch (start us, length us, event | category | flops | bytes accessed | tf_op | source)
XLA Modules:
  0.0 93.1 jit_solution(10257769081670826057)
XLA Ops:
  0.6 4.5 %collective-permute-start = (f32[64,1536]{1,0:T(8,128)}, f32[64,1536]{1,0:T(8,128)S(1)}, u32[]{:S(2)}, u32[]{:S(2)}) collective-permute-start(f32[64,1536]{1,0:T(8,128)} %in_ref.1), channel_id=1, source_target_pairs={{0,16},{16,32},{32,48},{48,64},{64,80},{80,96},{96,112},{128,144},... | collective-permute-start | bytes 1179656 | tf_op jit(solution)/shard_map/ppermute | solution.py:179
  5.1 12.8 %collective-permute-start.1 = (f32[64,1536]{1,0:T(8,128)}, f32[64,1536]{1,0:T(8,128)S(1)}, u32[]{:S(2)}, u32[]{:S(2)}) collective-permute-start(f32[64,1536]{1,0:T(8,128)} %in_ref.1), channel_id=1, source_target_pairs={{16,0},{32,16},{48,32},{64,48},{80,64},{96,80},{112,96},{144,128},... | collective-permute-start | bytes 1179656 | tf_op jit(solution)/shard_map/ppermute | solution.py:178
  18.0 0.7 collective-permute-start.2
  18.7 0.0 copy-start
  18.7 1.0 %copy-done = f32[64,1536]{1,0:T(8,128)S(1)} copy-done((f32[64,1536]{1,0:T(8,128)S(1)}, f32[64,1536]{1,0:T(8,128)}, u32[]{:S(2)}) %copy-start) | copy-done | bytes 393240
  19.7 0.0 collective-permute-done.previous_ref
  19.7 0.0 collective-permute-done.1.following_ref
  19.7 0.0 collective-permute-done.2.turned_ref
  19.7 0.2 inputs.1
  19.9 7.1 %triples.1 = f32[32,64,128]{2,1,0:T(8,128)S(1)} custom-call(f32[64,1536]{1,0:T(8,128)S(1)} %get-tuple-element.7.refs_0_, f32[64,1536]{1,0:T(8,128)S(1)} %fetch.1.refs_1_, bf16[1536,128]{1,0:T(8,128)(2,1)S(1)} %get-tuple-element.8.refs_2_), custom_call_target="tpu_custom_call" | custom-call | flops 3221225472 | bytes 2228224 | tf_op jit(solution)/shard_map/triples/pallas_call | solution.py:92
  27.0 33.0 %all_to_all.10.arrived_ref = f32[8,4,64,128]{3,2,1,0:T(8,128)S(1)} all-to-all(f32[8,4,64,128]{3,2,1,0:T(8,128)S(1)} %bitcast.3), channel_id=1, replica_groups={{0,2,4,6,8,10,12,14},{1,3,5,7,9,11,13,15},{16,18,20,22,24,26,28,30},{17..., dimensions={0} | all-to-all | bytes 2097152 | tf_op jit(solution)/shard_map/all_to_all | solution.py:186
  60.0 0.7 regroup.1
  60.7 7.5 %all-to-all-start.1 = ((f32[16,16,128]{2,1,0:T(8,128)}), f32[16,16,128]{2,1,0:T(8,128)S(1)}, u32[]{:S(2)}, u32[]{:S(2)}) async-start(f32[16,16,128]{2,1,0:T(8,128)} %get-tuple-element.11), calls=%async_computation.1 | async-start | bytes 262144 | tf_op jit(solution)/shard_map/all_to_all | solution.py:189
  68.2 9.3 %collective-permute-start.3 = (f32[2,64,128]{2,1,0:T(8,128)S(1)}, f32[2,64,128]{2,1,0:T(8,128)S(1)}, u32[]{:S(2)}, u32[]{:S(2)}) collective-permute-start(f32[2,64,128]{2,1,0:T(8,128)S(1)} %get-tuple-element.9), channel_id=1, source_target_pairs={{0,1008},{16,0},{32,16},{48,32},{64,48},{80,64},{96,80},{112,96},{... | collective-permute-start | bytes 196616 | tf_op jit(solution)/shard_map/ppermute | solution.py:17
  77.5 13.5 %collective-permute-start.4 = (f32[2,64,128]{2,1,0:T(8,128)S(1)}, f32[2,64,128]{2,1,0:T(8,128)S(1)}, u32[]{:S(2)}, u32[]{:S(2)}) collective-permute-start(f32[2,64,128]{2,1,0:T(8,128)S(1)} %get-tuple-element.10), channel_id=1, source_target_pairs={{0,1009},{1,1008},{2,1011},{3,1010},{4,1013},{5,1012},{6,1015},{7,... | collective-permute-start | bytes 196616 | tf_op jit(solution)/shard_map/ppermute | solution.py:190
  91.0 0.0 collective-permute-done.3.own_ref
  91.1 1.3 %collective-permute-done.4.other_ref = f32[2,64,128]{2,1,0:T(8,128)S(1)} collective-permute-done((f32[2,64,128]{2,1,0:T(8,128)S(1)}, f32[2,64,128]{2,1,0:T(8,128)S(1)}, u32[]{:S(2)}, u32[]{:S(2)}) %collective-permute-start.4) | collective-permute-done | bytes 65568 | tf_op jit(solution)/shard_map/ppermute | solution.py:190
  92.4 0.0 all-to-all-done.1.turned_ref
  92.4 0.8 finish.1
  (1 shorter events, 0.0 us)
Async XLA Ops:
  0.6 19.1 %collective-permute-start = (f32[64,1536]{1,0:T(8,128)}, f32[64,1536]{1,0:T(8,128)S(1)}, u32[]{:S(2)}, u32[]{:S(2)}) collective-permute-start(f32[64,1536]{1,0:T(8,128)} %in_ref.1), channel_id=1, source_target_pairs={{0,16},{16,32},{32,48},{48,64},{64,80},{80,96},{96,112},{128,144},... | collective-permute-start | bytes 1179656 | tf_op jit(solution)/shard_map/ppermute | solution.py:179
  5.1 14.6 %collective-permute-start.1 = (f32[64,1536]{1,0:T(8,128)}, f32[64,1536]{1,0:T(8,128)S(1)}, u32[]{:S(2)}, u32[]{:S(2)}) collective-permute-start(f32[64,1536]{1,0:T(8,128)} %in_ref.1), channel_id=1, source_target_pairs={{16,0},{32,16},{48,32},{64,48},{80,64},{96,80},{112,96},{144,128},... | collective-permute-start | bytes 1179656 | tf_op jit(solution)/shard_map/ppermute | solution.py:178
  18.0 1.8 %collective-permute-start.2 = (f32[64,1536]{1,0:T(8,128)}, f32[64,1536]{1,0:T(8,128)S(1)}, u32[]{:S(2)}, u32[]{:S(2)}) collective-permute-start(f32[64,1536]{1,0:T(8,128)} %in_ref.1), channel_id=1, source_target_pairs={{1008,0},{112,128},{240,256},{368,384},{496,512},{624,640},{752,76... | collective-permute-start | bytes 1179656 | tf_op jit(solution)/shard_map/ppermute | solution.py:176
  18.7 1.0 %copy-start = (f32[64,1536]{1,0:T(8,128)S(1)}, f32[64,1536]{1,0:T(8,128)}, u32[]{:S(2)}) copy-start(f32[64,1536]{1,0:T(8,128)} %in_ref.1) | copy-start | bytes 1179652
  60.7 31.6 %all-to-all-start.1 = ((f32[16,16,128]{2,1,0:T(8,128)}), f32[16,16,128]{2,1,0:T(8,128)S(1)}, u32[]{:S(2)}, u32[]{:S(2)}) async-start(f32[16,16,128]{2,1,0:T(8,128)} %get-tuple-element.11), calls=%async_computation.1 | async-start | bytes 262144 | tf_op jit(solution)/shard_map/all_to_all | solution.py:189
  68.2 22.8 %collective-permute-start.3 = (f32[2,64,128]{2,1,0:T(8,128)S(1)}, f32[2,64,128]{2,1,0:T(8,128)S(1)}, u32[]{:S(2)}, u32[]{:S(2)}) collective-permute-start(f32[2,64,128]{2,1,0:T(8,128)S(1)} %get-tuple-element.9), channel_id=1, source_target_pairs={{0,1008},{16,0},{32,16},{48,32},{64,48},{80,64},{96,80},{112,96},{... | collective-permute-start | bytes 196616 | tf_op jit(solution)/shard_map/ppermute | solution.py:17
  77.5 14.8 %collective-permute-start.4 = (f32[2,64,128]{2,1,0:T(8,128)S(1)}, f32[2,64,128]{2,1,0:T(8,128)S(1)}, u32[]{:S(2)}, u32[]{:S(2)}) collective-permute-start(f32[2,64,128]{2,1,0:T(8,128)S(1)} %get-tuple-element.10), channel_id=1, source_target_pairs={{0,1009},{1,1008},{2,1011},{3,1010},{4,1013},{5,1012},{6,1015},{7,... | collective-permute-start | bytes 196616 | tf_op jit(solution)/shard_map/ppermute | solution.py:190

commit v10 on v5

--- a/solution.py
+++ b/solution.py
@@ -123,31 +123,31 @@
     )(mine, theirs.reshape(owners, 1, pairs, rows, lanes), *more)
 
 
-def regroup_kernel(half_ref, arrived_ref, send_ref, own_ref, other_ref, sum_ref):
+def regroup_kernel(arrived_ref, send_ref, own_ref, other_ref, sum_ref):
     pairs, rows, _ = sum_ref.shape
     per_owner = rows // send_ref.shape[0]
     sum_ref[...] = jnp.sum(arrived_ref[...], axis=0)
     for g in range(send_ref.shape[0]):
         for p in range(pairs):
             send_ref[g, p * per_owner : (p + 1) * per_owner] = sum_ref[p, g * per_owner : (g + 1) * per_owner]
-    half = half_ref[0]
+    half = lax.rem(lax.axis_index("field"), 2)
     for p in range(pairs // 2):
         own_ref[p] = sum_ref[half * (pairs // 2) + p]
         other_ref[p] = sum_ref[(1 - half) * (pairs // 2) + p]
 
 
-def regroup(half, arrived, parts):
+def regroup(arrived, parts):
     _, pairs, rows, lanes = arrived.shape
     kept = jax.ShapeDtypeStruct((pairs // 2, rows, lanes), jnp.float32)
     return pl.pallas_call(
         regroup_kernel,
         name="regroup",
         out_shape=(jax.ShapeDtypeStruct((parts, pairs * rows // parts, lanes), jnp.float32), kept, kept),
-        in_specs=[pl.BlockSpec(memory_space=pltpu.SMEM)] + in_vmem(1),
+        in_specs=in_vmem(1),
         out_specs=tuple(in_vmem(3)),
         scratch_shapes=[pltpu.VMEM((pairs, rows, lanes), jnp.float32)],
         compiler_params=pltpu.CompilerParams(vmem_limit_bytes=8 * 2**20),
-    )(half, arrived)
+    )(arrived)
 
 
 def finish_kernel(own_ref, other_ref, turned_ref, first_ref, second_ref, sum_ref, row_ref):
@@ -212,8 +212,7 @@
     along_z = [[2 * z + half for z in range(q, peers, 2)] for q in range(2) for half in range(2)]
     pieces = merged.reshape(peers // 2, run // 2, rows, 2 * rows)
     arrived = lax.all_to_all(pieces, "field", 0, 0, axis_index_groups=along_z, tiled=True)
-    half = (lax.axis_index("field") & 1).reshape(1)
-    send, own, other = regroup(half, arrived, parts)
+    send, own, other = regroup(arrived, parts)
     crossed = [(b * parts + f, (b - 1) % blocks * parts + (f ^ 1)) for b in range(blocks) for f in range(parts)]
     turned = lax.all_to_all(send, "field", split_axis=0, concat_axis=0, tiled=True)
     other = lax.ppermute(other, ("vec", "field"), crossed)

time: 91 us -> 91.4 us (level)
  blocking collectives: 0 us -> 15.1 us
  waiting for transfers between devices: 14.1 us -> 4.34 us
  starting transfers between devices: 64 us -> 60.5 us
  Pallas kernels: 10.6 us -> 9.24 us
    all_to_all x0 -> x1, blocking collectives: none -> 15.1 us  [per_device(): lax.all_to_all(pieces, 'field', 0, 0, axis_index_groups=along_z, tiled=True)]
    all_to_all x1 -> x0, waiting for transfers between devices: 10.7 us -> none  [per_device(): lax.all_to_all(pieces, 'field', 0, 0, axis_index_groups=along_z, tiled=True)]
    all_to_all x1 -> x0, starting transfers between devices: 3.47 us -> none  [per_device(): lax.all_to_all(pieces, 'field', 0, 0, axis_index_groups=along_z, tiled=True)]
    ppermute x4, starting transfers between devices: 35.2 us -> 37.8 us  [passed_along(): return lax.ppermute(x, axis, [(i, (i + by) % peers) for i in range(peers)])]
    ppermute x1, starting transfers between devices: 8.97 us -> 7.35 us  [per_device(): other = lax.ppermute(other, ('vec', 'field'), crossed)]
    pallas_call x2, Pallas kernels: 1.46 us -> 0.06 us  [merge(): pl.pallas_call(merge_kernel, name='merge', grid=(1,), out_shape=jax.Shape...]
    all_to_all x1, starting transfers between devices: 6.77 us -> 5.77 us  [per_device(): lax.all_to_all(send, 'field', split_axis=0, concat_axis=0, tiled=True)]
    ppermute x1, waiting for transfers between devices: 1.3 us -> 2.22 us  [per_device(): other = lax.ppermute(other, ('vec', 'field'), crossed)]
  transfers between devices with their start and end apart: 9 -> 8, of which waited for: 3 -> 2; matrix products, arithmetic and copies ran while one was open for 0% -> 0% of each run, Pallas kernels for 9% -> 9%
where the time goes in v10:
time: 91.4 us; the launch traced here: 91 us
  starting transfers between devices  60.5 us (66%)
  blocking collectives  15.1 us (17%)
  Pallas kernels  9.24 us (10%)
  waiting for transfers between devices  4.34 us (5%)
  local copies, waits for them, and re-layouts  0.99 us (1%)
    ppermute x4, starting transfers between devices, passed_along(): return lax.ppermute(x, axis, [(i, (i + by) % peers) for i in range(peers)])  37.8 us
    all_to_all x1, blocking collectives, per_device(): lax.all_to_all(pieces, 'field', 0, 0, axis_index_groups=along_z, tiled=True)  15.1 us
    ppermute x2, starting transfers between devices, sent(): return lax.ppermute(sums, 'field', moves)  9.56 us
    pallas_call x3, Pallas kernels, triples(): pl.pallas_call(lambda *refs: triple_kernel(scale, start, run, stride, *re...  7.52 us
    ppermute x1, starting transfers between devices, per_device(): other = lax.ppermute(other, ('vec', 'field'), crossed)  7.35 us
    all_to_all x1, starting transfers between devices, per_device(): lax.all_to_all(send, 'field', split_axis=0, concat_axis=0, tiled=True)  5.77 us
    ppermute x1, waiting for transfers between devices, per_device(): other = lax.ppermute(other, ('vec', 'field'), crossed)  2.22 us
    ppermute x4, waiting for transfers between devices, passed_along(): return lax.ppermute(x, axis, [(i, (i + by) % peers) for i in range(peers)])  2.11 us
  transfers between devices with their start and end apart: 8, of which 2 were waited for; matrix products, arithmetic and copies ran while one was open for 0% of the time, Pallas kernels for 9%

profile of v10, /device:TPU:1, one launch (start us, length us, event | category | flops | bytes accessed | tf_op | source)
XLA Modules:
  0.0 91.0 jit_solution(14671335222010939351)
XLA Ops:
  0.6 16.0 %collective-permute-start.1 = (f32[64,1536]{1,0:T(8,128)}, f32[64,1536]{1,0:T(8,128)S(1)}, u32[]{:S(2)}, u32[]{:S(2)}) collective-permute-start(f32[64,1536]{1,0:T(8,128)} %in_ref.1), channel_id=1, source_target_pairs={{0,1008},{16,0},{32,16},{48,32},{64,48},{80,64},{96,80},{112,96},{... | collective-permute-start | bytes 1179656 | tf_op jit(solution)/shard_map/ppermute | solution.py:17
  16.7 0.0 copy-start
  16.7 1.0 %copy-done = f32[64,1536]{1,0:T(8,128)S(1)} copy-done((f32[64,1536]{1,0:T(8,128)S(1)}, f32[64,1536]{1,0:T(8,128)}, u32[]{:S(2)}) %copy-start) | copy-done | bytes 393240
  17.7 0.1 fetch.1
  17.7 1.9 %collective-permute-start.2 = (f32[32,1536]{1,0:T(8,128)S(1)}, f32[32,1536]{1,0:T(8,128)S(1)}, u32[]{:S(2)}, u32[]{:S(2)}) collective-permute-start(f32[32,1536]{1,0:T(8,128)S(1)} %get-tuple-element.10), channel_id=1, source_target_pairs={{0,16},{16,32},{32,48},{48,64},{64,80},{80,96},{96,112},{112,128},... | collective-permute-start | bytes 589832 | tf_op jit(solution)/shard_map/ppermute | solution.py:17
  19.7 1.9 %collective-permute-start = (f32[32,1536]{1,0:T(8,128)S(1)}, f32[32,1536]{1,0:T(8,128)S(1)}, u32[]{:S(2)}, u32[]{:S(2)}) collective-permute-start(f32[32,1536]{1,0:T(8,128)S(1)} %get-tuple-element.8), channel_id=1, source_target_pairs={{0,16},{16,32},{32,48},{48,64},{64,80},{80,96},{96,112},{112,128},... | collective-permute-start | bytes 589832 | tf_op jit(solution)/shard_map/ppermute | solution.py:17
  21.6 0.0 collective-permute-done.1.c_ref
  21.6 0.2 weights.1.refs_2_
  21.8 2.1 %collective-permute-done.2.refs_0_ = f32[32,1536]{1,0:T(8,128)S(1)} collective-permute-done((f32[32,1536]{1,0:T(8,128)S(1)}, f32[32,1536]{1,0:T(8,128)S(1)}, u32[]{:S(2)}, u32[]{:S(2)}) %collective-permute-start.2) | collective-permute-done | bytes 196640 | tf_op jit(solution)/shard_map/ppermute | solution.py:17
  23.9 1.9 %triples.5 = f32[8,64,128]{2,1,0:T(8,128)S(1)} custom-call(f32[32,1536]{1,0:T(8,128)S(1)} %collective-permute-done.2.refs_0_, f32[64,1536]{1,0:T(8,128)S(1)} %get-tuple-element.9.refs_1_, bf16[1536,128]{1,0:T(8,128)(2,1)S(1)} %weights.1.refs_2_), custom_call_target="tpu_custom_call" | custom-call | flops 805306368 | bytes 1441792 | tf_op jit(solution)/shard_map/triples/pallas_call | solution.py:89
  25.7 1.9 %collective-permute-start.4 = (f32[8,64,128]{2,1,0:T(8,128)S(1)}, f32[8,64,128]{2,1,0:T(8,128)S(1)}, u32[]{:S(2)}, u32[]{:S(2)}) collective-permute-start(f32[8,64,128]{2,1,0:T(8,128)S(1)} %triples.5), channel_id=1, source_target_pairs={{0,2},{1,3},{2,0},{3,1},{4,6},{5,7},{6,4},{7,5},{8,10},{9,11},{10,... | collective-permute-start | bytes 786440 | tf_op jit(solution)/shard_map/ppermute | solution.py:205
  27.7 1.9 %triples.4 = f32[8,64,128]{2,1,0:T(8,128)S(1)} custom-call(f32[32,1536]{1,0:T(8,128)S(1)} %collective-permute-done.2.refs_0_, f32[64,1536]{1,0:T(8,128)S(1)} %get-tuple-element.9.refs_1_, bf16[1536,128]{1,0:T(8,128)(2,1)S(1)} %weights.1.refs_2_), custom_call_target="tpu_custom_call" | custom-call | flops 805306368 | bytes 1441792 | tf_op jit(solution)/shard_map/triples/pallas_call | solution.py:89
  29.5 7.6 %collective-permute-start.3 = (f32[8,64,128]{2,1,0:T(8,128)S(1)}, f32[8,64,128]{2,1,0:T(8,128)S(1)}, u32[]{:S(2)}, u32[]{:S(2)}) collective-permute-start(f32[8,64,128]{2,1,0:T(8,128)S(1)} %triples.4), channel_id=1, source_target_pairs={{0,14},{1,15},{2,4},{3,5},{4,2},{5,3},{6,8},{7,9},{8,6},{9,7},{10,... | collective-permute-start | bytes 786440 | tf_op jit(solution)/shard_map/ppermute | solution.py:205
  37.2 0.0 collective-permute-done.refs_0_
  37.2 3.8 %triples.3 = f32[16,64,128]{2,1,0:T(8,128)S(1)} custom-call(f32[32,1536]{1,0:T(8,128)S(1)} %collective-permute-done.refs_0_, f32[64,1536]{1,0:T(8,128)S(1)} %get-tuple-element.9.refs_1_, bf16[1536,128]{1,0:T(8,128)(2,1)S(1)} %weights.1.refs_2_), custom_call_target="tpu_custom_call" | custom-call | flops 1610612736 | bytes 1703936 | tf_op jit(solution)/shard_map/triples/pallas_call | solution.py:89
  41.0 0.0 collective-permute-done.4
  41.0 0.0 collective-permute-done.3
  41.1 15.1 %all_to_all.10.arrived_ref = f32[4,4,64,128]{3,2,1,0:T(8,128)S(1)} all-to-all(f32[4,4,64,128]{3,2,1,0:T(8,128)S(1)} %bitcast.5), channel_id=1, replica_groups={{0,4,8,12},{1,5,9,13},{2,6,10,14},{3,7,11,15},{16,20,24,28},{17,21,25,2..., dimensions={0} | all-to-all | bytes 1048576 | tf_op jit(solution)/shard_map/all_to_all | solution.py:214
  56.2 0.7 regroup.1
  56.9 5.8 %all-to-all-start.1 = ((f32[16,16,128]{2,1,0:T(8,128)}), f32[16,16,128]{2,1,0:T(8,128)S(1)}, u32[]{:S(2)}, u32[]{:S(2)}) async-start(f32[16,16,128]{2,1,0:T(8,128)} %get-tuple-element.13), calls=%async_computation.1 | async-start | bytes 262144 | tf_op jit(solution)/shard_map/all_to_all | solution.py:217
  62.7 18.0 %collective-permute-start.5 = (f32[2,64,128]{2,1,0:T(8,128)S(1)}, f32[2,64,128]{2,1,0:T(8,128)S(1)}, u32[]{:S(2)}, u32[]{:S(2)}) collective-permute-start(f32[2,64,128]{2,1,0:T(8,128)S(1)} %get-tuple-element.11), channel_id=1, source_target_pairs={{0,1008},{16,0},{32,16},{48,32},{64,48},{80,64},{96,80},{112,96},{... | collective-permute-start | bytes 196616 | tf_op jit(solution)/shard_map/ppermute | solution.py:17
  80.6 7.3 %collective-permute-start.6 = (f32[2,64,128]{2,1,0:T(8,128)S(1)}, f32[2,64,128]{2,1,0:T(8,128)S(1)}, u32[]{:S(2)}, u32[]{:S(2)}) collective-permute-start(f32[2,64,128]{2,1,0:T(8,128)S(1)} %get-tuple-element.12), channel_id=1, source_target_pairs={{0,1009},{1,1008},{2,1011},{3,1010},{4,1013},{5,1012},{6,1015},{7,... | collective-permute-start | bytes 196616 | tf_op jit(solution)/shard_map/ppermute | solution.py:218
  88.0 0.0 collective-permute-done.5.own_ref
  88.0 2.2 %collective-permute-done.6.other_ref = f32[2,64,128]{2,1,0:T(8,128)S(1)} collective-permute-done((f32[2,64,128]{2,1,0:T(8,128)S(1)}, f32[2,64,128]{2,1,0:T(8,128)S(1)}, u32[]{:S(2)}, u32[]{:S(2)}) %collective-permute-start.6) | collective-permute-done | bytes 65568 | tf_op jit(solution)/shard_map/ppermute | solution.py:218
  90.2 0.0 all-to-all-done.1.turned_ref
  90.2 0.8 finish.1
  (2 shorter events, 0.1 us)
Async XLA Ops:
  0.6 21.0 %collective-permute-start.1 = (f32[64,1536]{1,0:T(8,128)}, f32[64,1536]{1,0:T(8,128)S(1)}, u32[]{:S(2)}, u32[]{:S(2)}) collective-permute-start(f32[64,1536]{1,0:T(8,128)} %in_ref.1), channel_id=1, source_target_pairs={{0,1008},{16,0},{32,16},{48,32},{64,48},{80,64},{96,80},{112,96},{... | collective-permute-start | bytes 1179656 | tf_op jit(solution)/shard_map/ppermute | solution.py:17
  16.7 1.0 %copy-start = (f32[64,1536]{1,0:T(8,128)S(1)}, f32[64,1536]{1,0:T(8,128)}, u32[]{:S(2)}) copy-start(f32[64,1536]{1,0:T(8,128)} %in_ref.1) | copy-start | bytes 1179652
  17.7 6.1 %collective-permute-start.2 = (f32[32,1536]{1,0:T(8,128)S(1)}, f32[32,1536]{1,0:T(8,128)S(1)}, u32[]{:S(2)}, u32[]{:S(2)}) collective-permute-start(f32[32,1536]{1,0:T(8,128)S(1)} %get-tuple-element.10), channel_id=1, source_target_pairs={{0,16},{16,32},{32,48},{48,64},{64,80},{80,96},{96,112},{112,128},... | collective-permute-start | bytes 589832 | tf_op jit(solution)/shard_map/ppermute | solution.py:17
  19.7 17.5 %collective-permute-start = (f32[32,1536]{1,0:T(8,128)S(1)}, f32[32,1536]{1,0:T(8,128)S(1)}, u32[]{:S(2)}, u32[]{:S(2)}) collective-permute-start(f32[32,1536]{1,0:T(8,128)S(1)} %get-tuple-element.8), channel_id=1, source_target_pairs={{0,16},{16,32},{32,48},{48,64},{64,80},{80,96},{96,112},{112,128},... | collective-permute-start | bytes 589832 | tf_op jit(solution)/shard_map/ppermute | solution.py:17
  25.7 15.3 %collective-permute-start.4 = (f32[8,64,128]{2,1,0:T(8,128)S(1)}, f32[8,64,128]{2,1,0:T(8,128)S(1)}, u32[]{:S(2)}, u32[]{:S(2)}) collective-permute-start(f32[8,64,128]{2,1,0:T(8,128)S(1)} %triples.5), channel_id=1, source_target_pairs={{0,2},{1,3},{2,0},{3,1},{4,6},{5,7},{6,4},{7,5},{8,10},{9,11},{10,... | collective-permute-start | bytes 786440 | tf_op jit(solution)/shard_map/ppermute | solution.py:205
  29.5 11.5 %collective-permute-start.3 = (f32[8,64,128]{2,1,0:T(8,128)S(1)}, f32[8,64,128]{2,1,0:T(8,128)S(1)}, u32[]{:S(2)}, u32[]{:S(2)}) collective-permute-start(f32[8,64,128]{2,1,0:T(8,128)S(1)} %triples.4), channel_id=1, source_target_pairs={{0,14},{1,15},{2,4},{3,5},{4,2},{5,3},{6,8},{7,9},{8,6},{9,7},{10,... | collective-permute-start | bytes 786440 | tf_op jit(solution)/shard_map/ppermute | solution.py:205
  56.9 33.3 %all-to-all-start.1 = ((f32[16,16,128]{2,1,0:T(8,128)}), f32[16,16,128]{2,1,0:T(8,128)S(1)}, u32[]{:S(2)}, u32[]{:S(2)}) async-start(f32[16,16,128]{2,1,0:T(8,128)} %get-tuple-element.13), calls=%async_computation.1 | async-start | bytes 262144 | tf_op jit(solution)/shard_map/all_to_all | solution.py:217
  62.7 25.3 %collective-permute-start.5 = (f32[2,64,128]{2,1,0:T(8,128)S(1)}, f32[2,64,128]{2,1,0:T(8,128)S(1)}, u32[]{:S(2)}, u32[]{:S(2)}) collective-permute-start(f32[2,64,128]{2,1,0:T(8,128)S(1)} %get-tuple-element.11), channel_id=1, source_target_pairs={{0,1008},{16,0},{32,16},{48,32},{64,48},{80,64},{96,80},{112,96},{... | collective-permute-start | bytes 196616 | tf_op jit(solution)/shard_map/ppermute | solution.py:17
  80.6 9.6 %collective-permute-start.6 = (f32[2,64,128]{2,1,0:T(8,128)S(1)}, f32[2,64,128]{2,1,0:T(8,128)S(1)}, u32[]{:S(2)}, u32[]{:S(2)}) collective-permute-start(f32[2,64,128]{2,1,0:T(8,128)S(1)} %get-tuple-element.12), channel_id=1, source_target_pairs={{0,1009},{1,1008},{2,1011},{3,1010},{4,1013},{5,1012},{6,1015},{7,... | collective-permute-start | bytes 196616 | tf_op jit(solution)/shard_map/ppermute | solution.py:218
